TPU v7x, 256 devices: a whole 4x4x8 slice. The times are simulated.
256 devices in a mesh: ty: 16 (over y_lo, x, core), tx: 8 (over z), mode: 2 (over y_hi).
Axes of the slice: x: 4, y: 4 (y_hi: 2, y_lo: 2; y = y_hi * 2 + y_lo), z: 8, core: 2. Of those that a mesh axis runs over, the one named last changes fastest.
Arguments:
- object_field: float32 [2, 2, 4096, 2048], P(None, None, 'ty', 'tx'), may hold values from -2.4 to 2.4
- probe: float32 [4, 256, 512], P('mode'), may hold values from -6 to 6
- patterns: float32 [128, 256, 256], P(('ty', 'tx')), may hold values from 0.2 to 3
- offsets: int32 [128, 2], P(('ty', 'tx')), may hold values from 0 to 128
- phase: float32 [256, 256], replicated, may hold values from -3.140625 to 3.140625
- past_steps: bfloat16 [5, 2, 2, 4096, 2048], P(None, None, None, 'ty', 'tx'), may hold values from -4 to 4
- past_changes: bfloat16 [5, 2, 2, 4096, 2048], P(None, None, None, 'ty', 'tx'), may hold values from -16 to 16, as said below
Outputs:
- new_object: float32 [2, 2, 4096, 2048], P(None, None, 'ty', 'tx')
- gradient: float32 [2, 2, 4096, 2048], P(None, None, 'ty', 'tx')
Inputs may be any that keep to these rules, and one draw needn't show every extreme that they name: Every entry of past_changes has the sign of the same entry of past_steps.
All inputs are finite; a program needn't handle non-finite values.
Results may differ from a plain program's by a relative error of at most 0.02.
Values sent between devices are 32-bit elements; how exact they have to be, the bound alone decides.
No kernel may reach another device: no remote copies, remote signals or barrier semaphores. Data moves between devices by JAX's collectives and lax.ppermute only.
A program may use at most 64 MiB of HBM per device.

v0:
```python
import math

import jax
import jax.numpy as jnp
from jax import lax
from jax.sharding import PartitionSpec as P

MODES = 4
HALO = 64


REG_WEIGHT = 1.0


def extended_2(value, sides, width):
    for axis, dim in sides:
        size, length = (lax.axis_size(axis), value.shape[dim])
        up = [(i, (i + 1) % size) for i in range(size)]
        down = [(j, i) for i, j in up]
        last = lax.slice_in_dim(value, length - width, length, axis=dim)
        first = lax.slice_in_dim(value, 0, width, axis=dim)
        before = lax.ppermute(last, axis, up)
        after = lax.ppermute(first, axis, down)
        value = jnp.concatenate([before, value, after], axis=dim)
    return value


def dft_tables(length):
    indices = jnp.arange(length, dtype=jnp.int32)
    products = indices[:, None] * indices[None, :] % length
    angles = products.astype(jnp.float32) * (2.0 * math.pi / length)
    cosine_table = jnp.cos(angles) / math.sqrt(length)
    sine_table = jnp.sin(angles) / math.sqrt(length)
    forward_right = jnp.concatenate(
        [
            jnp.concatenate([cosine_table, -sine_table], 1),
            jnp.concatenate([sine_table, cosine_table], 1),
        ],
        0,
    )
    inverse_right = jnp.concatenate(
        [
            jnp.concatenate([cosine_table, sine_table], 1),
            jnp.concatenate([-sine_table, cosine_table], 1),
        ],
        0,
    )
    left_table = jnp.concatenate([cosine_table, sine_table], 0)
    return (
        forward_right.astype(jnp.bfloat16),
        inverse_right.astype(jnp.bfloat16),
        left_table.astype(jnp.bfloat16),
    )


def transform(wavefield, tables, inverse):
    right_table = tables[1] if inverse else tables[0]
    sign_value = -1.0 if inverse else 1.0
    lead_shape = wavefield.shape[:-2]
    length = wavefield.shape[-2]
    flat_wave = wavefield.reshape(-1, 2 * length).astype(jnp.bfloat16)
    first_pass = jnp.dot(flat_wave, right_table, preferred_element_type=jnp.float32)
    first_pass = first_pass.reshape(-1, length, 2 * length).astype(jnp.bfloat16)
    second_pass = jnp.einsum(
        "jk,bkl->bjl", tables[2], first_pass, preferred_element_type=jnp.float32
    )
    upper = second_pass[:, :length]
    lower = second_pass[:, length:]
    real_part = upper[:, :, :length] + sign_value * lower[:, :, length:]
    imag_part = upper[:, :, length:] - sign_value * lower[:, :, :length]
    return jnp.concatenate([real_part, imag_part], -1).reshape(lead_shape + (length, 2 * length))


def complex_product(first, second, conjugate_first):
    length = first.shape[-1] // 2
    first_real = first[..., :length]
    first_imag = first[..., length:]
    if conjugate_first:
        first_imag = -first_imag
    second_real = second[..., :length]
    second_imag = second[..., length:]
    return jnp.concatenate(
        [
            first_real * second_real - first_imag * second_imag,
            first_real * second_imag + first_imag * second_real,
        ],
        -1,
    )


def propagate(wavefield, kernel, tables, adjoint):
    spectrum = transform(wavefield, tables, False)
    spectrum = complex_product(kernel, spectrum, adjoint)
    return transform(spectrum, tables, True)


def forward_waves(windows, probe, kernel, tables):
    slice_count = windows.shape[1]
    wavefield = probe[None]
    entering = []
    for slice_index in range(slice_count):
        entering.append(wavefield)
        wavefield = complex_product(windows[:, slice_index][:, None], wavefield, False)
        if slice_index + 1 < slice_count:
            wavefield = propagate(wavefield, kernel, tables, False)
    return (transform(wavefield, tables, False), entering)


def window_gradients(far_field, entering, windows, residual, kernel, tables):
    slice_count = windows.shape[1]
    doubled = jnp.concatenate([residual, residual], -1)[:, None]
    adjoint_wave = transform(2.0 / MODES * doubled * far_field, tables, True)
    pieces = []
    for slice_index in reversed(range(slice_count)):
        pieces.append(jnp.sum(complex_product(entering[slice_index], adjoint_wave, True), axis=1))
        if slice_index > 0:
            adjoint_wave = complex_product(windows[:, slice_index][:, None], adjoint_wave, True)
            adjoint_wave = propagate(adjoint_wave, kernel, tables, True)
    return jnp.stack(pieces[::-1], 1)


def inner_product(first, second):
    return jnp.sum(first.astype(jnp.float32) * second.astype(jnp.float32))


def global_sums(values):
    return lax.psum(values, ("ty", "tx", "mode"))


def direction_search(gradient, past_steps, past_changes, portion):
    memory = past_steps.shape[0]
    step_parts = portion(past_steps)
    change_parts = portion(past_changes)
    search = gradient
    alphas = [None] * memory
    curvatures = None
    scaling = None
    for history_index in reversed(range(memory)):
        local_terms = [inner_product(step_parts[history_index], portion(search))]
        if history_index == memory - 1:
            local_terms = local_terms + [
                inner_product(step_parts[other_index], change_parts[other_index])
                for other_index in range(memory)
            ]
            local_terms = local_terms + [
                inner_product(change_parts[history_index], change_parts[history_index])
            ]
        totals = global_sums(jnp.stack(local_terms))
        if history_index == memory - 1:
            curvatures = totals[1 : memory + 1]
            scaling = totals[memory] / totals[memory + 1]
        alphas[history_index] = totals[0] / curvatures[history_index]
        search = search - alphas[history_index] * past_changes[history_index].astype(jnp.float32)
    search = scaling * search
    for history_index in range(memory):
        totals = global_sums(
            jnp.stack([inner_product(change_parts[history_index], portion(search))])
        )
        beta_value = totals[0] / curvatures[history_index]
        search = search + (alphas[history_index] - beta_value) * past_steps[history_index].astype(
            jnp.float32
        )
    return search


def per_device(object_field, probe, patterns, offsets, phase, past_steps, past_changes):
    slice_count = object_field.shape[0]
    tile_edge = object_field.shape[2]
    probe_edge = probe.shape[1]
    mode_index = lax.axis_index("mode")
    mode_count = lax.axis_size("mode")
    tables = dft_tables(probe_edge)
    kernel = jnp.concatenate([jnp.cos(phase), jnp.sin(phase)], -1)
    extended = extended_2(object_field, (("ty", 2), ("tx", 3)), HALO)
    pattern_index = 0
    starts = (0, 0, offsets[pattern_index, 0], offsets[pattern_index, 1])
    window = lax.dynamic_slice(extended, starts, (slice_count, 2, probe_edge, probe_edge))
    window_list = [jnp.concatenate([window[:, 0], window[:, 1]], -1)]
    windows = jnp.stack(window_list, 0)
    far_field, entering = forward_waves(windows, probe, kernel, tables)
    partial_intensity = jnp.sum(
        far_field[..., :probe_edge] ** 2 + far_field[..., probe_edge:] ** 2, axis=1
    )
    intensity = lax.psum(partial_intensity, "mode") / MODES
    residual = intensity - patterns
    pieces = window_gradients(far_field, entering, windows, residual, kernel, tables)
    extended_edge = tile_edge + 2 * HALO
    collected = jnp.zeros((slice_count, 2, extended_edge, extended_edge), jnp.float32)
    pattern_index = 0
    piece_now = pieces[pattern_index]
    unpacked = jnp.stack([piece_now[..., :probe_edge], piece_now[..., probe_edge:]], 1)
    starts = (0, 0, offsets[pattern_index, 0], offsets[pattern_index, 1])
    collected = lax.dynamic_update_slice(collected, unpacked, starts)
    returned = extended_2(collected, (("ty", 2), ("tx", 3)), HALO)
    columns = returned[..., 2 * HALO : 2 * HALO + tile_edge]
    columns = columns.at[..., :HALO].add(returned[..., :HALO])
    columns = columns.at[..., tile_edge - HALO :].add(returned[..., extended_edge + HALO :])
    tile_gradient = columns[:, :, 2 * HALO : 2 * HALO + tile_edge, :]
    tile_gradient = tile_gradient.at[:, :, :HALO].add(columns[:, :, :HALO])
    tile_gradient = tile_gradient.at[:, :, tile_edge - HALO :].add(
        columns[:, :, extended_edge + HALO :]
    )
    share_rows = tile_edge // mode_count

    def own_rows(array):
        return lax.dynamic_slice_in_dim(array, mode_index * share_rows, share_rows, array.ndim - 2)

    gradient = lax.psum(tile_gradient, "mode") + REG_WEIGHT * object_field
    search = direction_search(gradient, past_steps, past_changes, own_rows)
    return (object_field - search, gradient)


def solution(mesh):
    placed = (
        P(None, None, "ty", "tx"),
        P("mode", None, None),
        P(("ty", "tx"), None, None),
        P(("ty", "tx"), None),
        P(),
        P(None, None, None, "ty", "tx"),
        P(None, None, None, "ty", "tx"),
    )
    return jax.shard_map(
        per_device,
        mesh=mesh,
        in_specs=placed,
        out_specs=(P(None, None, "ty", "tx"), P(None, None, "ty", "tx")),
        check_vma=False,
    )
```

profile of v0, /device:TPU:1, one launch (start us, length us, event | category | flops | bytes accessed | tf_op | source)
XLA Modules:
  0.0 1045.5 jit_solution(16953772161357605310)
XLA Ops:
  9.0 2.7 collective-permute-start
  17.8 2.8 collective-permute-done.1
  23.4 3.9 collective-permute-start.3
  39.1 3.3 convolution_bitcast_fusion.5
  47.2 2.5 fusion.34
  52.9 3.3 convolution_bitcast_fusion.4
  65.1 31.1 %all-reduce.3.cloned.1.call-done = f32[1,256,256]{1,2,0:T(8,128)} async-done(((f32[1,256,256]{1,2,0:T(8,128)}), f32[1,256,256]{1,2,0:T(8,128)}) %all-reduce.3.cloned.1.call-update) | async-done | bytes 262160 | tf_op jit(solution)/shard_map/psum | solution.py:184
  98.1 3.6 convolution_bitcast_fusion.1
  104.7 3.4 convolution_bitcast_fusion.3
  116.9 13.6 %dynamic_update_slice.3 = f32[2,2,384,384]{3,2,1,0:T(8,128)S(1)} dynamic-update-slice(f32[2,2,384,384]{3,2,1,0:T(8,128)S(1)} %broadcast_in_dim.4, f32[2,2,256,256]{3,2,1,0:T(8,128)S(1)} %copy.74, s32[]{:T(128)} %constant.132.clone.1, s32[]{:T(128)} %constant.132.clone.1, s32[]{:T(128)S(6)} %select_n.48, s32[]{:T(128)S(6)} %select_n.49) | dynamic-update-slice | bytes 2097156 | tf_op jit(solution)/shard_map/dynamic_update_slice | solution.py:193
  130.5 3.0 collective-permute-start.4
  133.5 4.7 collective-permute-done.4
  138.2 2.8 collective-permute-done.5
  146.9 2.9 collective-permute-start.6
  155.2 7.0 collective-permute-done.6
  164.5 2.5 slice_add_fusion.1
  167.1 6.1 scatter-add.14
  173.2 2.5 copy.78
  177.6 5.8 scatter-add.15
  186.9 52.3 %all-reduce.5.cloned.1.call-done = f32[2,2,256,256]{3,2,1,0:T(8,128)} async-done(((f32[2,2,256,256]{3,2,1,0:T(8,128)}), f32[2,2,256,256]{3,2,1,0:T(8,128)}) %all-reduce.5.cloned.1.call-update) | async-done | bytes 1048592 | tf_op jit(solution)/shard_map/psum | solution.py:208
  244.2 4.5 stack.86
  248.7 76.1 %psum.86 = f32[7]{0:T(128)S(1)} all-reduce(f32[7]{0:T(128)S(1)} %stack.86), channel_id=1, replica_groups=mesh['ty'=16,'tx'=8,'mode'=2] {'ty','tx','mode'}, use_global_device_ids=true, to_apply=%region_12.13 | all-reduce | flops 7 | bytes 56 | tf_op jit(solution)/shard_map/psum | solution.py:127
  332.4 74.0 %psum.87 = f32[1]{0:T(128)} all-reduce(f32[1]{0:T(128)} %bitcast.61), channel_id=1, replica_groups=mesh['ty'=16,'tx'=8,'mode'=2] {'ty','tx','mode'}, use_global_device_ids=true, to_apply=%region_14.15 | all-reduce | flops 1 | bytes 8 | tf_op jit(solution)/shard_map/psum | solution.py:127
  411.7 73.4 %psum.88 = f32[1]{0:T(128)} all-reduce(f32[1]{0:T(128)} %bitcast.65), channel_id=1, replica_groups=mesh['ty'=16,'tx'=8,'mode'=2] {'ty','tx','mode'}, use_global_device_ids=true, to_apply=%region_16.17 | all-reduce | flops 1 | bytes 8 | tf_op jit(solution)/shard_map/psum | solution.py:127
  490.6 74.3 %psum.89 = f32[1]{0:T(128)} all-reduce(f32[1]{0:T(128)} %bitcast.69), channel_id=1, replica_groups=mesh['ty'=16,'tx'=8,'mode'=2] {'ty','tx','mode'}, use_global_device_ids=true, to_apply=%region_18.19 | all-reduce | flops 1 | bytes 8 | tf_op jit(solution)/shard_map/psum | solution.py:127
  570.2 73.4 %psum.90 = f32[1]{0:T(128)} all-reduce(f32[1]{0:T(128)} %bitcast.73), channel_id=1, replica_groups=mesh['ty'=16,'tx'=8,'mode'=2] {'ty','tx','mode'}, use_global_device_ids=true, to_apply=%region_20.21 | all-reduce | flops 1 | bytes 8 | tf_op jit(solution)/shard_map/psum | solution.py:127
  648.0 74.2 %psum.91 = f32[1]{0:T(128)} all-reduce(f32[1]{0:T(128)} %bitcast.77), channel_id=1, replica_groups=mesh['ty'=16,'tx'=8,'mode'=2] {'ty','tx','mode'}, use_global_device_ids=true, to_apply=%region_22.23 | all-reduce | flops 1 | bytes 8 | tf_op jit(solution)/shard_map/psum | solution.py:127
  726.7 73.3 %psum.92 = f32[1]{0:T(128)} all-reduce(f32[1]{0:T(128)} %bitcast.81), channel_id=1, replica_groups=mesh['ty'=16,'tx'=8,'mode'=2] {'ty','tx','mode'}, use_global_device_ids=true, to_apply=%region_24.25 | all-reduce | flops 1 | bytes 8 | tf_op jit(solution)/shard_map/psum | solution.py:127
  804.5 74.1 %psum.93 = f32[1]{0:T(128)} all-reduce(f32[1]{0:T(128)} %bitcast.85), channel_id=1, replica_groups=mesh['ty'=16,'tx'=8,'mode'=2] {'ty','tx','mode'}, use_global_device_ids=true, to_apply=%region_26.27 | all-reduce | flops 1 | bytes 8 | tf_op jit(solution)/shard_map/psum | solution.py:127
  883.1 73.5 %psum.94 = f32[1]{0:T(128)} all-reduce(f32[1]{0:T(128)} %bitcast.89), channel_id=1, replica_groups=mesh['ty'=16,'tx'=8,'mode'=2] {'ty','tx','mode'}, use_global_device_ids=true, to_apply=%region_28.29 | all-reduce | flops 1 | bytes 8 | tf_op jit(solution)/shard_map/psum | solution.py:127
  960.3 74.1 %psum.95 = f32[1]{0:T(128)} all-reduce(f32[1]{0:T(128)} %bitcast.92), channel_id=1, replica_groups=mesh['ty'=16,'tx'=8,'mode'=2] {'ty','tx','mode'}, use_global_device_ids=true, to_apply=%region_30.31 | all-reduce | flops 1 | bytes 8 | tf_op jit(solution)/shard_map/psum | solution.py:127
  1035.8 2.8 fusion.4
  (144 shorter events, 105.3 us)
Async XLA Ops:
  7.2 5.2 copy-start.23
  7.2 89.0 %all-reduce.3.cloned.1.call-start = ((), (), s32[]{:S(2)}) async-start(), calls=%async_computation | async-start | bytes 524288 | tf_op jit(solution)/shard_map/psum | solution.py:184
  9.0 8.8 collective-permute-start
  11.7 8.9 collective-permute-start.1
  21.8 14.6 %collective-permute-start.2 = (f32[2,2,384,64]{2,3,1,0:T(8,128)}, f32[2,2,384,64]{2,3,1,0:T(8,128)S(1)}, u32[]{:S(2)}, u32[]{:S(2)}) collective-permute-start(f32[2,2,384,64]{2,3,1,0:T(8,128)} %get-tuple-element.80), channel_id=1, source_target_pairs={{0,2},{2,4},{4,6},{6,8},{8,10},{10,12},{12,14},{14,0},{1,3},{3,5},... | collective-permute-start | bytes 1179656 | tf_op jit(solution)/shard_map/ppermute | solution.py:22
  23.4 12.9 %collective-permute-start.3 = (f32[2,2,384,64]{2,3,1,0:T(8,128)}, f32[2,2,384,64]{2,3,1,0:T(8,128)}, u32[]{:S(2)}, u32[]{:S(2)}) collective-permute-start(f32[2,2,384,64]{2,3,1,0:T(8,128)} %get-tuple-element.79), channel_id=1, source_target_pairs={{2,0},{4,2},{6,4},{8,6},{10,8},{12,10},{14,12},{0,14},{3,1},{5,3},... | collective-permute-start | bytes 1179656 | tf_op jit(solution)/shard_map/ppermute | solution.py:23
  37.6 1.3 copy-start.13
  37.7 1.4 copy-start.18
  44.0 0.9 copy-start.19
  44.0 1.0 copy-start.21
  58.7 180.5 %all-reduce.5.cloned.1.call-start = ((), (), s32[]{:S(2)}) async-start(), calls=%async_computation.1 | async-start | bytes 2097152 | tf_op jit(solution)/shard_map/psum | solution.py:208
  101.7 1.8 copy-start.16
  108.1 1.8 copy-start.17
  109.8 1.0 copy-start.22
  114.8 1.1 copy-start.14
  130.4 7.8 copy-start
  130.5 7.7 collective-permute-start.4
  133.5 7.5 collective-permute-start.5
  146.9 15.3 %collective-permute-start.6 = (f32[2,2,512,64]{2,3,1,0:T(8,128)}, f32[2,2,512,64]{2,3,1,0:T(8,128)}, u32[]{:S(2)}, u32[]{:S(2)}) collective-permute-start(f32[2,2,512,64]{2,3,1,0:T(8,128)} %copy.75), channel_id=1, source_target_pairs={{0,2},{2,4},{4,6},{6,8},{8,10},{10,12},{12,14},{14,0},{1,3},{3,5},... | collective-permute-start | bytes 1572872 | tf_op jit(solution)/shard_map/ppermute | solution.py:22
  152.1 21.1 %collective-permute-start.7 = (f32[2,2,512,64]{2,3,1,0:T(8,128)}, f32[2,2,512,64]{2,3,1,0:T(8,128)}, u32[]{:S(2)}, u32[]{:S(2)}) collective-permute-start(f32[2,2,512,64]{2,3,1,0:T(8,128)} %copy.77), channel_id=1, source_target_pairs={{2,0},{4,2},{6,4},{8,6},{10,8},{12,10},{14,12},{0,14},{3,1},{5,3},... | collective-permute-start | bytes 1572872 | tf_op jit(solution)/shard_map/ppermute | solution.py:23
  173.2 4.4 copy-start.1
  186.9 55.0 %copy-start.2 = (bf16[5,2,2,256,256]{4,3,2,1,0:T(8,128)(2,1)S(1)}, bf16[5,2,2,256,256]{4,3,2,1,0:T(8,128)(2,1)}, u32[]{:S(2)}) copy-start(bf16[5,2,2,256,256]{4,3,2,1,0:T(8,128)(2,1)} %param.21) | copy-start | bytes 7864324
  240.9 1.0 copy-start.3
  329.6 1.0 copy-start.11
  409.0 1.0 copy-start.9
  487.8 1.0 copy-start.10
  567.4 1.0 copy-start.8
  646.3 1.0 copy-start.7
  725.0 1.0 copy-start.4
  802.8 1.0 copy-start.5
  881.3 1.0 copy-start.6
  959.4 1.0 copy-start.12
  (2 other events, 1.8 us)
Sparse Core Ops, SparseCore 0:
  58.9 37.3 all-reduce.2
  187.0 52.1 all-reduce.4
where the time goes:
time: 1050 us
  blocking collectives  740 us (70%)
  waiting for transfers between devices  105 us (10%)
  local copies, waits for them, and re-layouts  68 us (6%)
  other arithmetic  65 us (6%)
  between operations  32.9 us (3%)
  matrix products  17.9 us (2%)
  starting transfers between devices  16.2 us (2%)
    psum x10, blocking collectives, global_sums(): return lax.psum(values, ('ty', 'tx', 'mode'))  740 us
    psum x1, waiting for transfers between devices, per_device(): gradient = lax.psum(tile_gradient, 'mode') + REG_WEIGHT * object_field  52.3 us
    psum x1, waiting for transfers between devices, per_device(): intensity = lax.psum(partial_intensity, 'mode') / MODES  31.1 us
  transfers between devices with their start and end apart: 10, of which 8 were waited for; matrix products, arithmetic and copies ran while one was open for 3% of the time, Pallas kernels for 0%

commit v1 on v0

v1 whole, which is shorter than its diff:
```python
import math

import jax
import jax.numpy as jnp
import numpy as np
from jax import lax
from jax.experimental import pallas as pl
from jax.experimental.pallas import tpu as pltpu
from jax.sharding import PartitionSpec as P

MODES = 4
HALO = 64
REG_WEIGHT = 1.0
N = 256
FRAME = N + 2 * HALO
MEM = 5
CHUNK = 32
F32 = jnp.float32
BF16 = jnp.bfloat16
TILES = ("ty", "tx")
VMEM = pl.BlockSpec(memory_space=pltpu.VMEM)
SMEM = pl.BlockSpec(memory_space=pltpu.SMEM)
PARAMS = pltpu.CompilerParams(vmem_limit_bytes=40 * 1024 * 1024)
SY_PAIRS = [(i, j) for i in range(MEM) for j in range(i, MEM)]
SY_ROW = {pair: k for k, pair in enumerate(SY_PAIRS)}
YY_ROW = {pair: len(SY_PAIRS) + k for k, pair in enumerate(SY_PAIRS)}
SG_ROW = 2 * len(SY_PAIRS)
YG_ROW = SG_ROW + MEM
ROWS = YG_ROW + MEM


def dft_tables():
    indices = np.arange(N, dtype=np.int32)
    products = indices[:, None] * indices[None, :] % N
    angles = products.astype(np.float32) * np.float32(2.0 * math.pi / N)
    cosine = (np.cos(angles) / np.float32(math.sqrt(N))).astype(np.float32)
    sine = (np.sin(angles) / np.float32(math.sqrt(N))).astype(np.float32)
    forward = np.block([[cosine, -sine], [sine, cosine]])
    inverse = np.block([[cosine, sine], [-sine, cosine]])
    left = np.concatenate([cosine, sine], 1)
    return tuple(jnp.asarray(t, BF16) for t in (forward, inverse, left))


def lanes(shape):
    return lax.broadcasted_iota(jnp.int32, shape, len(shape) - 1)


def chunks(total=N, step=CHUNK):
    return [slice(c, c + step) for c in range(0, total, step)]


def aligned(offset):
    base = pl.multiple_of((offset // 8) * 8, 8)
    return base, offset - base


def product(a, b, conjugate):
    ar, ai = a
    br, bi = b
    if conjugate:
        return ar * br + ai * bi, ar * bi - ai * br
    return ar * br - ai * bi, ar * bi + ai * br


def halves(ref, index, rows):
    return ref[index, rows, 0:N], ref[index, rows, N : 2 * N]


def first_pass(xb, ks, m, right, inverse):
    y = jnp.dot(xb[m], right[...], preferred_element_type=F32).astype(BF16)
    yr, yi = y[:, :N], y[:, N:]
    ks[m, 0:N, :] = y
    if inverse:
        ks[m, N : 2 * N, 0:N] = -yi
        ks[m, N : 2 * N, N : 2 * N] = yr
    else:
        ks[m, N : 2 * N, 0:N] = yi
        ks[m, N : 2 * N, N : 2 * N] = -yr


def second_pass(ks, m, left):
    return jnp.dot(left[...], ks[m], preferred_element_type=F32)


def propagate(xb, ks, zs, m, kernel, tables, adjoint):
    forward, inverse, left = tables
    first_pass(xb, ks, m, forward, False)
    zs[m] = second_pass(ks, m, left)
    for rows in chunks():
        h = (kernel[0, rows, :], kernel[1, rows, :])
        re, im = product(h, halves(zs, m, rows), adjoint)
        xb[m, rows, 0:N] = re.astype(BF16)
        xb[m, rows, N : 2 * N] = im.astype(BF16)
    first_pass(xb, ks, m, inverse, True)
    return second_pass(ks, m, left)


def forward_mode(m, psi0, window, kernel, tables, psi1, far, xb, ks, zs):
    forward, inverse, left = tables
    for rows in chunks():
        re, im = product(halves(window, 0, rows), (psi0[rows, 0:N], psi0[rows, N : 2 * N]), False)
        xb[m, rows, 0:N] = re.astype(BF16)
        xb[m, rows, N : 2 * N] = im.astype(BF16)
    psi1[m] = propagate(xb, ks, zs, m, kernel, tables, False)
    for rows in chunks():
        re, im = product(halves(window, 1, rows), halves(psi1, m, rows), False)
        xb[m, rows, 0:N] = re.astype(BF16)
        xb[m, rows, N : 2 * N] = im.astype(BF16)
    first_pass(xb, ks, m, forward, False)
    far[m] = second_pass(ks, m, left)


def add_intensity(far, out, base):
    for rows in chunks():
        terms = []
        for m in range(2):
            re, im = halves(far, m, rows)
            terms.append(re * re + im * im)
        total = terms[0] + terms[1]
        out[rows, :] = total if base is None else base[rows, :] + total


def own_kernel(offsets, obj, top, bottom, left_in, right_in, corner_left, corner_right, probe, kernel,
               fwd_t, inv_t, left_t, window, psi1, far, intensity, ext, xb, ks, zs):
    tables = (fwd_t, inv_t, left_t)
    low = lanes((HALO, 2 * HALO)) < HALO

    def border(right_block, left_block, part):
        if part == 0:
            return jnp.where(low, right_block, pltpu.roll(left_block, HALO, 1))
        return jnp.where(low, pltpu.roll(right_block, HALO, 1), left_block)

    row_base, row_rest = aligned(offsets[0, 0])
    shift = lax.rem(HALO + FRAME - offsets[0, 1], FRAME)
    for s in range(2):
        for part in range(2):
            q = 2 * s + part
            ext[q, 0:HALO, 0:N] = top[s, part]
            ext[q, HALO : HALO + N, 0:N] = obj[s, part]
            ext[q, HALO + N : FRAME, 0:N] = bottom[s, part]
            ext[q, 0:HALO, N:FRAME] = border(
                corner_right[s, HALO : 2 * HALO], corner_left[s, HALO : 2 * HALO], part)
            ext[q, HALO + N : FRAME, N:FRAME] = border(
                corner_right[s, 0:HALO], corner_left[s, 0:HALO], part)
            for rows in chunks(N, HALO):
                ext[q, HALO + rows.start : HALO + rows.stop, N:FRAME] = border(
                    right_in[s, rows], left_in[s, rows], part)
            for rows in chunks(N, 64):
                block = ext[q, pl.ds(row_base + rows.start, 72), :]
                block = pltpu.roll(block, lax.rem(72 - row_rest, 72), 0)[:64]
                window[s, rows, part * N : (part + 1) * N] = pltpu.roll(block, shift, 1)[:, :N]
    for m in range(2):
        forward_mode(m, probe.at[m], window, kernel, tables, psi1, far, xb, ks, zs)
    add_intensity(far, intensity, None)


def other_kernel(offsets, obj, probe, near, swapped, kernel, fwd_t, inv_t, left_t, patterns, window,
                 psi1_own, far_own, intensity, gradient, row_top, row_bottom, col_left, col_right,
                 corner_left, corner_right, psi1, far, inten, xb, ks, zs, back, frame):
    tables = (fwd_t, inv_t, left_t)
    others = (near, swapped)
    for m in range(2):
        forward_mode(m, others[m], window, kernel, tables, psi1, far, xb, ks, zs)
    add_intensity(far, inten, intensity)
    for rows in chunks():
        inten[rows, :] = (inten[rows, :] * (1.0 / MODES) - patterns[0, rows, :]) * (2.0 / MODES)
    row_base, row_rest = aligned(offsets[0, 0])
    shift = lax.rem(HALO + N + offsets[0, 1], FRAME)
    for pair in range(2):
        far_now = far_own if pair == 0 else far
        psi_now = psi1_own if pair == 0 else psi1
        first = (probe.at[0], probe.at[1]) if pair == 0 else others
        for m in range(2):
            for rows in chunks():
                scale = inten[rows, :]
                re, im = halves(far_now, m, rows)
                xb[m, rows, 0:N] = (scale * re).astype(BF16)
                xb[m, rows, N : 2 * N] = (scale * im).astype(BF16)
            first_pass(xb, ks, m, inv_t, True)
            zs[m] = second_pass(ks, m, left_t)
            for rows in chunks():
                current = halves(zs, m, rows)
                re, im = product(halves(psi_now, m, rows), current, True)
                if pair or m:
                    re, im = re + back[1, rows, 0:N], im + back[1, rows, N : 2 * N]
                back[1, rows, 0:N] = re
                back[1, rows, N : 2 * N] = im
                re, im = product(halves(window, 1, rows), current, True)
                xb[m, rows, 0:N] = re.astype(BF16)
                xb[m, rows, N : 2 * N] = im.astype(BF16)
            zs[m] = propagate(xb, ks, zs, m, kernel, tables, True)
            for rows in chunks():
                psi0 = first[m]
                re, im = product((psi0[rows, 0:N], psi0[rows, N : 2 * N]), halves(zs, m, rows), True)
                if pair or m:
                    re, im = re + back[0, rows, 0:N], im + back[0, rows, N : 2 * N]
                back[0, rows, 0:N] = re
                back[0, rows, N : 2 * N] = im
    low = lanes((HALO, 2 * HALO)) < HALO
    zero = jnp.zeros((HALO, 2 * HALO), F32)
    gap = jnp.zeros((8, FRAME), F32)
    frame[...] = jnp.zeros(frame.shape, F32)
    for q in range(4):
        s, part = divmod(q, 2)
        for rows in chunks(N, 64):
            block = back[s, rows, part * N : (part + 1) * N]
            block = pltpu.roll(jnp.concatenate([block, zero], 1), shift, 1)
            block = pltpu.roll(jnp.concatenate([block, gap], 0), row_rest, 0)
            frame[q, pl.ds(row_base + rows.start, 72), :] += block
    for s in range(2):
        for part in range(2):
            q = 2 * s + part
            gradient[s, part] = frame[q, HALO : HALO + N, 0:N] + REG_WEIGHT * obj[s, part]
            row_top[s, part] = frame[q, 0:HALO, 0:N]
            row_bottom[s, part] = frame[q, HALO + N : FRAME, 0:N]

        def strips(rows):
            re, im = frame[2 * s, rows, N:FRAME], frame[2 * s + 1, rows, N:FRAME]
            right = jnp.where(low, re, pltpu.roll(im, HALO, 1))
            left = jnp.where(low, pltpu.roll(re, HALO, 1), im)
            return right, left

        for rows in chunks(N, HALO):
            right, left = strips(slice(HALO + rows.start, HALO + rows.stop))
            col_right[s, rows] = right
            col_left[s, rows] = left
        right, left = strips(slice(HALO + N, FRAME))
        corner_right[s, 0:HALO] = right
        corner_left[s, 0:HALO] = left
        right, left = strips(slice(0, HALO))
        corner_right[s, HALO : 2 * HALO] = right
        corner_left[s, HALO : 2 * HALO] = left


def put_rows(out, first_row, sums):
    for k, value in enumerate(sums):
        out[first_row + k : first_row + k + 1, :] = jnp.sum(value, axis=0, keepdims=True)


def fold(value):
    rows = value.shape[0]
    value = value[:, : N // 2] + value[:, N // 2 :]
    return sum(value[r : r + 8] for r in range(0, rows, 8))


def gram_kernel(steps, changes, out):
    count = 2 * len(SY_PAIRS)

    def body(k, carry):
        q = k // (N // 16)
        rows = pl.ds((k % (N // 16)) * 16, 16)
        s, part = q // 2, q % 2
        st = [steps[i, s, part, rows, :].astype(F32) for i in range(MEM)]
        ch = [changes[i, s, part, rows, :].astype(F32) for i in range(MEM)]
        new = [fold(st[i] * ch[j]) for i, j in SY_PAIRS] + [fold(ch[i] * ch[j]) for i, j in SY_PAIRS]
        return tuple(a + b for a, b in zip(carry, new))

    zero = tuple(jnp.zeros((8, N // 2), F32) for _ in range(count))
    put_rows(out, 0, lax.fori_loop(0, 4 * (N // 16), body, zero))


def dots_kernel(gradient_in, row_up, row_down, col_left, col_right, steps, changes, gram, gradient, out, sums):
    low = lanes((N, 2 * HALO)) < HALO
    for s in range(2):
        for part in range(2):
            gradient[s, part] = gradient_in[s, part]
            gradient[s, part, 0:HALO, :] += row_up[s, part]
            gradient[s, part, N - HALO : N, :] += row_down[s, part]
        from_left, from_right = col_left[s], col_right[s]
        flip_left, flip_right = pltpu.roll(from_left, HALO, 1), pltpu.roll(from_right, HALO, 1)
        for part in range(2):
            a = from_left if part == 0 else flip_left
            b = flip_right if part == 0 else from_right
            gradient[s, part, :, 0 : 2 * HALO] += jnp.where(low, a, 0.0)
            gradient[s, part, :, N - 2 * HALO : N] += jnp.where(low, 0.0, b)

    def body(k, carry):
        q = k // (N // 16)
        rows = pl.ds((k % (N // 16)) * 16, 16)
        s, part = q // 2, q % 2
        g = gradient[s, part, rows, :]
        new = [fold(steps[i, s, part, rows, :].astype(F32) * g) for i in range(MEM)]
        new += [fold(changes[i, s, part, rows, :].astype(F32) * g) for i in range(MEM)]
        return tuple(a + b for a, b in zip(carry, new))

    zero = tuple(jnp.zeros((8, N // 2), F32) for _ in range(2 * MEM))
    sums[...] = jnp.zeros(sums.shape, F32)
    sums[0:SG_ROW, :] = gram[0:SG_ROW, :]
    put_rows(sums, SG_ROW, lax.fori_loop(0, 4 * (N // 16), body, zero))
    totals = jnp.sum(sums[...], axis=1, keepdims=True)
    row = lax.broadcasted_iota(jnp.int32, (128, 128), 0)
    spread = jnp.where(row == lanes((128, 128)), totals, 0.0)
    total_row = jnp.sum(spread, axis=0, keepdims=True)
    out[...] = jnp.broadcast_to(total_row[None], (128, 1, 128))


def final_kernel(parts, obj, gradient, steps, changes, out):
    total = jnp.sum(parts[:, 0, :], axis=0, keepdims=True)
    row = lax.broadcasted_iota(jnp.int32, (128, 128), 0)
    diagonal = jnp.where(row == lanes((128, 128)), total, 0.0)
    splats = jnp.broadcast_to(jnp.sum(diagonal, axis=1, keepdims=True), (128, 128))

    def value(k):
        return splats[k : k + 1, :]

    sy = {pair: value(k) for pair, k in SY_ROW.items()}
    yy = {pair: value(k) for pair, k in YY_ROW.items()}
    inverse = [1.0 / sy[i, i] for i in range(MEM)]
    scaling = sy[MEM - 1, MEM - 1] / yy[MEM - 1, MEM - 1]
    alpha = [None] * MEM
    for i in reversed(range(MEM)):
        term = value(SG_ROW + i)
        for j in reversed(range(i + 1, MEM)):
            term = term - alpha[j] * sy[i, j]
        alpha[i] = term * inverse[i]
    weights = []
    for i in range(MEM):
        term = value(YG_ROW + i)
        for j in reversed(range(MEM)):
            term = term - alpha[j] * yy[min(i, j), max(i, j)]
        term = scaling * term
        for j in range(i):
            term = term + weights[j] * sy[j, i]
        weights.append(alpha[i] - term * inverse[i])

    def wide(x):
        return jnp.broadcast_to(jnp.concatenate([x, x], 1), (16, N))

    scale = wide(scaling)
    step_weights = [wide(w) for w in weights]
    change_weights = [wide(scaling * a) for a in alpha]

    def body(k, carry):
        q = k // (N // 16)
        rows = pl.ds((k % (N // 16)) * 16, 16)
        s, part = q // 2, q % 2
        acc = scale * gradient[s, part, rows, :]
        for j in range(MEM):
            acc = acc - change_weights[j] * changes[j, s, part, rows, :].astype(F32)
            acc = acc + step_weights[j] * steps[j, s, part, rows, :].astype(F32)
        out[s, part, rows, :] = obj[s, part, rows, :] - acc
        return carry

    lax.fori_loop(0, 4 * (N // 16), body, 0)


def shape(*dims, dtype=F32):
    return jax.ShapeDtypeStruct(dims, dtype)


def scratch(*dims, dtype=F32):
    return pltpu.VMEM(dims, dtype)


def call(kernel, outs, scratches, args, smem=0):
    return pl.pallas_call(
        kernel,
        out_shape=outs,
        in_specs=[SMEM] * smem + [VMEM] * (len(args) - smem),
        out_specs=jax.tree.map(lambda _: VMEM, outs),
        scratch_shapes=scratches,
        compiler_params=PARAMS,
    )(*args)


def shifted(value, axis, step):
    size = lax.axis_size(axis)
    return lax.ppermute(value, axis, [(i, (i + step) % size) for i in range(size)])


def packed(value, columns):
    return jnp.concatenate([value[:, 0, :, columns], value[:, 1, :, columns]], -1)


def near_pairs(rows, modes):
    half = rows // modes
    pairs = []
    for t in range(rows):
        for m in range(modes):
            y = m * modes + t // half
            other = 2 * modes - 1 - y
            target = (other % modes) * half + t % half
            pairs.append((t * modes + m, target * modes + other // modes))
    return pairs


def per_device(object_field, probe, patterns, offsets, phase, past_steps, past_changes):
    rows_axis, modes_axis = lax.axis_size("ty"), lax.axis_size("mode")
    core = lax.axis_index("ty") % 2
    tables = dft_tables()
    kernel = jnp.stack([jnp.cos(phase), jnp.sin(phase)])
    chosen = lax.dynamic_slice_in_dim(probe, core, 1, 0)[0]
    near = lax.ppermute(chosen, ("ty", "mode"), near_pairs(rows_axis, modes_axis))
    first, last = slice(0, HALO), slice(N - HALO, N)
    top = shifted(object_field[:, :, last, :], "ty", 1)
    bottom = shifted(object_field[:, :, first, :], "ty", -1)
    left = shifted(packed(object_field, last), "tx", 1)
    right = shifted(packed(object_field, first), "tx", -1)
    strips = jnp.concatenate([bottom, top], 2)
    corner_left = shifted(packed(strips, last), "tx", 1)
    corner_right = shifted(packed(strips, first), "tx", -1)
    near, left, right, corner_left, corner_right = lax.optimization_barrier(
        (near, left, right, corner_left, corner_right))
    swapped = lax.ppermute(near, "ty", [(i, i ^ 1) for i in range(rows_axis)])
    gram = call(gram_kernel, shape(32, 128), [], (past_steps, past_changes))
    work = [scratch(2, N, 2 * N, dtype=BF16), scratch(2, 2 * N, 2 * N, dtype=BF16), scratch(2, N, 2 * N)]
    window, psi1, far, intensity = call(
        own_kernel,
        (shape(2, N, 2 * N), shape(2, N, 2 * N), shape(2, N, 2 * N), shape(N, N)),
        [scratch(4, FRAME + 8, FRAME)] + work,
        (offsets, object_field, top, bottom, left, right, corner_left, corner_right, probe, kernel) + tables,
        smem=1,
    )
    strip, side, corner = shape(2, 2, HALO, N), shape(2, N, 2 * HALO), shape(2, 2 * HALO, 2 * HALO)
    partial, row_top, row_bottom, col_left, col_right, corner_left, corner_right = call(
        other_kernel,
        (shape(2, 2, N, N), strip, strip, side, side, corner, corner),
        [scratch(2, N, 2 * N), scratch(2, N, 2 * N), scratch(N, N)] + work
        + [scratch(2, N, 2 * N), scratch(4, FRAME + 8, FRAME)],
        (offsets, object_field, probe, near, swapped, kernel) + tables
        + (patterns, window, psi1, far, intensity),
        smem=1,
    )
    from_left = shifted(corner_right, "tx", 1)
    from_right = shifted(corner_left, "tx", -1)
    side_left = shifted(col_right, "tx", 1)
    side_right = shifted(col_left, "tx", -1)

    def with_corners(strip_now, rows):
        def unpacked(block):
            return jnp.stack([block[:, rows, :HALO], block[:, rows, HALO:]], 1)

        gap = jnp.zeros(strip_now.shape[:3] + (N - 2 * HALO,), F32)
        return strip_now + jnp.concatenate([unpacked(from_left), gap, unpacked(from_right)], -1)

    row_up = shifted(with_corners(row_bottom, slice(0, HALO)), "ty", 1)
    row_down = shifted(with_corners(row_top, slice(HALO, 2 * HALO)), "ty", -1)
    gradient, sums = call(
        dots_kernel,
        (shape(2, 2, N, N), shape(128, 1, 128)),
        [scratch(128, 128)],
        (partial, row_up, row_down, side_left, side_right, past_steps, past_changes, gram),
    )
    parts = lax.all_to_all(sums, TILES, 0, 0)
    new_object = call(
        final_kernel, shape(2, 2, N, N), [], (parts, object_field, gradient, past_steps, past_changes))
    return (new_object, gradient)


def solution(mesh):
    placed = (
        P(None, None, "ty", "tx"),
        P("mode", None, None),
        P(TILES, None, None),
        P(TILES, None),
        P(),
        P(None, None, None, "ty", "tx"),
        P(None, None, None, "ty", "tx"),
    )
    return jax.shard_map(
        per_device,
        mesh=mesh,
        in_specs=placed,
        out_specs=(P(None, None, "ty", "tx"), P(None, None, "ty", "tx")),
        check_vma=False,
    )
```

time: 1050 us -> 88.7 us (0.08)
  blocking collectives: 740 us -> 22.1 us
  waiting for transfers between devices: 105 us -> 7.2 us
  other arithmetic: 65 us -> 0.67 us
  local copies, waits for them, and re-layouts: 68 us -> 5.16 us
  between operations: 32.9 us -> 1.01 us
  Pallas kernels: 0 us -> 25.2 us
  matrix products: 17.9 us -> 0 us
  starting transfers between devices: 16.2 us -> 27.1 us
    psum x10 -> x0, blocking collectives: 740 us -> none  [global_sums(): return lax.psum(values, ('ty', 'tx', 'mode'))]
    psum x2 -> x0, waiting for transfers between devices: 83.4 us -> none  [the longest x1 52.3 us: per_device(): gradient = lax.psum(tile_gradient, 'mode') + REG_WEIGHT * object_field]
    pallas_call x0 -> x5, Pallas kernels: none -> 25.2 us  [call(): pl.pallas_call(kernel, out_shape=outs, in_specs=[SMEM] * smem + [VMEM] *...]
    add x13 -> x1, other arithmetic: 22.9 us -> 0.15 us  [with_corners(): strip_now + jnp.concatenate([unpacked(from_left), gap, unpacked(from_righ...]
    all_to_all x0 -> x1, blocking collectives: none -> 22.1 us  [per_device(): parts = lax.all_to_all(sums, TILES, 0, 0)]
    dot_general x6 -> x0, matrix products: 17.9 us -> none  [transform(): jnp.einsum('jk,bkl->bjl', tables[2], first_pass, preferred_element_type=j...]
    ppermute x8 -> x14, waiting for transfers between devices: 21.7 us -> 7.2 us  [the longest x12 7.2 us: shifted(): lax.ppermute(value, axis, [(i, (i + step) % size) for i in range(size)])]
    reduce_sum x13 -> x0, other arithmetic: 14.3 us -> none  [the longest x10 13.4 us: inner_product(): return jnp.sum(first.astype(jnp.float32) * second.astype(jnp.float32))]
  transfers between devices with their start and end apart: 10 -> 14, of which waited for: 8 -> 5; matrix products, arithmetic and copies ran while one was open for 3% -> 4% of each run, Pallas kernels for 0% -> 9%
where the time goes in v1:
time: 88.7 us; the launch traced here: 88.5 us
  starting transfers between devices  27.1 us (31%)
  Pallas kernels  25.2 us (28%)
  blocking collectives  22.1 us (25%)
  waiting for transfers between devices  7.2 us (8%)
  local copies, waits for them, and re-layouts  5.16 us (6%)
  between operations  1.01 us (1%)
    pallas_call x5, Pallas kernels, call(): pl.pallas_call(kernel, out_shape=outs, in_specs=[SMEM] * smem + [VMEM] *...  25.2 us
    all_to_all x1, blocking collectives, per_device(): parts = lax.all_to_all(sums, TILES, 0, 0)  22.1 us
    ppermute x12, starting transfers between devices, shifted(): lax.ppermute(value, axis, [(i, (i + step) % size) for i in range(size)])  18.1 us
    ppermute x12, waiting for transfers between devices, shifted(): lax.ppermute(value, axis, [(i, (i + step) % size) for i in range(size)])  7.2 us
    ppermute x1, starting transfers between devices, per_device(): swapped = lax.ppermute(near, 'ty', [(i, i ^ 1) for i in range(rows_axis)])  5.38 us
    ppermute x1, starting transfers between devices, per_device(): lax.ppermute(chosen, ('ty', 'mode'), near_pairs(rows_axis, modes_axis))  3.65 us
  transfers between devices with their start and end apart: 14, of which 5 were waited for; matrix products, arithmetic and copies ran while one was open for 4% of the time, Pallas kernels for 9%

profile of v1, /device:TPU:1, one launch (start us, length us, event | category | flops | bytes accessed | tf_op | source)
XLA Modules:
  0.0 88.5 jit_solution(4242519095696702331)
XLA Ops:
  0.7 1.2 %dynamic-slice_bitcast_fusion = f32[256,512]{1,0:T(8,128)S(1)} fusion(f32[2,256,512]{2,1,0:T(8,128)} %probe.3, s32[]{:T(128)S(6)} %select_n.11), kind=kLoop, calls=%fused_computation.1 | loop fusion | bytes 1048580 | tf_op jit(solution)/shard_map/squeeze | solution.py:392
  1.8 3.7 %collective-permute-start = (f32[256,512]{1,0:T(8,128)S(1)}, f32[256,512]{1,0:T(8,128)S(1)}, u32[]{:S(2)}, u32[]{:S(2)}) collective-permute-start(f32[256,512]{1,0:T(8,128)S(1)} %dynamic-slice_bitcast_fusion), channel_id=1, source_target_pairs={{0,129},{1,128},{16,145},{17,144},{32,161},{33,160},{48,177},{49,1... | collective-permute-start | bytes 1572872 | tf_op jit(solution)/shard_map/ppermute | solution.py:393
  5.5 1.1 %fusion = (f32[2,2,64,256]{3,2,1,0:T(8,128)S(1)}, f32[2,2,64,256]{3,2,1,0:T(8,128)S(1)}) fusion(f32[2,2,256,256]{3,2,1,0:T(8,128)} %obj.5), kind=kLoop, calls=%fused_computation.30 | loop fusion | bytes 1048576 | tf_op jit(solution)/shard_map/slice | solution.py:395
  6.6 1.0 %collective-permute-start.3 = (f32[2,2,64,256]{3,2,0,1:T(8,128)S(1)}, f32[2,2,64,256]{3,2,0,1:T(8,128)S(1)}, u32[]{:S(2)}, u32[]{:S(2)}) collective-permute-start(f32[2,2,64,256]{3,2,0,1:T(8,128)S(1)} %copy.28), channel_id=1, source_target_pairs={{0,240},{16,0},{32,16},{48,32},{64,48},{80,64},{96,80},{112,96},{1... | collective-permute-start | bytes 786440 | tf_op jit(solution)/shard_map/ppermute | solution.py:368
  7.6 1.2 %collective-permute-start.4 = (f32[2,2,64,256]{3,2,0,1:T(8,128)S(1)}, f32[2,2,64,256]{3,2,0,1:T(8,128)S(1)}, u32[]{:S(2)}, u32[]{:S(2)}) collective-permute-start(f32[2,2,64,256]{3,2,0,1:T(8,128)S(1)} %copy.29), channel_id=1, source_target_pairs={{0,16},{16,32},{32,48},{48,64},{64,80},{80,96},{96,112},{112,128},... | collective-permute-start | bytes 786440 | tf_op jit(solution)/shard_map/ppermute | solution.py:368
  8.8 0.2 slice_bitcast_fusion.1
  9.0 0.1 pad_maximum_fusion.1
  9.2 1.7 %collective-permute-start.1 = (f32[2,256,128]{2,1,0:T(8,128)S(1)}, f32[2,256,128]{2,1,0:T(8,128)S(1)}, u32[]{:S(2)}, u32[]{:S(2)}) collective-permute-start(f32[2,256,128]{2,1,0:T(8,128)S(1)} %pad_maximum_fusion.1), channel_id=1, source_target_pairs={{0,2},{2,4},{4,6},{6,8},{8,10},{10,12},{12,14},{14,0},{1,3},{3,5},... | collective-permute-start | bytes 786440 | tf_op jit(solution)/shard_map/ppermute | solution.py:368
  10.9 0.1 pad_maximum_fusion.2
  11.0 4.0 %collective-permute-start.2 = (f32[2,256,128]{2,1,0:T(8,128)S(1)}, f32[2,256,128]{2,1,0:T(8,128)S(1)}, u32[]{:S(2)}, u32[]{:S(2)}) collective-permute-start(f32[2,256,128]{2,1,0:T(8,128)S(1)} %pad_maximum_fusion.2), channel_id=1, source_target_pairs={{0,14},{2,0},{4,2},{6,4},{8,6},{10,8},{12,10},{14,12},{1,15},{3,1}... | collective-permute-start | bytes 786440 | tf_op jit(solution)/shard_map/ppermute | solution.py:368
  15.2 0.1 slice_bitcast_fusion.5
  15.3 0.1 pad_maximum_fusion.4
  15.4 3.6 %collective-permute-start.6 = (f32[2,128,128]{2,1,0:T(8,128)S(1)}, f32[2,128,128]{2,1,0:T(8,128)S(1)}, u32[]{:S(2)}, u32[]{:S(2)}) collective-permute-start(f32[2,128,128]{2,1,0:T(8,128)S(1)} %pad_maximum_fusion.4), channel_id=1, source_target_pairs={{0,14},{2,0},{4,2},{6,4},{8,6},{10,8},{12,10},{14,12},{1,15},{3,1}... | collective-permute-start | bytes 393224 | tf_op jit(solution)/shard_map/ppermute | solution.py:368
  19.1 0.1 pad_maximum_fusion.3
  19.3 1.9 %collective-permute-done.1.left_in = f32[2,256,128]{2,1,0:T(8,128)S(1)} collective-permute-done((f32[2,256,128]{2,1,0:T(8,128)S(1)}, f32[2,256,128]{2,1,0:T(8,128)S(1)}, u32[]{:S(2)}, u32[]{:S(2)}) %collective-permute-start.1) | collective-permute-done | bytes 262176 | tf_op jit(solution)/shard_map/ppermute | solution.py:368
  21.2 1.4 %collective-permute-done.6.corner_right = f32[2,128,128]{2,1,0:T(8,128)S(1)} collective-permute-done((f32[2,128,128]{2,1,0:T(8,128)S(1)}, f32[2,128,128]{2,1,0:T(8,128)S(1)}, u32[]{:S(2)}, u32[]{:S(2)}) %collective-permute-start.6) | collective-permute-done | bytes 131104 | tf_op jit(solution)/shard_map/ppermute | solution.py:368
  22.6 1.7 %collective-permute-done.5.corner_left = f32[2,128,128]{2,1,0:T(8,128)S(1)} collective-permute-done((f32[2,128,128]{2,1,0:T(8,128)S(1)}, f32[2,128,128]{2,1,0:T(8,128)S(1)}, u32[]{:S(2)}, u32[]{:S(2)}) %collective-permute-start.5) | collective-permute-done | bytes 131104 | tf_op jit(solution)/shard_map/ppermute | solution.py:368
  24.3 5.4 %collective-permute-start.7 = (f32[256,512]{1,0:T(8,128)S(1)}, f32[256,512]{1,0:T(8,128)S(1)}, u32[]{:S(2)}, u32[]{:S(2)}) collective-permute-start(f32[256,512]{1,0:T(8,128)S(1)} %collective-permute-done.near), channel_id=1, source_target_pairs={{0,16},{16,0},{32,48},{48,32},{64,80},{80,64},{96,112},{112,96},{1... | collective-permute-start | bytes 1572872 | tf_op jit(solution)/shard_map/ppermute | solution.py:404
  29.7 0.9 %cosine_bitcast_fusion = (f32[1,256,256]{2,1,0:T(8,128)S(1)}, f32[1,256,256]{2,1,0:T(8,128)S(1)}) fusion(f32[256,256]{1,0:T(8,128)S(1)} %copy-done.10), kind=kLoop, calls=%fused_computation.7 | loop fusion | bytes 786432 | tf_op jit(solution)/shard_map/stack | solution.py:391
  30.8 4.1 %shard_map.113 = (f32[2,256,512]{2,1,0:T(8,128)S(1)}, f32[2,256,512]{2,1,0:T(8,128)S(1)}, f32[2,256,512]{2,1,0:T(8,128)S(1)}, f32[256,256]{1,0:T(8,128)S(1)}) custom-call(s32[1,2]{1,0:T(1,128)S(1)} %copy-done.9, f32[2,2,256,256]{3,2,1,0:T(8,128)S(1)} %copy-done.2, f32[2,2,64,256]{3,2,1,0:T(8,128)S(1)} %copy.18.top, f32[2,2,64,256]{3,2,1,0:T(8,128)S(1)} %copy.19.bottom, ...), custom_call_target="tpu_custom_call" | custom-call | tf_op jit(solution)/shard_map/pallas_call | solution.py:356
  34.9 10.2 %shard_map.114 = (f32[2,2,256,256]{3,2,1,0:T(8,128)S(1)}, f32[2,2,64,256]{3,2,1,0:T(8,128)S(1)}, f32[2,2,64,256]{3,2,1,0:T(8,128)S(1)}, f32[2,256,128]{2,1,0:T(8...) custom-call(s32[1,2]{1,0:T(1,128)S(1)} %copy-done.9, ...), custom_call_target="tpu_custom_call" | custom-call | tf_op jit(solution)/shard_map/pallas_call | solution.py:356
  45.3 2.7 %collective-permute-start.9 = (f32[2,128,128]{2,1,0:T(8,128)S(1)}, f32[2,128,128]{2,1,0:T(8,128)S(1)}, u32[]{:S(2)}, u32[]{:S(2)}) collective-permute-start(f32[2,128,128]{2,1,0:T(8,128)S(1)} %get-tuple-element.32), channel_id=1, source_target_pairs={{0,14},{2,0},{4,2},{6,4},{8,6},{10,8},{12,10},{14,12},{1,15},{3,1}... | collective-permute-start | bytes 393224 | tf_op jit(solution)/shard_map/ppermute | solution.py:368
  48.0 2.7 %collective-permute-start.13 = (f32[2,256,128]{2,1,0:T(8,128)S(1)}, f32[2,256,128]{2,1,0:T(8,128)S(1)}, u32[]{:S(2)}, u32[]{:S(2)}) collective-permute-start(f32[2,256,128]{2,1,0:T(8,128)S(1)} %get-tuple-element.35), channel_id=1, source_target_pairs={{0,14},{2,0},{4,2},{6,4},{8,6},{10,8},{12,10},{14,12},{1,15},{3,1}... | collective-permute-start | bytes 786440 | tf_op jit(solution)/shard_map/ppermute | solution.py:368
  50.7 0.9 collective-permute-done.8
  51.8 0.1 maximum_add_fusion.1
  52.0 0.9 collective-permute-start.11
  52.9 4.0 %shard_map.115.gram = f32[32,128]{1,0:T(8,128)S(1)} custom-call(bf16[5,2,2,256,256]{4,3,2,1,0:T(8,128)(2,1)S(1)} %copy-done, bf16[5,2,2,256,256]{4,3,2,1,0:T(8,128)(2,1)S(1)} %copy-done.1), custom_call_target="tpu_custom_call" | custom-call | tf_op jit(solution)/shard_map/pallas_call | solution.py:356
  56.9 1.3 %collective-permute-done.11.row_down = f32[2,2,64,256]{3,2,1,0:T(8,128)S(1)} collective-permute-done((f32[2,2,64,256]{3,2,1,0:T(8,128)S(1)}, f32[2,2,64,256]{3,2,1,0:T(8,128)S(1)}, u32[]{:S(2)}, u32[]{:S(2)}) %collective-permute-start.11) | collective-permute-done | bytes 262176 | tf_op jit(solution)/shard_map/ppermute | solution.py:368
  58.2 3.4 %shard_map.116 = (f32[2,2,256,256]{3,2,1,0:T(8,128)}, f32[128,1,128]{2,1,0:T(1,128)S(1)}) custom-call(f32[2,2,256,256]{3,2,1,0:T(8,128)S(1)} %get-tuple-element.29.gradient_in, f32[2,2,64,256]{3,2,1,0:T(8,128)S(1)} %collective-permute-done.10.row_up, f32[2,2,64,256]{3,2,1,0:T(8,128)S(1)} %collective-permute-done.11.row_down, ...), custom_call_target="tpu_custom_call" | custom-call | tf_op jit(solution)/shard_map/pallas_call | solution.py:356
  61.6 22.1 %all_to_all.5.parts = f32[128,1,128]{2,1,0:T(1,128)S(1)} all-to-all(f32[128,1,128]{2,1,0:T(1,128)S(1)} %get-tuple-element.36), channel_id=1, replica_groups=mesh['ty'=16,'tx'=8,'mode'=2] {'ty','tx'}, dimensions={0} | all-to-all | bytes 131072 | tf_op jit(solution)/shard_map/all_to_all | solution.py:444
  83.7 1.2 %copy-done.6 = f32[2,2,256,256]{3,2,1,0:T(8,128)S(1)} copy-done((f32[2,2,256,256]{3,2,1,0:T(8,128)S(1)}, f32[2,2,256,256]{3,2,1,0:T(8,128)}, u32[]{:S(2)}) %copy-start.6) | copy-done | bytes 1048600
  85.0 3.5 %shard_map.117 = f32[2,2,256,256]{3,2,1,0:T(8,128)} custom-call(f32[128,1,128]{2,1,0:T(1,128)S(1)} %all_to_all.5.parts, f32[2,2,256,256]{3,2,1,0:T(8,128)S(1)} %copy-done.2, f32[2,2,256,256]{3,2,1,0:T(8,128)S(1)} %copy-done.6, bf16[5,2,2,256,256]{4,3,2,1,0:T(8,128)(2,1)S(1)} %copy-done, bf16[5,2,2,256,256]{4,3,2,1,0:T(8,128)(2,1)S(1)} %copy-done.1), custom_call_target="tpu_custom_call" | custom-call | tf_op jit(solution)/shard_map/pallas_call | solution.py:356
  (46 shorter events, 0.8 us)
Async XLA Ops:
  0.6 8.2 %copy-start.2 = (f32[2,2,256,256]{3,2,1,0:T(8,128)S(1)}, f32[2,2,256,256]{3,2,1,0:T(8,128)}, u32[]{:S(2)}) copy-start(f32[2,2,256,256]{3,2,1,0:T(8,128)} %obj.5) | copy-start | bytes 3145732
  1.8 22.5 %collective-permute-start = (f32[256,512]{1,0:T(8,128)S(1)}, f32[256,512]{1,0:T(8,128)S(1)}, u32[]{:S(2)}, u32[]{:S(2)}) collective-permute-start(f32[256,512]{1,0:T(8,128)S(1)} %dynamic-slice_bitcast_fusion), channel_id=1, source_target_pairs={{0,129},{1,128},{16,145},{17,144},{32,161},{33,160},{48,177},{49,1... | collective-permute-start | bytes 1572872 | tf_op jit(solution)/shard_map/ppermute | solution.py:393
  6.6 8.5 %collective-permute-start.3 = (f32[2,2,64,256]{3,2,0,1:T(8,128)S(1)}, f32[2,2,64,256]{3,2,0,1:T(8,128)S(1)}, u32[]{:S(2)}, u32[]{:S(2)}) collective-permute-start(f32[2,2,64,256]{3,2,0,1:T(8,128)S(1)} %copy.28), channel_id=1, source_target_pairs={{0,240},{16,0},{32,16},{48,32},{64,48},{80,64},{96,80},{112,96},{1... | collective-permute-start | bytes 786440 | tf_op jit(solution)/shard_map/ppermute | solution.py:368
  7.6 7.5 %collective-permute-start.4 = (f32[2,2,64,256]{3,2,0,1:T(8,128)S(1)}, f32[2,2,64,256]{3,2,0,1:T(8,128)S(1)}, u32[]{:S(2)}, u32[]{:S(2)}) collective-permute-start(f32[2,2,64,256]{3,2,0,1:T(8,128)S(1)} %copy.29), channel_id=1, source_target_pairs={{0,16},{16,32},{32,48},{48,64},{64,80},{80,96},{96,112},{112,128},... | collective-permute-start | bytes 786440 | tf_op jit(solution)/shard_map/ppermute | solution.py:368
  9.0 20.6 %copy-start.10 = (f32[256,256]{1,0:T(8,128)S(1)}, f32[256,256]{1,0:T(8,128)}, u32[]{:S(2)}) copy-start(f32[256,256]{1,0:T(8,128)} %param.14) | copy-start | bytes 786436
  9.2 12.0 %collective-permute-start.1 = (f32[2,256,128]{2,1,0:T(8,128)S(1)}, f32[2,256,128]{2,1,0:T(8,128)S(1)}, u32[]{:S(2)}, u32[]{:S(2)}) collective-permute-start(f32[2,256,128]{2,1,0:T(8,128)S(1)} %pad_maximum_fusion.1), channel_id=1, source_target_pairs={{0,2},{2,4},{4,6},{6,8},{8,10},{10,12},{12,14},{14,0},{1,3},{3,5},... | collective-permute-start | bytes 786440 | tf_op jit(solution)/shard_map/ppermute | solution.py:368
  11.0 10.1 %collective-permute-start.2 = (f32[2,256,128]{2,1,0:T(8,128)S(1)}, f32[2,256,128]{2,1,0:T(8,128)S(1)}, u32[]{:S(2)}, u32[]{:S(2)}) collective-permute-start(f32[2,256,128]{2,1,0:T(8,128)S(1)} %pad_maximum_fusion.2), channel_id=1, source_target_pairs={{0,14},{2,0},{4,2},{6,4},{8,6},{10,8},{12,10},{14,12},{1,15},{3,1}... | collective-permute-start | bytes 786440 | tf_op jit(solution)/shard_map/ppermute | solution.py:368
  15.1 15.6 %copy-start.3 = (f32[2,256,512]{2,1,0:T(8,128)S(1)}, f32[2,256,512]{2,1,0:T(8,128)}, u32[]{:S(2)}) copy-start(f32[2,256,512]{2,1,0:T(8,128)} %probe.3) | copy-start | bytes 3145732
  15.1 15.6 %copy-start.4 = (bf16[512,512]{1,0:T(8,128)(2,1)S(1)}, bf16[512,512]{1,0:T(8,128)(2,1)}, u32[]{:S(2)}) copy-start(bf16[512,512]{1,0:T(8,128)(2,1)} %constant.27.clone.fwd_t) | copy-start | bytes 1572868
  15.1 15.6 %copy-start.5 = (bf16[512,512]{1,0:T(8,128)(2,1)S(1)}, bf16[512,512]{1,0:T(8,128)(2,1)}, u32[]{:S(2)}) copy-start(bf16[512,512]{1,0:T(8,128)(2,1)} %constant.28.clone.inv_t) | copy-start | bytes 1572868
  15.1 15.6 %copy-start.7 = (bf16[256,512]{1,0:T(8,128)(2,1)S(1)}, bf16[256,512]{1,0:T(8,128)(2,1)}, u32[]{:S(2)}) copy-start(bf16[256,512]{1,0:T(8,128)(2,1)} %constant.29.clone.left_t) | copy-start | bytes 786436
  15.1 15.6 %copy-start.9 = (s32[1,2]{1,0:T(1,128)S(1)}, s32[1,2]{1,0:T(1,128)}, u32[]{:S(2)}) copy-start(s32[1,2]{1,0:T(1,128)} %offsets.3) | copy-start | bytes 28
  15.4 7.2 %collective-permute-start.6 = (f32[2,128,128]{2,1,0:T(8,128)S(1)}, f32[2,128,128]{2,1,0:T(8,128)S(1)}, u32[]{:S(2)}, u32[]{:S(2)}) collective-permute-start(f32[2,128,128]{2,1,0:T(8,128)S(1)} %pad_maximum_fusion.4), channel_id=1, source_target_pairs={{0,14},{2,0},{4,2},{6,4},{8,6},{10,8},{12,10},{14,12},{1,15},{3,1}... | collective-permute-start | bytes 393224 | tf_op jit(solution)/shard_map/ppermute | solution.py:368
  19.2 5.1 %collective-permute-start.5 = (f32[2,128,128]{2,1,0:T(8,128)S(1)}, f32[2,128,128]{2,1,0:T(8,128)S(1)}, u32[]{:S(2)}, u32[]{:S(2)}) collective-permute-start(f32[2,128,128]{2,1,0:T(8,128)S(1)} %pad_maximum_fusion.3), channel_id=1, source_target_pairs={{0,2},{2,4},{4,6},{6,8},{8,10},{10,12},{12,14},{14,0},{1,3},{3,5},... | collective-permute-start | bytes 393224 | tf_op jit(solution)/shard_map/ppermute | solution.py:368
  24.3 10.6 %collective-permute-start.7 = (f32[256,512]{1,0:T(8,128)S(1)}, f32[256,512]{1,0:T(8,128)S(1)}, u32[]{:S(2)}, u32[]{:S(2)}) collective-permute-start(f32[256,512]{1,0:T(8,128)S(1)} %collective-permute-done.near), channel_id=1, source_target_pairs={{0,16},{16,0},{32,48},{48,32},{64,80},{80,64},{96,112},{112,96},{1... | collective-permute-start | bytes 1572872 | tf_op jit(solution)/shard_map/ppermute | solution.py:404
  30.8 4.1 %copy-start.8 = (f32[1,256,256]{2,1,0:T(8,128)S(1)}, f32[1,256,256]{2,1,0:T(8,128)}, u32[]{:S(2)}) copy-start(f32[1,256,256]{2,1,0:T(8,128)} %patterns.1) | copy-start | bytes 786436
  34.9 18.0 %copy-start.1 = (bf16[5,2,2,256,256]{4,3,2,1,0:T(8,128)(2,1)S(1)}, bf16[5,2,2,256,256]{4,3,2,1,0:T(8,128)(2,1)}, u32[]{:S(2)}) copy-start(bf16[5,2,2,256,256]{4,3,2,1,0:T(8,128)(2,1)} %changes.5) | copy-start | bytes 7864324
  45.2 7.8 %copy-start = (bf16[5,2,2,256,256]{4,3,2,1,0:T(8,128)(2,1)S(1)}, bf16[5,2,2,256,256]{4,3,2,1,0:T(8,128)(2,1)}, u32[]{:S(2)}) copy-start(bf16[5,2,2,256,256]{4,3,2,1,0:T(8,128)(2,1)} %steps.5) | copy-start | bytes 7864324
  45.2 6.4 %collective-permute-start.8 = (f32[2,128,128]{2,1,0:T(8,128)S(1)}, f32[2,128,128]{2,1,0:T(8,128)S(1)}, u32[]{:S(2)}, u32[]{:S(2)}) collective-permute-start(f32[2,128,128]{2,1,0:T(8,128)S(1)} %get-tuple-element.31), channel_id=1, source_target_pairs={{0,2},{2,4},{4,6},{6,8},{8,10},{10,12},{12,14},{14,0},{1,3},{3,5},... | collective-permute-start | bytes 393224 | tf_op jit(solution)/shard_map/ppermute | solution.py:368
  45.3 6.4 %collective-permute-start.9 = (f32[2,128,128]{2,1,0:T(8,128)S(1)}, f32[2,128,128]{2,1,0:T(8,128)S(1)}, u32[]{:S(2)}, u32[]{:S(2)}) collective-permute-start(f32[2,128,128]{2,1,0:T(8,128)S(1)} %get-tuple-element.32), channel_id=1, source_target_pairs={{0,14},{2,0},{4,2},{6,4},{8,6},{10,8},{12,10},{14,12},{1,15},{3,1}... | collective-permute-start | bytes 393224 | tf_op jit(solution)/shard_map/ppermute | solution.py:368
  48.0 8.9 %collective-permute-start.12 = (f32[2,256,128]{2,1,0:T(8,128)S(1)}, f32[2,256,128]{2,1,0:T(8,128)S(1)}, u32[]{:S(2)}, u32[]{:S(2)}) collective-permute-start(f32[2,256,128]{2,1,0:T(8,128)S(1)} %get-tuple-element.34), channel_id=1, source_target_pairs={{0,2},{2,4},{4,6},{6,8},{8,10},{10,12},{12,14},{14,0},{1,3},{3,5},... | collective-permute-start | bytes 786440 | tf_op jit(solution)/shard_map/ppermute | solution.py:368
  48.0 8.9 %collective-permute-start.13 = (f32[2,256,128]{2,1,0:T(8,128)S(1)}, f32[2,256,128]{2,1,0:T(8,128)S(1)}, u32[]{:S(2)}, u32[]{:S(2)}) collective-permute-start(f32[2,256,128]{2,1,0:T(8,128)S(1)} %get-tuple-element.35), channel_id=1, source_target_pairs={{0,14},{2,0},{4,2},{6,4},{8,6},{10,8},{12,10},{14,12},{1,15},{3,1}... | collective-permute-start | bytes 786440 | tf_op jit(solution)/shard_map/ppermute | solution.py:368
  52.0 5.0 %collective-permute-start.10 = (f32[2,2,64,256]{3,2,1,0:T(8,128)S(1)}, f32[2,2,64,256]{3,2,1,0:T(8,128)S(1)}, u32[]{:S(2)}, u32[]{:S(2)}) collective-permute-start(f32[2,2,64,256]{3,2,1,0:T(8,128)S(1)} %get-tuple-element.59), channel_id=1, source_target_pairs={{0,16},{16,32},{32,48},{48,64},{64,80},{80,96},{96,112},{112,128},... | collective-permute-start | bytes 786440 | tf_op jit(solution)/shard_map/ppermute | solution.py:368
  52.0 6.2 %collective-permute-start.11 = (f32[2,2,64,256]{3,2,1,0:T(8,128)S(1)}, f32[2,2,64,256]{3,2,1,0:T(8,128)S(1)}, u32[]{:S(2)}, u32[]{:S(2)}) collective-permute-start(f32[2,2,64,256]{3,2,1,0:T(8,128)S(1)} %get-tuple-element.58), channel_id=1, source_target_pairs={{0,240},{16,0},{32,16},{48,32},{64,48},{80,64},{96,80},{112,96},{1... | collective-permute-start | bytes 786440 | tf_op jit(solution)/shard_map/ppermute | solution.py:368
  83.7 1.2 %copy-start.6 = (f32[2,2,256,256]{3,2,1,0:T(8,128)S(1)}, f32[2,2,256,256]{3,2,1,0:T(8,128)}, u32[]{:S(2)}) copy-start(f32[2,2,256,256]{3,2,1,0:T(8,128)} %get-tuple-element.19.gradient) | copy-start | bytes 3145732

commit v2 on v1

v2 whole, which is shorter than its diff:
```python
import math

import jax
import jax.numpy as jnp
import numpy as np
from jax import lax
from jax.experimental import pallas as pl
from jax.experimental.pallas import tpu as pltpu
from jax.sharding import PartitionSpec as P

MODES = 4
HALO = 64
REG_WEIGHT = 1.0
N = 256
FRAME = N + 2 * HALO
MEM = 5
CHUNK = 32
F32 = jnp.float32
BF16 = jnp.bfloat16
TILES = ("ty", "tx")
VMEM = pl.BlockSpec(memory_space=pltpu.VMEM)
ANY = pl.BlockSpec(memory_space=pltpu.HBM)
SMEM = pl.BlockSpec(memory_space=pltpu.SMEM)
PARAMS = pltpu.CompilerParams(vmem_limit_bytes=40 * 1024 * 1024)
SY_PAIRS = [(i, j) for i in range(MEM) for j in range(i, MEM)]
SY_ROW = {pair: k for k, pair in enumerate(SY_PAIRS)}
YY_ROW = {pair: len(SY_PAIRS) + k for k, pair in enumerate(SY_PAIRS)}
SG_ROW = 2 * len(SY_PAIRS)
YG_ROW = SG_ROW + MEM
ROWS = YG_ROW + MEM


def dft_tables():
    indices = np.arange(N, dtype=np.int32)
    products = indices[:, None] * indices[None, :] % N
    angles = products.astype(np.float32) * np.float32(2.0 * math.pi / N)
    cosine = (np.cos(angles) / np.float32(math.sqrt(N))).astype(np.float32)
    sine = (np.sin(angles) / np.float32(math.sqrt(N))).astype(np.float32)
    forward = np.block([[cosine, -sine], [sine, cosine]])
    inverse = np.block([[cosine, sine], [-sine, cosine]])
    left = np.concatenate([cosine, sine], 1)
    return tuple(jnp.asarray(t, BF16) for t in (forward, inverse, left))


def lanes(shape):
    return lax.broadcasted_iota(jnp.int32, shape, len(shape) - 1)


def chunks(total=N, step=CHUNK):
    return [slice(c, c + step) for c in range(0, total, step)]


def aligned(offset):
    base = pl.multiple_of((offset // 8) * 8, 8)
    return base, offset - base


def product(a, b, conjugate):
    ar, ai = a
    br, bi = b
    if conjugate:
        return ar * br + ai * bi, ar * bi - ai * br
    return ar * br - ai * bi, ar * bi + ai * br


def halves(ref, index, rows):
    return ref[index, rows, 0:N], ref[index, rows, N : 2 * N]


def first_pass(xb, ks, m, right, inverse):
    y = jnp.dot(xb[m], right[...], preferred_element_type=F32).astype(BF16)
    yr, yi = y[:, :N], y[:, N:]
    ks[m, 0:N, :] = y
    if inverse:
        ks[m, N : 2 * N, 0:N] = -yi
        ks[m, N : 2 * N, N : 2 * N] = yr
    else:
        ks[m, N : 2 * N, 0:N] = yi
        ks[m, N : 2 * N, N : 2 * N] = -yr


def second_pass(ks, m, left):
    return jnp.dot(left[...], ks[m], preferred_element_type=F32)


def propagate(xb, ks, zs, m, kernel, tables, adjoint):
    forward, inverse, left = tables
    first_pass(xb, ks, m, forward, False)
    yield
    zs[m] = second_pass(ks, m, left)
    yield
    for rows in chunks():
        h = (kernel[0, rows, :], kernel[1, rows, :])
        re, im = product(h, halves(zs, m, rows), adjoint)
        xb[m, rows, 0:N] = re.astype(BF16)
        xb[m, rows, N : 2 * N] = im.astype(BF16)
    yield
    first_pass(xb, ks, m, inverse, True)
    yield


def forward_mode(m, psi0, window, kernel, tables, psi1, far, xb, ks, zs):
    forward, inverse, left = tables
    for rows in chunks():
        re, im = product(halves(window, 0, rows), (psi0[rows, 0:N], psi0[rows, N : 2 * N]), False)
        xb[m, rows, 0:N] = re.astype(BF16)
        xb[m, rows, N : 2 * N] = im.astype(BF16)
    yield
    yield from propagate(xb, ks, zs, m, kernel, tables, False)
    psi1[m] = second_pass(ks, m, left)
    yield
    for rows in chunks():
        re, im = product(halves(window, 1, rows), halves(psi1, m, rows), False)
        xb[m, rows, 0:N] = re.astype(BF16)
        xb[m, rows, N : 2 * N] = im.astype(BF16)
    yield
    first_pass(xb, ks, m, forward, False)
    yield
    far[m] = second_pass(ks, m, left)
    yield


def backward_mode(slot, psi0, psi1, far, scale, window, kernel, tables, pieces, xb, ks, zs):
    forward, inverse, left = tables
    pair, m = divmod(slot, 2)
    k = slot

    def collect(s, rows, re, im):
        if m:
            re, im = re + pieces[pair, s, rows, 0:N], im + pieces[pair, s, rows, N : 2 * N]
        pieces[pair, s, rows, 0:N] = re
        pieces[pair, s, rows, N : 2 * N] = im

    for rows in chunks():
        factor = scale[rows, :]
        re, im = (far[rows, 0:N], far[rows, N : 2 * N])
        xb[k, rows, 0:N] = (factor * re).astype(BF16)
        xb[k, rows, N : 2 * N] = (factor * im).astype(BF16)
    yield
    first_pass(xb, ks, k, inverse, True)
    yield
    zs[k] = second_pass(ks, k, left)
    yield
    for rows in chunks():
        current = halves(zs, k, rows)
        collect(1, rows, *product((psi1[rows, 0:N], psi1[rows, N : 2 * N]), current, True))
        re, im = product(halves(window, 1, rows), current, True)
        xb[k, rows, 0:N] = re.astype(BF16)
        xb[k, rows, N : 2 * N] = im.astype(BF16)
    yield
    yield from propagate(xb, ks, zs, k, kernel, tables, True)
    zs[k] = second_pass(ks, k, left)
    yield
    for rows in chunks():
        collect(0, rows, *product((psi0[rows, 0:N], psi0[rows, N : 2 * N]), halves(zs, k, rows), True))
    yield


def interleave(tasks):
    waiting, running = list(tasks), []
    while waiting or running:
        if waiting:
            running.append(waiting.pop(0))
        running = [task for task in running if next(task, running) is not running]


def add_intensity(far, out):
    for rows in chunks():
        terms = []
        for m in range(2):
            re, im = halves(far, m, rows)
            terms.append(re * re + im * im)
        out[rows, :] = terms[0] + terms[1]


def pack_kernel(core, obj, probe, row_first, row_last, col_first, col_last, chosen, edge_first, edge_last, sems):
    low = lanes((N, 2 * HALO)) < HALO
    moves = [
        (obj.at[:, :, :, 0 : 2 * HALO], edge_first),
        (obj.at[:, :, :, N - 2 * HALO : N], edge_last),
        (obj.at[:, :, 0:HALO, :], row_first),
        (obj.at[:, :, N - HALO : N, :], row_last),
        (probe.at[core[0]], chosen),
    ]
    copies = [pltpu.make_async_copy(src, dst, sems.at[k]) for k, (src, dst) in enumerate(moves)]
    for copy in copies:
        copy.start()
    copies[0].wait()
    for s in range(2):
        col_first[s] = jnp.where(low, edge_first[s, 0], pltpu.roll(edge_first[s, 1], HALO, 1))
    copies[1].wait()
    for s in range(2):
        col_last[s] = jnp.where(low, pltpu.roll(edge_last[s, 0], HALO, 1), edge_last[s, 1])
    for copy in copies[2:]:
        copy.wait()


def own_kernel(offsets, obj, top, bottom, left_in, right_in, corner_left, corner_right, probe, kernel,
               gram, fwd_t, inv_t, left_t, window, psi1, far, intensity, ext, xb, ks, zs):
    tables = (fwd_t, inv_t, left_t)
    low = lanes((HALO, 2 * HALO)) < HALO

    def border(right_block, left_block, part):
        if part == 0:
            return jnp.where(low, right_block, pltpu.roll(left_block, HALO, 1))
        return jnp.where(low, pltpu.roll(right_block, HALO, 1), left_block)

    row_base, row_rest = aligned(offsets[0, 0])
    shift = lax.rem(HALO + FRAME - offsets[0, 1], FRAME)
    for s in range(2):
        for part in range(2):
            q = 2 * s + part
            ext[q, 0:HALO, 0:N] = top[s, part]
            ext[q, HALO : HALO + N, 0:N] = obj[s, part]
            ext[q, HALO + N : FRAME, 0:N] = bottom[s, part]
            ext[q, 0:HALO, N:FRAME] = border(
                corner_right[s, HALO : 2 * HALO], corner_left[s, HALO : 2 * HALO], part)
            ext[q, HALO + N : FRAME, N:FRAME] = border(
                corner_right[s, 0:HALO], corner_left[s, 0:HALO], part)
            for rows in chunks(N, HALO):
                ext[q, HALO + rows.start : HALO + rows.stop, N:FRAME] = border(
                    right_in[s, rows], left_in[s, rows], part)
            for rows in chunks(N, 64):
                block = ext[q, pl.ds(row_base + rows.start, 72), :]
                block = pltpu.roll(block, lax.rem(72 - row_rest, 72), 0)[:64]
                window[s, rows, part * N : (part + 1) * N] = pltpu.roll(block, shift, 1)[:, :N]
    interleave(forward_mode(m, probe.at[m], window, kernel, tables, psi1, far, xb, ks, zs) for m in range(2))
    add_intensity(far, intensity)


def near_kernel(probe, kernel, fwd_t, inv_t, left_t, window, psi1, far, intensity, xb, ks, zs):
    interleave([forward_mode(0, probe, window, kernel, (fwd_t, inv_t, left_t), psi1, far, xb, ks, zs)])
    for rows in chunks():
        re, im = halves(far, 0, rows)
        intensity[rows, :] = re * re + im * im


def other_kernel(offsets, obj, probe, near, swapped, kernel, fwd_t, inv_t, left_t, patterns, window,
                 psi1_own, far_own, intensity, psi1_near, far_near, intensity_near, gradient, row_top, row_bottom,
                 col_left, col_right, corner_left, corner_right, psi1, far, inten, xb, ks, zs, back, frame):
    tables = (fwd_t, inv_t, left_t)
    interleave([forward_mode(0, swapped, window, kernel, tables, psi1, far, xb, ks, zs)])
    for rows in chunks():
        re, im = halves(far, 0, rows)
        inten[rows, :] = intensity[rows, :] + (intensity_near[rows, :] + (re * re + im * im))
    for rows in chunks():
        inten[rows, :] = (inten[rows, :] * (1.0 / MODES) - patterns[0, rows, :]) * (2.0 / MODES)
    row_base, row_rest = aligned(offsets[0, 0])
    shift = lax.rem(HALO + N + offsets[0, 1], FRAME)
    modes = [
        (probe.at[0], psi1_own.at[0], far_own.at[0]),
        (probe.at[1], psi1_own.at[1], far_own.at[1]),
        (near, psi1_near.at[0], far_near.at[0]),
        (swapped, psi1.at[0], far.at[0]),
    ]
    interleave(
        backward_mode(k, psi0, psi, wave, inten, window, kernel, tables, back, xb, ks, zs)
        for k, (psi0, psi, wave) in enumerate(modes))
    low = lanes((HALO, 2 * HALO)) < HALO
    zero = jnp.zeros((HALO, 2 * HALO), F32)
    gap = jnp.zeros((8, FRAME), F32)
    frame[...] = jnp.zeros(frame.shape, F32)
    for q in range(4):
        s, part = divmod(q, 2)
        for rows in chunks(N, 64):
            columns = slice(part * N, (part + 1) * N)
            block = back[0, s, rows, columns] + back[1, s, rows, columns]
            block = pltpu.roll(jnp.concatenate([block, zero], 1), shift, 1)
            block = pltpu.roll(jnp.concatenate([block, gap], 0), row_rest, 0)
            frame[q, pl.ds(row_base + rows.start, 72), :] += block
    for s in range(2):
        for part in range(2):
            q = 2 * s + part
            gradient[s, part] = frame[q, HALO : HALO + N, 0:N] + REG_WEIGHT * obj[s, part]
            row_top[s, part] = frame[q, 0:HALO, 0:N]
            row_bottom[s, part] = frame[q, HALO + N : FRAME, 0:N]

        def strips(rows):
            re, im = frame[2 * s, rows, N:FRAME], frame[2 * s + 1, rows, N:FRAME]
            right = jnp.where(low, re, pltpu.roll(im, HALO, 1))
            left = jnp.where(low, pltpu.roll(re, HALO, 1), im)
            return right, left

        for rows in chunks(N, HALO):
            right, left = strips(slice(HALO + rows.start, HALO + rows.stop))
            col_right[s, rows] = right
            col_left[s, rows] = left
        right, left = strips(slice(HALO + N, FRAME))
        corner_right[s, 0:HALO] = right
        corner_left[s, 0:HALO] = left
        right, left = strips(slice(0, HALO))
        corner_right[s, HALO : 2 * HALO] = right
        corner_left[s, HALO : 2 * HALO] = left


def put_rows(out, first_row, sums):
    for k, value in enumerate(sums):
        out[first_row + k : first_row + k + 1, :] = jnp.sum(value, axis=0, keepdims=True)


def fold(value):
    rows = value.shape[0]
    value = value[:, : N // 2] + value[:, N // 2 :]
    return sum(value[r : r + 8] for r in range(0, rows, 8))


def accumulate(terms, count, out):
    def body(k, carry):
        rows = pl.ds((k % (N // 16)) * 16, 16)
        q = k // (N // 16)
        return tuple(a + fold(b) for a, b in zip(carry, terms(q // 2, q % 2, rows)))

    zero = tuple(jnp.zeros((8, N // 2), F32) for _ in range(count))
    put_rows(out, 0, lax.fori_loop(0, 4 * (N // 16), body, zero))


def sy_kernel(steps, changes, after, out):
    def terms(s, part, rows):
        st = [steps[i, s, part, rows, :].astype(F32) for i in range(MEM)]
        ch = [changes[i, s, part, rows, :].astype(F32) for i in range(MEM)]
        return [st[i] * ch[j] for i, j in SY_PAIRS]

    accumulate(terms, len(SY_PAIRS), out)


def yy_kernel(changes, after, out):
    def terms(s, part, rows):
        ch = [changes[i, s, part, rows, :].astype(F32) for i in range(MEM)]
        return [ch[i] * ch[j] for i, j in SY_PAIRS]

    accumulate(terms, len(SY_PAIRS), out)


def dots_kernel(gradient_in, row_up, row_down, col_left, col_right, steps, changes,
                gram_sy, gram_yy, gradient, out, stored, sums, sem):
    low = lanes((64, 2 * HALO)) < HALO
    for s in range(2):
        for part in range(2):
            for rows in chunks(N, 64):
                now = gradient_in[s, part, rows, :]
                if rows.start == 0:
                    now = now + row_up[s, part]
                if rows.stop == N:
                    now = now + row_down[s, part]
                a, b = col_left[s, rows], col_right[s, rows]
                if part == 0:
                    b = pltpu.roll(b, HALO, 1)
                else:
                    a = pltpu.roll(a, HALO, 1)
                gradient[s, part, rows, 0 : 2 * HALO] = now[:, : 2 * HALO] + jnp.where(low, a, 0.0)
                gradient[s, part, rows, N - 2 * HALO : N] = now[:, N - 2 * HALO :] + jnp.where(low, 0.0, b)
    copy = pltpu.make_async_copy(gradient, stored, sem)
    copy.start()

    def body(k, carry):
        q = k // (N // 64)
        rows = pl.ds((k % (N // 64)) * 64, 64)
        s, part = q // 2, q % 2
        g = gradient[s, part, rows, :]
        new = [fold(steps[i, s, part, rows, :].astype(F32) * g) for i in range(MEM)]
        new += [fold(changes[i, s, part, rows, :].astype(F32) * g) for i in range(MEM)]
        return tuple(a + b for a, b in zip(carry, new))

    zero = tuple(jnp.zeros((8, N // 2), F32) for _ in range(2 * MEM))
    sums[...] = jnp.zeros(sums.shape, F32)
    sums[0 : len(SY_PAIRS), :] = gram_sy[0 : len(SY_PAIRS), :]
    sums[len(SY_PAIRS) : SG_ROW, :] = gram_yy[0 : len(SY_PAIRS), :]
    put_rows(sums, SG_ROW, lax.fori_loop(0, 4 * (N // 64), body, zero))
    totals = jnp.sum(sums[...], axis=1, keepdims=True)
    row = lax.broadcasted_iota(jnp.int32, (128, 128), 0)
    spread = jnp.where(row == lanes((128, 128)), totals, 0.0)
    total_row = jnp.sum(spread, axis=0, keepdims=True)
    out[...] = jnp.broadcast_to(total_row[None], (128, 1, 128))
    copy.wait()


def final_kernel(parts, obj, gradient, steps, changes, out, result, sems):
    total = jnp.sum(parts[:, 0, :], axis=0, keepdims=True)
    row = lax.broadcasted_iota(jnp.int32, (128, 128), 0)
    diagonal = jnp.where(row == lanes((128, 128)), total, 0.0)
    splats = jnp.broadcast_to(jnp.sum(diagonal, axis=1, keepdims=True), (128, 128))

    def value(k):
        return splats[k : k + 1, :]

    sy = {pair: value(k) for pair, k in SY_ROW.items()}
    yy = {pair: value(k) for pair, k in YY_ROW.items()}
    inverse = [1.0 / sy[i, i] for i in range(MEM)]
    scaling = sy[MEM - 1, MEM - 1] / yy[MEM - 1, MEM - 1]
    alpha = [None] * MEM
    for i in reversed(range(MEM)):
        term = value(SG_ROW + i)
        for j in reversed(range(i + 1, MEM)):
            term = term - alpha[j] * sy[i, j]
        alpha[i] = term * inverse[i]
    weights = []
    for i in range(MEM):
        term = value(YG_ROW + i)
        for j in reversed(range(MEM)):
            term = term - alpha[j] * yy[min(i, j), max(i, j)]
        term = scaling * term
        for j in range(i):
            term = term + weights[j] * sy[j, i]
        weights.append(alpha[i] - term * inverse[i])

    def wide(x):
        return jnp.broadcast_to(jnp.concatenate([x, x], 1), (CHUNK, N))

    scale = wide(scaling)
    step_weights = [wide(w) for w in weights]
    change_weights = [wide(scaling * a) for a in alpha]
    copies = []
    for s in range(2):
        for part in range(2):

            def body(k, carry):
                rows = pl.ds(k * CHUNK, CHUNK)
                acc = scale * gradient[s, part, rows, :]
                for j in range(MEM):
                    acc = acc - change_weights[j] * changes[j, s, part, rows, :].astype(F32)
                    acc = acc + step_weights[j] * steps[j, s, part, rows, :].astype(F32)
                result[s, part, rows, :] = obj[s, part, rows, :] - acc
                return carry

            lax.fori_loop(0, N // CHUNK, body, 0)
            copies.append(pltpu.make_async_copy(result.at[s, part], out.at[s, part], sems.at[2 * s + part]))
            copies[-1].start()
    for copy in copies:
        copy.wait()


def shape(*dims, dtype=F32):
    return jax.ShapeDtypeStruct(dims, dtype)


def scratch(*dims, dtype=F32):
    return pltpu.VMEM(dims, dtype)


def call(kernel, outs, scratches, args, smem=0, raw=0, stored=()):
    return pl.pallas_call(
        kernel,
        out_shape=outs,
        in_specs=[SMEM] * smem + [ANY] * raw + [VMEM] * (len(args) - smem - raw),
        out_specs=tuple(ANY if k in stored else VMEM for k in range(len(outs))),
        scratch_shapes=scratches,
        compiler_params=PARAMS,
    )(*args)


def shifted(value, axis, step):
    size = lax.axis_size(axis)
    return lax.ppermute(value, axis, [(i, (i + step) % size) for i in range(size)])


def packed(value, columns):
    return jnp.concatenate([value[:, 0, :, columns], value[:, 1, :, columns]], -1)


def near_pairs(rows, modes):
    half = rows // modes
    pairs = []
    for t in range(rows):
        for m in range(modes):
            y = m * modes + t // half
            other = 2 * modes - 1 - y
            target = (other % modes) * half + t % half
            pairs.append((t * modes + m, target * modes + other // modes))
    return pairs


def per_device(object_field, probe, patterns, offsets, phase, past_steps, past_changes):
    rows_axis, modes_axis = lax.axis_size("ty"), lax.axis_size("mode")
    core = (lax.axis_index("ty") & 1).astype(jnp.int32).reshape(1)
    tables = dft_tables()
    first, last = slice(0, HALO), slice(N - HALO, N)
    strip, side, corner = shape(2, 2, HALO, N), shape(2, N, 2 * HALO), shape(2, 2 * HALO, 2 * HALO)
    row_first, row_last, col_first, col_last, chosen = call(
        pack_kernel, (strip, strip, side, side, shape(N, 2 * N)),
        [scratch(2, 2, N, 2 * HALO), scratch(2, 2, N, 2 * HALO), pltpu.SemaphoreType.DMA((5,))],
        (core, pltpu.with_memory_space_constraint(object_field, pltpu.HBM),
         pltpu.with_memory_space_constraint(probe, pltpu.HBM)), smem=1, raw=2)
    top = shifted(row_last, "ty", 1)
    bottom = shifted(row_first, "ty", -1)
    left = shifted(col_last, "tx", 1)
    right = shifted(col_first, "tx", -1)
    near = lax.ppermute(chosen, ("ty", "mode"), near_pairs(rows_axis, modes_axis))
    strips, phase = lax.optimization_barrier((jnp.concatenate([bottom, top], 2), phase))
    corner_last, corner_first = packed(strips, last), packed(strips, first)
    corner_left = shifted(corner_last, "tx", 1)
    corner_right = shifted(corner_first, "tx", -1)
    kernel = jnp.stack([jnp.cos(phase), jnp.sin(phase)])
    gram_sy = call(sy_kernel, (shape(16, 128),), [], (past_steps, past_changes, corner_first))[0]

    def work(slots):
        return [scratch(slots, N, 2 * N, dtype=BF16), scratch(slots, 2 * N, 2 * N, dtype=BF16),
                scratch(slots, N, 2 * N)]

    window, psi1, far, intensity = call(
        own_kernel,
        (shape(2, N, 2 * N), shape(2, N, 2 * N), shape(2, N, 2 * N), shape(N, N)),
        [scratch(4, FRAME + 8, FRAME)] + work(2),
        (offsets, object_field, top, bottom, left, right, corner_left, corner_right, probe, kernel,
         gram_sy) + tables,
        smem=1,
    )
    near, intensity = lax.optimization_barrier((near, intensity))
    swapped = lax.ppermute(near, "ty", [(i, i ^ 1) for i in range(rows_axis)])
    psi1_near, far_near, intensity_near = call(
        near_kernel, (shape(1, N, 2 * N), shape(1, N, 2 * N), shape(N, N)), work(1),
        (near, kernel) + tables + (window,))
    partial, row_top, row_bottom, col_left, col_right, corner_left, corner_right = call(
        other_kernel,
        (shape(2, 2, N, N), strip, strip, side, side, corner, corner),
        [scratch(1, N, 2 * N), scratch(1, N, 2 * N), scratch(N, N)] + work(4)
        + [scratch(2, 2, N, 2 * N), scratch(4, FRAME + 8, FRAME)],
        (offsets, object_field, probe, near, swapped, kernel) + tables
        + (patterns, window, psi1, far, intensity, psi1_near, far_near, intensity_near),
        smem=1,
    )
    from_left = shifted(corner_right, "tx", 1)
    from_right = shifted(corner_left, "tx", -1)
    side_left = shifted(col_right, "tx", 1)
    side_right = shifted(col_left, "tx", -1)


    def with_corners(strip_now, rows):
        def unpacked(block):
            return jnp.stack([block[:, rows, :HALO], block[:, rows, HALO:]], 1)

        gap = jnp.zeros(strip_now.shape[:3] + (N - 2 * HALO,), F32)
        return strip_now + jnp.concatenate([unpacked(from_left), gap, unpacked(from_right)], -1)

    below, above = with_corners(row_bottom, slice(0, HALO)), with_corners(row_top, slice(HALO, 2 * HALO))
    row_up = shifted(below, "ty", 1)
    row_down = shifted(above, "ty", -1)
    gram_yy = call(yy_kernel, (shape(16, 128),), [], (past_changes, above))[0]
    gradient, sums, stored = call(
        dots_kernel,
        (shape(2, 2, N, N), shape(128, 1, 128), shape(2, 2, N, N)),
        [scratch(128, 128), pltpu.SemaphoreType.DMA],
        (partial, row_up, row_down, side_left, side_right, past_steps, past_changes,
         gram_sy, gram_yy),
        stored=(2,),
    )
    parts = lax.all_to_all(sums, TILES, 0, 0)
    new_object = call(
        final_kernel, (shape(2, 2, N, N),), [scratch(2, 2, N, N), pltpu.SemaphoreType.DMA((4,))],
        (parts, object_field, gradient, past_steps, past_changes), stored=(0,))[0]
    return (new_object, stored)


def solution(mesh):
    placed = (
        P(None, None, "ty", "tx"),
        P("mode", None, None),
        P(TILES, None, None),
        P(TILES, None),
        P(),
        P(None, None, None, "ty", "tx"),
        P(None, None, None, "ty", "tx"),
    )
    return jax.shard_map(
        per_device,
        mesh=mesh,
        in_specs=placed,
        out_specs=(P(None, None, "ty", "tx"), P(None, None, "ty", "tx")),
        check_vma=False,
    )
```

time: 88.7 us -> 78.1 us (0.88)
  local copies, waits for them, and re-layouts: 5.16 us -> 1.49 us
  starting transfers between devices: 27.1 us -> 24.4 us
  waiting for transfers between devices: 7.2 us -> 5.52 us
  Pallas kernels: 25.2 us -> 24 us
  blocking collectives: 22.1 us -> 21 us
    ppermute x1, starting transfers between devices: 5.38 us -> 3.12 us  [per_device(): swapped = lax.ppermute(near, 'ty', [(i, i ^ 1) for i in range(rows_axis)])]
    ppermute x12, waiting for transfers between devices: 7.2 us -> 5.51 us  [shifted(): lax.ppermute(value, axis, [(i, (i + step) % size) for i in range(size)])]
    unnamed x25 -> x20, local copies, waits for them, and re-layouts: 1.34 us -> 0.06 us
    pallas_call x5 -> x8, Pallas kernels: 25.2 us -> 24 us  [call(): pl.pallas_call(kernel, out_shape=outs, in_specs=[SMEM] * smem + [ANY] * r...]
    squeeze x1 -> x0, local copies, waits for them, and re-layouts: 1.16 us -> none  [per_device(): chosen = lax.dynamic_slice_in_dim(probe, core, 1, 0)[0]]
    all_to_all x1, blocking collectives: 22.1 us -> 21 us  [per_device(): parts = lax.all_to_all(sums, TILES, 0, 0)]
    slice x1 -> x0, local copies, waits for them, and re-layouts: 1.06 us -> none  [per_device(): top = shifted(object_field[:, :, last, :], 'ty', 1)]
    ppermute x1, starting transfers between devices: 3.65 us -> 2.73 us  [per_device(): lax.ppermute(chosen, ('ty', 'mode'), near_pairs(rows_axis, modes_axis))]
  transfers between devices with their start and end apart: 14 -> 14, of which waited for: 5 -> 4; matrix products, arithmetic and copies ran while one was open for 4% -> 2% of each run, Pallas kernels for 9% -> 14%
where the time goes in v2:
time: 78.1 us; the launch traced here: 78 us
  starting transfers between devices  24.4 us (31%)
  Pallas kernels  24 us (31%)
  blocking collectives  21 us (27%)
  waiting for transfers between devices  5.52 us (7%)
  local copies, waits for them, and re-layouts  1.49 us (2%)
  between operations  1.17 us (1%)
    pallas_call x8, Pallas kernels, call(): pl.pallas_call(kernel, out_shape=outs, in_specs=[SMEM] * smem + [ANY] * r...  24 us
    all_to_all x1, blocking collectives, per_device(): parts = lax.all_to_all(sums, TILES, 0, 0)  21 us
    ppermute x12, starting transfers between devices, shifted(): lax.ppermute(value, axis, [(i, (i + step) % size) for i in range(size)])  18.5 us
    ppermute x12, waiting for transfers between devices, shifted(): lax.ppermute(value, axis, [(i, (i + step) % size) for i in range(size)])  5.51 us
    ppermute x1, starting transfers between devices, per_device(): swapped = lax.ppermute(near, 'ty', [(i, i ^ 1) for i in range(rows_axis)])  3.12 us
    ppermute x1, starting transfers between devices, per_device(): lax.ppermute(chosen, ('ty', 'mode'), near_pairs(rows_axis, modes_axis))  2.73 us
  transfers between devices with their start and end apart: 14, of which 4 were waited for; matrix products, arithmetic and copies ran while one was open for 2% of the time, Pallas kernels for 14%

profile of v2, /device:TPU:1, one launch (start us, length us, event | category | flops | bytes accessed | tf_op | source)
XLA Modules:
  0.0 78.0 jit_solution(14496414557205275825)
XLA Ops:
  0.7 1.7 %shard_map.113 = (f32[2,2,64,256]{3,2,1,0:T(8,128)S(1)}, f32[2,2,64,256]{3,2,1,0:T(8,128)S(1)}, f32[2,256,128]{2,1,0:T(8,128)S(1)}, f32[2,256,128]{2,1,0:T(8,128)S(1)}, f32[256,512]{1,0:T(8,128)S(1)}) custom-call(s32[1]{0:T(128)} %bitcast.core, f32[2,2,256,256]{3,2,1,0:T(8,128)} %obj.7, f32[2,256,512]{2,1,0:T(8,128)} %probe.5), custom_call_target="tpu_custom_call" | custom-call | tf_op jit(solution)/shard_map/pallas_call | solution.py:441
  2.4 2.7 %collective-permute-start.1 = (f32[2,2,64,256]{3,2,0,1:T(8,128)S(1)}, f32[2,2,64,256]{3,2,0,1:T(8,128)S(1)}, u32[]{:S(2)}, u32[]{:S(2)}) collective-permute-start(f32[2,2,64,256]{3,2,0,1:T(8,128)S(1)} %copy.12), channel_id=1, source_target_pairs={{0,16},{16,32},{32,48},{48,64},{64,80},{80,96},{96,112},{112,128},... | collective-permute-start | bytes 786440 | tf_op jit(solution)/shard_map/ppermute | solution.py:453
  5.1 0.7 collective-permute-start.2
  5.8 1.1 %collective-permute-start.3 = (f32[2,256,128]{2,1,0:T(8,128)S(1)}, f32[2,256,128]{2,1,0:T(8,128)S(1)}, u32[]{:S(2)}, u32[]{:S(2)}) collective-permute-start(f32[2,256,128]{2,1,0:T(8,128)S(1)} %get-tuple-element.31), channel_id=1, source_target_pairs={{0,2},{2,4},{4,6},{6,8},{8,10},{10,12},{12,14},{14,0},{1,3},{3,5},... | collective-permute-start | bytes 786440 | tf_op jit(solution)/shard_map/ppermute | solution.py:453
  6.9 4.0 %collective-permute-start.4 = (f32[2,256,128]{2,1,0:T(8,128)S(1)}, f32[2,256,128]{2,1,0:T(8,128)S(1)}, u32[]{:S(2)}, u32[]{:S(2)}) collective-permute-start(f32[2,256,128]{2,1,0:T(8,128)S(1)} %get-tuple-element.32), channel_id=1, source_target_pairs={{0,14},{2,0},{4,2},{6,4},{8,6},{10,8},{12,10},{14,12},{1,15},{3,1}... | collective-permute-start | bytes 786440 | tf_op jit(solution)/shard_map/ppermute | solution.py:453
  10.9 2.7 %collective-permute-start = (f32[256,512]{1,0:T(8,128)S(1)}, f32[256,512]{1,0:T(8,128)S(1)}, u32[]{:S(2)}, u32[]{:S(2)}) collective-permute-start(f32[256,512]{1,0:T(8,128)S(1)} %get-tuple-element.28), channel_id=1, source_target_pairs={{0,129},{1,128},{16,145},{17,144},{32,161},{33,160},{48,177},{49,1... | collective-permute-start | bytes 1572872 | tf_op jit(solution)/shard_map/ppermute | solution.py:487
  13.7 0.1 slice_bitcast_fusion.1
  13.9 0.1 pad_maximum_fusion.3.after
  14.0 3.2 %collective-permute-start.6 = (f32[2,128,128]{2,1,0:T(8,128)S(1)}, f32[2,128,128]{2,1,0:T(8,128)S(1)}, u32[]{:S(2)}, u32[]{:S(2)}) collective-permute-start(f32[2,128,128]{2,1,0:T(8,128)S(1)} %pad_maximum_fusion.3.after), channel_id=1, source_target_pairs={{0,14},{2,0},{4,2},{6,4},{8,6},{10,8},{12,10},{14,12},{1,15},{3,1}... | collective-permute-start | bytes 393224 | tf_op jit(solution)/shard_map/ppermute | solution.py:453
  17.2 0.1 pad_maximum_fusion.2
  17.3 0.1 collective-permute-start.5
  17.4 1.0 %cosine_bitcast_fusion = (f32[1,256,256]{2,1,0:T(8,128)S(1)}, f32[1,256,256]{2,1,0:T(8,128)S(1)}) fusion(f32[256,256]{1,0:T(8,128)S(1)} %copy-done.9), kind=kLoop, calls=%fused_computation.5 | loop fusion | bytes 786432 | tf_op jit(solution)/shard_map/stack | solution.py:492
  18.5 2.8 %shard_map.114.gram.gram_sy = f32[16,128]{1,0:T(8,128)S(1)} custom-call(bf16[5,2,2,256,256]{4,3,2,1,0:T(8,128)(2,1)S(1)} %copy-done.1, bf16[5,2,2,256,256]{4,3,2,1,0:T(8,128)(2,1)S(1)} %copy-done, f32[2,128,128]{2,1,0:T(8,128)S(1)} %pad_maximum_fusion.3.after), custom_call_target="tpu_custom_call" | custom-call | tf_op jit(solution)/shard_map/pallas_call | solution.py:441
  21.4 1.3 %collective-permute-done.5.corner_left = f32[2,128,128]{2,1,0:T(8,128)S(1)} collective-permute-done((f32[2,128,128]{2,1,0:T(8,128)S(1)}, f32[2,128,128]{2,1,0:T(8,128)S(1)}, u32[]{:S(2)}, u32[]{:S(2)}) %collective-permute-start.5) | collective-permute-done | bytes 131104 | tf_op jit(solution)/shard_map/ppermute | solution.py:453
  22.8 3.9 %shard_map.115 = (f32[2,256,512]{2,1,0:T(8,128)S(1)}, f32[2,256,512]{2,1,0:T(8,128)S(1)}, f32[2,256,512]{2,1,0:T(8,128)S(1)}, f32[256,256]{1,0:T(8,128)S(1)}) custom-call(s32[1,2]{1,0:T(1,128)S(1)} %copy-done.8, f32[2,2,256,256]{3,2,1,0:T(8,128)S(1)} %copy-done.2, f32[2,2,64,256]{3,2,1,0:T(8,128)S(1)} %copy.14.top, f32[2,2,64,256]{3,2,1,0:T(8,128)S(1)} %copy.15.bottom, ...), custom_call_target="tpu_custom_call" | custom-call | tf_op jit(solution)/shard_map/pallas_call | solution.py:441
  26.7 3.1 %collective-permute-start.7 = (f32[256,512]{1,0:T(8,128)S(1)}, f32[256,512]{1,0:T(8,128)S(1)}, u32[]{:S(2)}, u32[]{:S(2)}) collective-permute-start(f32[256,512]{1,0:T(8,128)S(1)} %collective-permute-done.probe.near), channel_id=1, source_target_pairs={{0,16},{16,0},{32,48},{48,32},{64,80},{80,64},{96,112},{112,96},{1... | collective-permute-start | bytes 1572872 | tf_op jit(solution)/shard_map/ppermute | solution.py:508
  29.8 1.6 %shard_map.116 = (f32[1,256,512]{2,1,0:T(8,128)S(1)}, f32[1,256,512]{2,1,0:T(8,128)S(1)}, f32[256,256]{1,0:T(8,128)S(1)}) custom-call(f32[256,512]{1,0:T(8,128)S(1)} %collective-permute-done.probe.near, f32[2,256,256]{2,1,0:T(8,128)S(1)} %pad_maximum_fusion.1.kernel, bf16[512,512]{1,0:T(8,128)(2,1)S(1)} %copy-done.4, bf16[512,512]{1,0:T(8,128)(2,1)S(1)} %copy-done.5, ...), custom_call_target="tpu_custom_call" | custom-call | tf_op jit(solution)/shard_map/pallas_call | solution.py:441
  31.4 7.5 %shard_map.117 = (f32[2,2,256,256]{3,2,1,0:T(8,128)S(1)}, f32[2,2,64,256]{3,2,1,0:T(8,128)S(1)}, f32[2,2,64,256]{3,2,1,0:T(8,128)S(1)}, f32[2,256,128]{2,1,0:T(8...) custom-call(s32[1,2]{1,0:T(1,128)S(1)} %copy-done.8, ...), custom_call_target="tpu_custom_call" | custom-call | tf_op jit(solution)/shard_map/pallas_call | solution.py:441
  38.9 0.1 collective-permute-start.8
  39.1 2.7 %collective-permute-start.9 = (f32[2,128,128]{2,1,0:T(8,128)S(1)}, f32[2,128,128]{2,1,0:T(8,128)S(1)}, u32[]{:S(2)}, u32[]{:S(2)}) collective-permute-start(f32[2,128,128]{2,1,0:T(8,128)S(1)} %get-tuple-element.47), channel_id=1, source_target_pairs={{0,14},{2,0},{4,2},{6,4},{8,6},{10,8},{12,10},{14,12},{1,15},{3,1}... | collective-permute-start | bytes 393224 | tf_op jit(solution)/shard_map/ppermute | solution.py:453
  41.8 2.7 %collective-permute-start.13 = (f32[2,256,128]{2,1,0:T(8,128)S(1)}, f32[2,256,128]{2,1,0:T(8,128)S(1)}, u32[]{:S(2)}, u32[]{:S(2)}) collective-permute-start(f32[2,256,128]{2,1,0:T(8,128)S(1)} %get-tuple-element.50), channel_id=1, source_target_pairs={{0,14},{2,0},{4,2},{6,4},{8,6},{10,8},{12,10},{14,12},{1,15},{3,1}... | collective-permute-start | bytes 786440 | tf_op jit(solution)/shard_map/ppermute | solution.py:453
  44.5 0.6 collective-permute-done.8
  45.0 0.1 slice_bitcast_fusion.7
  45.2 0.1 slice_bitcast_fusion.5
  45.3 0.1 maximum_add_fusion.1
  45.4 1.2 %collective-permute-start.10 = (f32[2,2,64,256]{3,2,1,0:T(8,128)S(1)}, f32[2,2,64,256]{3,2,1,0:T(8,128)S(1)}, u32[]{:S(2)}, u32[]{:S(2)}) collective-permute-start(f32[2,2,64,256]{3,2,1,0:T(8,128)S(1)} %get-tuple-element.69), channel_id=1, source_target_pairs={{0,16},{16,32},{32,48},{48,64},{64,80},{80,96},{96,112},{112,128},... | collective-permute-start | bytes 786440 | tf_op jit(solution)/shard_map/ppermute | solution.py:453
  46.7 2.4 %shard_map.118.gram_yy = f32[16,128]{1,0:T(8,128)S(1)} custom-call(bf16[5,2,2,256,256]{4,3,2,1,0:T(8,128)(2,1)S(1)} %copy-done, f32[2,2,64,256]{3,2,1,0:T(8,128)S(1)} %get-tuple-element.68.after), custom_call_target="tpu_custom_call" | custom-call | tf_op jit(solution)/shard_map/pallas_call | solution.py:441
  49.1 1.0 %collective-permute-done.12.col_left = f32[2,256,128]{2,1,0:T(8,128)S(1)} collective-permute-done((f32[2,256,128]{2,1,0:T(8,128)S(1)}, f32[2,256,128]{2,1,0:T(8,128)S(1)}, u32[]{:S(2)}, u32[]{:S(2)}) %collective-permute-start.12) | collective-permute-done | bytes 262176 | tf_op jit(solution)/shard_map/ppermute | solution.py:453
  50.1 2.7 %collective-permute-done.11.row_down = f32[2,2,64,256]{3,2,1,0:T(8,128)S(1)} collective-permute-done((f32[2,2,64,256]{3,2,1,0:T(8,128)S(1)}, f32[2,2,64,256]{3,2,1,0:T(8,128)S(1)}, u32[]{:S(2)}, u32[]{:S(2)}) %collective-permute-start.11) | collective-permute-done | bytes 262176 | tf_op jit(solution)/shard_map/ppermute | solution.py:453
  52.7 1.8 %shard_map.119 = (f32[2,2,256,256]{3,2,1,0:T(8,128)S(1)}, f32[128,1,128]{2,1,0:T(1,128)S(1)}, f32[2,2,256,256]{3,2,1,0:T(8,128)}) custom-call(f32[2,2,256,256]{3,2,1,0:T(8,128)S(1)} %get-tuple-element.44.gradient_in, f32[2,2,64,256]{3,2,1,0:T(8,128)S(1)} %collective-permute-done.10.row_up, f32[2,2,64,256]{3,2,1,0:T(8,128)S(1)} %collective-permute-done.11.row_down, ...), custom_call_target="tpu_custom_call" | custom-call | tf_op jit(solution)/shard_map/pallas_call | solution.py:441
  54.5 21.0 %all_to_all.5.parts = f32[128,1,128]{2,1,0:T(1,128)S(1)} all-to-all(f32[128,1,128]{2,1,0:T(1,128)S(1)} %get-tuple-element.51), channel_id=1, replica_groups=mesh['ty'=16,'tx'=8,'mode'=2] {'ty','tx'}, dimensions={0} | all-to-all | bytes 131072 | tf_op jit(solution)/shard_map/all_to_all | solution.py:546
  75.5 2.3 %shard_map.120 = f32[2,2,256,256]{3,2,1,0:T(8,128)} custom-call(f32[128,1,128]{2,1,0:T(1,128)S(1)} %all_to_all.5.parts, f32[2,2,256,256]{3,2,1,0:T(8,128)S(1)} %copy-done.2, f32[2,2,256,256]{3,2,1,0:T(8,128)S(1)} %get-tuple-element.52.gradient, bf16[5,2,2,256,256]{4,3,2,1,0:T(8,128)(2,1)S(1)} %copy-done.1, bf16[5,2,2,256,256]{4,3,2,1,0:T(8,128)(2,1)S(1)} %copy-done), custom_call_target="tpu_custom_call" | custom-call | tf_op jit(solution)/shard_map/pallas_call | solution.py:441
  (41 shorter events, 0.4 us)
Async XLA Ops:
  0.6 16.8 %copy-start.9 = (f32[256,256]{1,0:T(8,128)S(1)}, f32[256,256]{1,0:T(8,128)}, u32[]{:S(2)}) copy-start(f32[256,256]{1,0:T(8,128)} %param.14) | copy-start | bytes 786436
  0.6 17.8 %copy-start.1 = (bf16[5,2,2,256,256]{4,3,2,1,0:T(8,128)(2,1)S(1)}, bf16[5,2,2,256,256]{4,3,2,1,0:T(8,128)(2,1)}, u32[]{:S(2)}) copy-start(bf16[5,2,2,256,256]{4,3,2,1,0:T(8,128)(2,1)} %steps.5) | copy-start | bytes 7864324
  2.4 16.0 %copy-start = (bf16[5,2,2,256,256]{4,3,2,1,0:T(8,128)(2,1)S(1)}, bf16[5,2,2,256,256]{4,3,2,1,0:T(8,128)(2,1)}, u32[]{:S(2)}) copy-start(bf16[5,2,2,256,256]{4,3,2,1,0:T(8,128)(2,1)} %changes.7) | copy-start | bytes 7864324
  2.4 11.3 %collective-permute-start.1 = (f32[2,2,64,256]{3,2,0,1:T(8,128)S(1)}, f32[2,2,64,256]{3,2,0,1:T(8,128)S(1)}, u32[]{:S(2)}, u32[]{:S(2)}) collective-permute-start(f32[2,2,64,256]{3,2,0,1:T(8,128)S(1)} %copy.12), channel_id=1, source_target_pairs={{0,16},{16,32},{32,48},{48,64},{64,80},{80,96},{96,112},{112,128},... | collective-permute-start | bytes 786440 | tf_op jit(solution)/shard_map/ppermute | solution.py:453
  5.1 8.6 %collective-permute-start.2 = (f32[2,2,64,256]{3,2,0,1:T(8,128)S(1)}, f32[2,2,64,256]{3,2,0,1:T(8,128)S(1)}, u32[]{:S(2)}, u32[]{:S(2)}) collective-permute-start(f32[2,2,64,256]{3,2,0,1:T(8,128)S(1)} %copy.13), channel_id=1, source_target_pairs={{0,240},{16,0},{32,16},{48,32},{64,48},{80,64},{96,80},{112,96},{1... | collective-permute-start | bytes 786440 | tf_op jit(solution)/shard_map/ppermute | solution.py:453
  5.8 15.6 %collective-permute-start.3 = (f32[2,256,128]{2,1,0:T(8,128)S(1)}, f32[2,256,128]{2,1,0:T(8,128)S(1)}, u32[]{:S(2)}, u32[]{:S(2)}) collective-permute-start(f32[2,256,128]{2,1,0:T(8,128)S(1)} %get-tuple-element.31), channel_id=1, source_target_pairs={{0,2},{2,4},{4,6},{6,8},{8,10},{10,12},{12,14},{14,0},{1,3},{3,5},... | collective-permute-start | bytes 786440 | tf_op jit(solution)/shard_map/ppermute | solution.py:453
  6.9 14.5 %collective-permute-start.4 = (f32[2,256,128]{2,1,0:T(8,128)S(1)}, f32[2,256,128]{2,1,0:T(8,128)S(1)}, u32[]{:S(2)}, u32[]{:S(2)}) collective-permute-start(f32[2,256,128]{2,1,0:T(8,128)S(1)} %get-tuple-element.32), channel_id=1, source_target_pairs={{0,14},{2,0},{4,2},{6,4},{8,6},{10,8},{12,10},{14,12},{1,15},{3,1}... | collective-permute-start | bytes 786440 | tf_op jit(solution)/shard_map/ppermute | solution.py:453
  10.9 15.7 %collective-permute-start = (f32[256,512]{1,0:T(8,128)S(1)}, f32[256,512]{1,0:T(8,128)S(1)}, u32[]{:S(2)}, u32[]{:S(2)}) collective-permute-start(f32[256,512]{1,0:T(8,128)S(1)} %get-tuple-element.28), channel_id=1, source_target_pairs={{0,129},{1,128},{16,145},{17,144},{32,161},{33,160},{48,177},{49,1... | collective-permute-start | bytes 1572872 | tf_op jit(solution)/shard_map/ppermute | solution.py:487
  14.0 7.5 %collective-permute-start.6 = (f32[2,128,128]{2,1,0:T(8,128)S(1)}, f32[2,128,128]{2,1,0:T(8,128)S(1)}, u32[]{:S(2)}, u32[]{:S(2)}) collective-permute-start(f32[2,128,128]{2,1,0:T(8,128)S(1)} %pad_maximum_fusion.3.after), channel_id=1, source_target_pairs={{0,14},{2,0},{4,2},{6,4},{8,6},{10,8},{12,10},{14,12},{1,15},{3,1}... | collective-permute-start | bytes 393224 | tf_op jit(solution)/shard_map/ppermute | solution.py:453
  17.3 5.4 %collective-permute-start.5 = (f32[2,128,128]{2,1,0:T(8,128)S(1)}, f32[2,128,128]{2,1,0:T(8,128)S(1)}, u32[]{:S(2)}, u32[]{:S(2)}) collective-permute-start(f32[2,128,128]{2,1,0:T(8,128)S(1)} %pad_maximum_fusion.2), channel_id=1, source_target_pairs={{0,2},{2,4},{4,6},{6,8},{8,10},{10,12},{12,14},{14,0},{1,3},{3,5},... | collective-permute-start | bytes 393224 | tf_op jit(solution)/shard_map/ppermute | solution.py:453
  18.4 4.3 %copy-start.2 = (f32[2,2,256,256]{3,2,1,0:T(8,128)S(1)}, f32[2,2,256,256]{3,2,1,0:T(8,128)}, u32[]{:S(2)}) copy-start(f32[2,2,256,256]{3,2,1,0:T(8,128)} %obj.7) | copy-start | bytes 3145732
  18.4 4.3 %copy-start.3 = (f32[2,256,512]{2,1,0:T(8,128)S(1)}, f32[2,256,512]{2,1,0:T(8,128)}, u32[]{:S(2)}) copy-start(f32[2,256,512]{2,1,0:T(8,128)} %probe.5) | copy-start | bytes 3145732
  18.4 4.3 %copy-start.4 = (bf16[512,512]{1,0:T(8,128)(2,1)S(1)}, bf16[512,512]{1,0:T(8,128)(2,1)}, u32[]{:S(2)}) copy-start(bf16[512,512]{1,0:T(8,128)(2,1)} %constant.15.clone.fwd_t) | copy-start | bytes 1572868
  18.5 4.3 %copy-start.5 = (bf16[512,512]{1,0:T(8,128)(2,1)S(1)}, bf16[512,512]{1,0:T(8,128)(2,1)}, u32[]{:S(2)}) copy-start(bf16[512,512]{1,0:T(8,128)(2,1)} %constant.16.clone.inv_t) | copy-start | bytes 1572868
  18.5 4.3 %copy-start.6 = (bf16[256,512]{1,0:T(8,128)(2,1)S(1)}, bf16[256,512]{1,0:T(8,128)(2,1)}, u32[]{:S(2)}) copy-start(bf16[256,512]{1,0:T(8,128)(2,1)} %constant.17.clone.left_t) | copy-start | bytes 786436
  18.5 4.3 %copy-start.8 = (s32[1,2]{1,0:T(1,128)S(1)}, s32[1,2]{1,0:T(1,128)}, u32[]{:S(2)}) copy-start(s32[1,2]{1,0:T(1,128)} %offsets.3) | copy-start | bytes 28
  26.6 4.8 %copy-start.7 = (f32[1,256,256]{2,1,0:T(8,128)S(1)}, f32[1,256,256]{2,1,0:T(8,128)}, u32[]{:S(2)}) copy-start(f32[1,256,256]{2,1,0:T(8,128)} %patterns.1) | copy-start | bytes 786436
  26.7 4.7 %collective-permute-start.7 = (f32[256,512]{1,0:T(8,128)S(1)}, f32[256,512]{1,0:T(8,128)S(1)}, u32[]{:S(2)}, u32[]{:S(2)}) collective-permute-start(f32[256,512]{1,0:T(8,128)S(1)} %collective-permute-done.probe.near), channel_id=1, source_target_pairs={{0,16},{16,0},{32,48},{48,32},{64,80},{80,64},{96,112},{112,96},{1... | collective-permute-start | bytes 1572872 | tf_op jit(solution)/shard_map/ppermute | solution.py:508
  38.9 6.1 %collective-permute-start.8 = (f32[2,128,128]{2,1,0:T(8,128)S(1)}, f32[2,128,128]{2,1,0:T(8,128)S(1)}, u32[]{:S(2)}, u32[]{:S(2)}) collective-permute-start(f32[2,128,128]{2,1,0:T(8,128)S(1)} %get-tuple-element.46), channel_id=1, source_target_pairs={{0,2},{2,4},{4,6},{6,8},{8,10},{10,12},{12,14},{14,0},{1,3},{3,5},... | collective-permute-start | bytes 393224 | tf_op jit(solution)/shard_map/ppermute | solution.py:453
  39.1 6.0 %collective-permute-start.9 = (f32[2,128,128]{2,1,0:T(8,128)S(1)}, f32[2,128,128]{2,1,0:T(8,128)S(1)}, u32[]{:S(2)}, u32[]{:S(2)}) collective-permute-start(f32[2,128,128]{2,1,0:T(8,128)S(1)} %get-tuple-element.47), channel_id=1, source_target_pairs={{0,14},{2,0},{4,2},{6,4},{8,6},{10,8},{12,10},{14,12},{1,15},{3,1}... | collective-permute-start | bytes 393224 | tf_op jit(solution)/shard_map/ppermute | solution.py:453
  41.8 8.3 %collective-permute-start.12 = (f32[2,256,128]{2,1,0:T(8,128)S(1)}, f32[2,256,128]{2,1,0:T(8,128)S(1)}, u32[]{:S(2)}, u32[]{:S(2)}) collective-permute-start(f32[2,256,128]{2,1,0:T(8,128)S(1)} %get-tuple-element.49), channel_id=1, source_target_pairs={{0,2},{2,4},{4,6},{6,8},{8,10},{10,12},{12,14},{14,0},{1,3},{3,5},... | collective-permute-start | bytes 786440 | tf_op jit(solution)/shard_map/ppermute | solution.py:453
  41.8 8.3 %collective-permute-start.13 = (f32[2,256,128]{2,1,0:T(8,128)S(1)}, f32[2,256,128]{2,1,0:T(8,128)S(1)}, u32[]{:S(2)}, u32[]{:S(2)}) collective-permute-start(f32[2,256,128]{2,1,0:T(8,128)S(1)} %get-tuple-element.50), channel_id=1, source_target_pairs={{0,14},{2,0},{4,2},{6,4},{8,6},{10,8},{12,10},{14,12},{1,15},{3,1}... | collective-permute-start | bytes 786440 | tf_op jit(solution)/shard_map/ppermute | solution.py:453
  45.4 4.6 %collective-permute-start.10 = (f32[2,2,64,256]{3,2,1,0:T(8,128)S(1)}, f32[2,2,64,256]{3,2,1,0:T(8,128)S(1)}, u32[]{:S(2)}, u32[]{:S(2)}) collective-permute-start(f32[2,2,64,256]{3,2,1,0:T(8,128)S(1)} %get-tuple-element.69), channel_id=1, source_target_pairs={{0,16},{16,32},{32,48},{48,64},{64,80},{80,96},{96,112},{112,128},... | collective-permute-start | bytes 786440 | tf_op jit(solution)/shard_map/ppermute | solution.py:453
  46.6 6.1 %collective-permute-start.11 = (f32[2,2,64,256]{3,2,1,0:T(8,128)S(1)}, f32[2,2,64,256]{3,2,1,0:T(8,128)S(1)}, u32[]{:S(2)}, u32[]{:S(2)}) collective-permute-start(f32[2,2,64,256]{3,2,1,0:T(8,128)S(1)} %get-tuple-element.68.after), channel_id=1, source_target_pairs={{0,240},{16,0},{32,16},{48,32},{64,48},{80,64},{96,80},{112,96},{1... | collective-permute-start | bytes 786440 | tf_op jit(solution)/shard_map/ppermute | solution.py:453

commit v3 on v2

--- a/solution.py
+++ b/solution.py
@@ -99,25 +99,40 @@
     yield
 
 
-def forward_mode(m, psi0, window, kernel, tables, psi1, far, xb, ks, zs):
-    forward, inverse, left = tables
+def enter_mode(slot, psi0, psi1, window, kernel, tables, xb, ks, zs):
     for rows in chunks():
         re, im = product(halves(window, 0, rows), (psi0[rows, 0:N], psi0[rows, N : 2 * N]), False)
-        xb[m, rows, 0:N] = re.astype(BF16)
-        xb[m, rows, N : 2 * N] = im.astype(BF16)
-    yield
-    yield from propagate(xb, ks, zs, m, kernel, tables, False)
-    psi1[m] = second_pass(ks, m, left)
-    yield
-    for rows in chunks():
-        re, im = product(halves(window, 1, rows), halves(psi1, m, rows), False)
-        xb[m, rows, 0:N] = re.astype(BF16)
-        xb[m, rows, N : 2 * N] = im.astype(BF16)
-    yield
-    first_pass(xb, ks, m, forward, False)
-    yield
-    far[m] = second_pass(ks, m, left)
-    yield
+        xb[slot, rows, 0:N] = re.astype(BF16)
+        xb[slot, rows, N : 2 * N] = im.astype(BF16)
+    yield
+    yield from propagate(xb, ks, zs, slot, kernel, tables, False)
+    psi1[...] = second_pass(ks, slot, tables[2])
+    yield
+
+
+def leave_mode(slot, psi1, far, window, tables, xb, ks):
+    for rows in chunks():
+        re, im = product(halves(window, 1, rows), (psi1[rows, 0:N], psi1[rows, N : 2 * N]), False)
+        xb[slot, rows, 0:N] = re.astype(BF16)
+        xb[slot, rows, N : 2 * N] = im.astype(BF16)
+    yield
+    first_pass(xb, ks, slot, tables[0], False)
+    yield
+    far[...] = second_pass(ks, slot, tables[2])
+    yield
+
+
+def chain(*tasks):
+    for task in tasks:
+        yield from task
+
+
+def together(tasks):
+    tasks = list(tasks)
+    while tasks:
+        tasks = [task for task in tasks if next(task, tasks) is not tasks]
+        if tasks:
+            yield
 
 
 def backward_mode(slot, psi0, psi1, far, scale, window, kernel, tables, pieces, xb, ks, zs):
@@ -162,15 +177,6 @@
         if waiting:
             running.append(waiting.pop(0))
         running = [task for task in running if next(task, running) is not running]
-
-
-def add_intensity(far, out):
-    for rows in chunks():
-        terms = []
-        for m in range(2):
-            re, im = halves(far, m, rows)
-            terms.append(re * re + im * im)
-        out[rows, :] = terms[0] + terms[1]
 
 
 def pack_kernel(core, obj, probe, row_first, row_last, col_first, col_last, chosen, edge_first, edge_last, sems):
@@ -195,8 +201,8 @@
         copy.wait()
 
 
-def own_kernel(offsets, obj, top, bottom, left_in, right_in, corner_left, corner_right, probe, kernel,
-               gram, fwd_t, inv_t, left_t, window, psi1, far, intensity, ext, xb, ks, zs):
+def own_kernel(offsets, obj, top, bottom, left_in, right_in, corner_up, corner_down, probe, kernel,
+               fwd_t, inv_t, left_t, window, psi1, ext, xb, ks, zs):
     tables = (fwd_t, inv_t, left_t)
     low = lanes((HALO, 2 * HALO)) < HALO
 
@@ -214,9 +220,9 @@
             ext[q, HALO : HALO + N, 0:N] = obj[s, part]
             ext[q, HALO + N : FRAME, 0:N] = bottom[s, part]
             ext[q, 0:HALO, N:FRAME] = border(
-                corner_right[s, HALO : 2 * HALO], corner_left[s, HALO : 2 * HALO], part)
+                corner_up[s, 1], corner_up[s, 0], part)
             ext[q, HALO + N : FRAME, N:FRAME] = border(
-                corner_right[s, 0:HALO], corner_left[s, 0:HALO], part)
+                corner_down[s, 1], corner_down[s, 0], part)
             for rows in chunks(N, HALO):
                 ext[q, HALO + rows.start : HALO + rows.stop, N:FRAME] = border(
                     right_in[s, rows], left_in[s, rows], part)
@@ -224,38 +230,38 @@
                 block = ext[q, pl.ds(row_base + rows.start, 72), :]
                 block = pltpu.roll(block, lax.rem(72 - row_rest, 72), 0)[:64]
                 window[s, rows, part * N : (part + 1) * N] = pltpu.roll(block, shift, 1)[:, :N]
-    interleave(forward_mode(m, probe.at[m], window, kernel, tables, psi1, far, xb, ks, zs) for m in range(2))
-    add_intensity(far, intensity)
-
-
-def near_kernel(probe, kernel, fwd_t, inv_t, left_t, window, psi1, far, intensity, xb, ks, zs):
-    interleave([forward_mode(0, probe, window, kernel, (fwd_t, inv_t, left_t), psi1, far, xb, ks, zs)])
-    for rows in chunks():
-        re, im = halves(far, 0, rows)
-        intensity[rows, :] = re * re + im * im
-
-
-def other_kernel(offsets, obj, probe, near, swapped, kernel, fwd_t, inv_t, left_t, patterns, window,
-                 psi1_own, far_own, intensity, psi1_near, far_near, intensity_near, gradient, row_top, row_bottom,
-                 col_left, col_right, corner_left, corner_right, psi1, far, inten, xb, ks, zs, back, frame):
+    interleave([together(
+        enter_mode(m, probe.at[m], psi1.at[m], window, kernel, tables, xb, ks, zs) for m in range(2))])
+
+
+def other_kernel(offsets, obj, probe, near, swapped, kernel, fwd_t, inv_t, left_t, patterns, window, psi1_own,
+                 gradient, row_top, row_bottom, col_left, col_right, corner_left, corner_right,
+                 psi1, far, inten, xb, ks, zs, back, frame):
     tables = (fwd_t, inv_t, left_t)
-    interleave([forward_mode(0, swapped, window, kernel, tables, psi1, far, xb, ks, zs)])
-    for rows in chunks():
-        re, im = halves(far, 0, rows)
-        inten[rows, :] = intensity[rows, :] + (intensity_near[rows, :] + (re * re + im * im))
+    entering = [(probe.at[0], psi1_own.at[0]), (probe.at[1], psi1_own.at[1]), (near, psi1.at[0]), (swapped, psi1.at[1])]
+
+    def leaving(k):
+        return leave_mode(k, entering[k][1], far.at[k], window, tables, xb, ks)
+
+    interleave([
+        together(
+            chain(enter_mode(k, *entering[k], window, kernel, tables, xb, ks, zs), leaving(k)) for k in (2, 3)),
+        together(leaving(k) for k in (0, 1)),
+    ])
+    for rows in chunks():
+        terms = []
+        for k in range(4):
+            re, im = halves(far, k, rows)
+            terms.append(re * re + im * im)
+        inten[rows, :] = (terms[0] + terms[1]) + (terms[2] + terms[3])
     for rows in chunks():
         inten[rows, :] = (inten[rows, :] * (1.0 / MODES) - patterns[0, rows, :]) * (2.0 / MODES)
     row_base, row_rest = aligned(offsets[0, 0])
     shift = lax.rem(HALO + N + offsets[0, 1], FRAME)
-    modes = [
-        (probe.at[0], psi1_own.at[0], far_own.at[0]),
-        (probe.at[1], psi1_own.at[1], far_own.at[1]),
-        (near, psi1_near.at[0], far_near.at[0]),
-        (swapped, psi1.at[0], far.at[0]),
-    ]
     interleave(
-        backward_mode(k, psi0, psi, wave, inten, window, kernel, tables, back, xb, ks, zs)
-        for k, (psi0, psi, wave) in enumerate(modes))
+        together(
+            backward_mode(k, *entering[k], far.at[k], inten, window, kernel, tables, back, xb, ks, zs) for k in pair)
+        for pair in ((0, 1), (2, 3)))
     low = lanes((HALO, 2 * HALO)) < HALO
     zero = jnp.zeros((HALO, 2 * HALO), F32)
     gap = jnp.zeros((8, FRAME), F32)
@@ -285,12 +291,8 @@
             right, left = strips(slice(HALO + rows.start, HALO + rows.stop))
             col_right[s, rows] = right
             col_left[s, rows] = left
-        right, left = strips(slice(HALO + N, FRAME))
-        corner_right[s, 0:HALO] = right
-        corner_left[s, 0:HALO] = left
-        right, left = strips(slice(0, HALO))
-        corner_right[s, HALO : 2 * HALO] = right
-        corner_left[s, HALO : 2 * HALO] = left
+        corner_right[s, 0], corner_left[s, 0] = strips(slice(HALO + N, FRAME))
+        corner_right[s, 1], corner_left[s, 1] = strips(slice(0, HALO))
 
 
 def put_rows(out, first_row, sums):
@@ -314,25 +316,17 @@
     put_rows(out, 0, lax.fori_loop(0, 4 * (N // 16), body, zero))
 
 
-def sy_kernel(steps, changes, after, out):
+def gram_kernel(steps, changes, after, out):
     def terms(s, part, rows):
         st = [steps[i, s, part, rows, :].astype(F32) for i in range(MEM)]
         ch = [changes[i, s, part, rows, :].astype(F32) for i in range(MEM)]
-        return [st[i] * ch[j] for i, j in SY_PAIRS]
-
-    accumulate(terms, len(SY_PAIRS), out)
-
-
-def yy_kernel(changes, after, out):
-    def terms(s, part, rows):
-        ch = [changes[i, s, part, rows, :].astype(F32) for i in range(MEM)]
-        return [ch[i] * ch[j] for i, j in SY_PAIRS]
-
-    accumulate(terms, len(SY_PAIRS), out)
+        return [st[i] * ch[j] for i, j in SY_PAIRS] + [ch[i] * ch[j] for i, j in SY_PAIRS]
+
+    accumulate(terms, 2 * len(SY_PAIRS), out)
 
 
 def dots_kernel(gradient_in, row_up, row_down, col_left, col_right, steps, changes,
-                gram_sy, gram_yy, gradient, out, stored, sums, sem):
+                gram, gradient, out, stored, sums, sem):
     low = lanes((64, 2 * HALO)) < HALO
     for s in range(2):
         for part in range(2):
@@ -363,8 +357,7 @@
 
     zero = tuple(jnp.zeros((8, N // 2), F32) for _ in range(2 * MEM))
     sums[...] = jnp.zeros(sums.shape, F32)
-    sums[0 : len(SY_PAIRS), :] = gram_sy[0 : len(SY_PAIRS), :]
-    sums[len(SY_PAIRS) : SG_ROW, :] = gram_yy[0 : len(SY_PAIRS), :]
+    sums[0:SG_ROW, :] = gram[0:SG_ROW, :]
     put_rows(sums, SG_ROW, lax.fori_loop(0, 4 * (N // 64), body, zero))
     totals = jnp.sum(sums[...], axis=1, keepdims=True)
     row = lax.broadcasted_iota(jnp.int32, (128, 128), 0)
@@ -453,10 +446,6 @@
     return lax.ppermute(value, axis, [(i, (i + step) % size) for i in range(size)])
 
 
-def packed(value, columns):
-    return jnp.concatenate([value[:, 0, :, columns], value[:, 1, :, columns]], -1)
-
-
 def near_pairs(rows, modes):
     half = rows // modes
     pairs = []
@@ -474,7 +463,7 @@
     core = (lax.axis_index("ty") & 1).astype(jnp.int32).reshape(1)
     tables = dft_tables()
     first, last = slice(0, HALO), slice(N - HALO, N)
-    strip, side, corner = shape(2, 2, HALO, N), shape(2, N, 2 * HALO), shape(2, 2 * HALO, 2 * HALO)
+    strip, side, corner = shape(2, 2, HALO, N), shape(2, N, 2 * HALO), shape(2, 2, HALO, 2 * HALO)
     row_first, row_last, col_first, col_last, chosen = call(
         pack_kernel, (strip, strip, side, side, shape(N, 2 * N)),
         [scratch(2, 2, N, 2 * HALO), scratch(2, 2, N, 2 * HALO), pltpu.SemaphoreType.DMA((5,))],
@@ -485,37 +474,34 @@
     left = shifted(col_last, "tx", 1)
     right = shifted(col_first, "tx", -1)
     near = lax.ppermute(chosen, ("ty", "mode"), near_pairs(rows_axis, modes_axis))
-    strips, phase = lax.optimization_barrier((jnp.concatenate([bottom, top], 2), phase))
-    corner_last, corner_first = packed(strips, last), packed(strips, first)
-    corner_left = shifted(corner_last, "tx", 1)
-    corner_right = shifted(corner_first, "tx", -1)
+    sides = jnp.stack([left, right], 1)
+    going_down, going_up = sides[:, :, last], sides[:, :, first]
+    corner_up = shifted(going_down, "ty", 1)
+    corner_down = shifted(going_up, "ty", -1)
     kernel = jnp.stack([jnp.cos(phase), jnp.sin(phase)])
-    gram_sy = call(sy_kernel, (shape(16, 128),), [], (past_steps, past_changes, corner_first))[0]
+    near, top, bottom, corner_up, corner_down, kernel = lax.optimization_barrier(
+        (near, top, bottom, corner_up, corner_down, kernel))
+    swapped = lax.ppermute(near, "ty", [(i, i ^ 1) for i in range(rows_axis)])
 
     def work(slots):
         return [scratch(slots, N, 2 * N, dtype=BF16), scratch(slots, 2 * N, 2 * N, dtype=BF16),
                 scratch(slots, N, 2 * N)]
 
-    window, psi1, far, intensity = call(
+    window, psi1 = call(
         own_kernel,
-        (shape(2, N, 2 * N), shape(2, N, 2 * N), shape(2, N, 2 * N), shape(N, N)),
+        (shape(2, N, 2 * N), shape(2, N, 2 * N)),
         [scratch(4, FRAME + 8, FRAME)] + work(2),
-        (offsets, object_field, top, bottom, left, right, corner_left, corner_right, probe, kernel,
-         gram_sy) + tables,
+        (offsets, object_field, top, bottom, left, right, corner_up, corner_down, probe, kernel)
+        + tables,
         smem=1,
     )
-    near, intensity = lax.optimization_barrier((near, intensity))
-    swapped = lax.ppermute(near, "ty", [(i, i ^ 1) for i in range(rows_axis)])
-    psi1_near, far_near, intensity_near = call(
-        near_kernel, (shape(1, N, 2 * N), shape(1, N, 2 * N), shape(N, N)), work(1),
-        (near, kernel) + tables + (window,))
     partial, row_top, row_bottom, col_left, col_right, corner_left, corner_right = call(
         other_kernel,
         (shape(2, 2, N, N), strip, strip, side, side, corner, corner),
-        [scratch(1, N, 2 * N), scratch(1, N, 2 * N), scratch(N, N)] + work(4)
+        [scratch(2, N, 2 * N), scratch(4, N, 2 * N), scratch(N, N)] + work(4)
         + [scratch(2, 2, N, 2 * N), scratch(4, FRAME + 8, FRAME)],
         (offsets, object_field, probe, near, swapped, kernel) + tables
-        + (patterns, window, psi1, far, intensity, psi1_near, far_near, intensity_near),
+        + (patterns, window, psi1),
         smem=1,
     )
     from_left = shifted(corner_right, "tx", 1)
@@ -523,24 +509,23 @@
     side_left = shifted(col_right, "tx", 1)
     side_right = shifted(col_left, "tx", -1)
 
-
-    def with_corners(strip_now, rows):
+    def with_corners(strip_now, k):
         def unpacked(block):
-            return jnp.stack([block[:, rows, :HALO], block[:, rows, HALO:]], 1)
+            return jnp.stack([block[:, k, :, :HALO], block[:, k, :, HALO:]], 1)
 
         gap = jnp.zeros(strip_now.shape[:3] + (N - 2 * HALO,), F32)
         return strip_now + jnp.concatenate([unpacked(from_left), gap, unpacked(from_right)], -1)
 
-    below, above = with_corners(row_bottom, slice(0, HALO)), with_corners(row_top, slice(HALO, 2 * HALO))
+    below, above = with_corners(row_bottom, 0), with_corners(row_top, 1)
     row_up = shifted(below, "ty", 1)
     row_down = shifted(above, "ty", -1)
-    gram_yy = call(yy_kernel, (shape(16, 128),), [], (past_changes, above))[0]
+    gram = call(gram_kernel, (shape(32, 128),), [], (past_steps, past_changes, above))[0]
     gradient, sums, stored = call(
         dots_kernel,
         (shape(2, 2, N, N), shape(128, 1, 128), shape(2, 2, N, N)),
         [scratch(128, 128), pltpu.SemaphoreType.DMA],
         (partial, row_up, row_down, side_left, side_right, past_steps, past_changes,
-         gram_sy, gram_yy),
+         gram),
         stored=(2,),
     )
     parts = lax.all_to_all(sums, TILES, 0, 0)

time: 78.1 us -> 76.3 us (0.977)
  Pallas kernels: 24 us -> 20.7 us
  waiting for transfers between devices: 5.52 us -> 7.06 us
  starting transfers between devices: 24.4 us -> 23.4 us
    pallas_call x8 -> x6, Pallas kernels: 24 us -> 20.7 us  [call(): pl.pallas_call(kernel, out_shape=outs, in_specs=[SMEM] * smem + [ANY] * r...]
    ppermute x1, starting transfers between devices: 3.12 us -> 1.78 us  [per_device(): swapped = lax.ppermute(near, 'ty', [(i, i ^ 1) for i in range(rows_axis)])]
    another operation x1, local copies, waits for them, and re-layouts: 0.97 us -> 1.85 us  [per_device(): kernel = jnp.stack([jnp.cos(phase), jnp.sin(phase)])]
  transfers between devices with their start and end apart: 14 -> 14, of which waited for: 4 -> 6; matrix products, arithmetic and copies ran while one was open for 2% -> 3% of each run, Pallas kernels for 14% -> 9%
where the time goes in v3:
time: 76.3 us; the launch traced here: 76.1 us
  starting transfers between devices  23.4 us (31%)
  blocking collectives  21.5 us (28%)
  Pallas kernels  20.7 us (27%)
  waiting for transfers between devices  7.06 us (9%)
  local copies, waits for them, and re-layouts  2.16 us (3%)
  between operations  1.07 us (1%)
    all_to_all x1, blocking collectives, per_device(): parts = lax.all_to_all(sums, TILES, 0, 0)  21.5 us
    pallas_call x6, Pallas kernels, call(): pl.pallas_call(kernel, out_shape=outs, in_specs=[SMEM] * smem + [ANY] * r...  20.7 us
    ppermute x12, starting transfers between devices, shifted(): lax.ppermute(value, axis, [(i, (i + step) % size) for i in range(size)])  18.9 us
    ppermute x12, waiting for transfers between devices, shifted(): lax.ppermute(value, axis, [(i, (i + step) % size) for i in range(size)])  6.29 us
    ppermute x1, starting transfers between devices, per_device(): lax.ppermute(chosen, ('ty', 'mode'), near_pairs(rows_axis, modes_axis))  2.73 us
    another operation x1, local copies, waits for them, and re-layouts, per_device(): kernel = jnp.stack([jnp.cos(phase), jnp.sin(phase)])  1.85 us
    ppermute x1, starting transfers between devices, per_device(): swapped = lax.ppermute(near, 'ty', [(i, i ^ 1) for i in range(rows_axis)])  1.78 us
  transfers between devices with their start and end apart: 14, of which 6 were waited for; matrix products, arithmetic and copies ran while one was open for 3% of the time, Pallas kernels for 9%

profile of v3, /device:TPU:1, one launch (start us, length us, event | category | flops | bytes accessed | tf_op | source)
XLA Modules:
  0.0 76.1 jit_solution(10923003690433910845)
XLA Ops:
  0.6 0.0 copy-start.4
  0.6 0.0 copy-start.5
  0.7 0.0 copy-start.6
  0.7 1.7 %shard_map.113 = (f32[2,2,64,256]{3,2,1,0:T(8,128)S(1)}, f32[2,2,64,256]{3,2,1,0:T(8,128)S(1)}, f32[2,256,128]{2,1,0:T(8,128)S(1)}, f32[2,256,128]{2,1,0:T(8,128)S(1)}, f32[256,512]{1,0:T(8,128)S(1)}) custom-call(s32[1]{0:T(128)} %bitcast.core, f32[2,2,256,256]{3,2,1,0:T(8,128)} %obj.7, f32[2,256,512]{2,1,0:T(8,128)} %probe.5), custom_call_target="tpu_custom_call" | custom-call | tf_op jit(solution)/shard_map/pallas_call | solution.py:434
  2.4 2.5 %collective-permute-start.3 = (f32[2,256,128]{2,1,0:T(8,128)S(1)}, f32[2,256,128]{2,1,0:T(8,128)S(1)}, u32[]{:S(2)}, u32[]{:S(2)}) collective-permute-start(f32[2,256,128]{2,1,0:T(8,128)S(1)} %get-tuple-element.28), channel_id=1, source_target_pairs={{0,2},{2,4},{4,6},{6,8},{8,10},{10,12},{12,14},{14,0},{1,3},{3,5},... | collective-permute-start | bytes 786440 | tf_op jit(solution)/shard_map/ppermute | solution.py:446
  5.0 4.0 %collective-permute-start.4 = (f32[2,256,128]{2,1,0:T(8,128)S(1)}, f32[2,256,128]{2,1,0:T(8,128)S(1)}, u32[]{:S(2)}, u32[]{:S(2)}) collective-permute-start(f32[2,256,128]{2,1,0:T(8,128)S(1)} %get-tuple-element.29), channel_id=1, source_target_pairs={{0,14},{2,0},{4,2},{6,4},{8,6},{10,8},{12,10},{14,12},{1,15},{3,1}... | collective-permute-start | bytes 786440 | tf_op jit(solution)/shard_map/ppermute | solution.py:446
  9.0 2.7 %collective-permute-start = (f32[256,512]{1,0:T(8,128)S(1)}, f32[256,512]{1,0:T(8,128)S(1)}, u32[]{:S(2)}, u32[]{:S(2)}) collective-permute-start(f32[256,512]{1,0:T(8,128)S(1)} %get-tuple-element.25), channel_id=1, source_target_pairs={{0,129},{1,128},{16,145},{17,144},{32,161},{33,160},{48,177},{49,1... | collective-permute-start | bytes 1572872 | tf_op jit(solution)/shard_map/ppermute | solution.py:476
  11.7 2.3 %collective-permute-start.1 = (f32[2,2,64,256]{3,2,1,0:T(8,128)S(1)}, f32[2,2,64,256]{3,2,1,0:T(8,128)S(1)}, u32[]{:S(2)}, u32[]{:S(2)}) collective-permute-start(f32[2,2,64,256]{3,2,1,0:T(8,128)S(1)} %get-tuple-element.26), channel_id=1, source_target_pairs={{0,16},{16,32},{32,48},{48,64},{64,80},{80,96},{96,112},{112,128},... | collective-permute-start | bytes 786440 | tf_op jit(solution)/shard_map/ppermute | solution.py:446
  14.1 0.9 %collective-permute-done.3.left_in = f32[2,256,128]{2,1,0:T(8,128)S(1)} collective-permute-done((f32[2,256,128]{2,1,0:T(8,128)S(1)}, f32[2,256,128]{2,1,0:T(8,128)S(1)}, u32[]{:S(2)}, u32[]{:S(2)}) %collective-permute-start.3) | collective-permute-done | bytes 262176 | tf_op jit(solution)/shard_map/ppermute | solution.py:446
  15.0 2.4 %collective-permute-start.5 = (f32[2,2,64,128]{3,2,1,0:T(8,128)S(1)}, f32[2,2,64,128]{3,2,1,0:T(8,128)S(1)}, u32[]{:S(2)}, u32[]{:S(2)}) collective-permute-start(f32[2,2,64,128]{3,2,1,0:T(8,128)S(1)} %get-tuple-element.49), channel_id=1, source_target_pairs={{0,16},{16,32},{32,48},{48,64},{64,80},{80,96},{96,112},{112,128},... | collective-permute-start | bytes 393224 | tf_op jit(solution)/shard_map/ppermute | solution.py:446
  17.4 1.9 %cosine_bitcast_fusion = (f32[1,256,256]{2,1,0:T(8,128)S(1)}, f32[1,256,256]{2,1,0:T(8,128)S(1)}) fusion(f32[256,256]{1,0:T(8,128)} %param.14), kind=kLoop, calls=%fused_computation.4 | loop fusion | bytes 786432 | tf_op jit(solution)/shard_map/stack | solution.py:481
  19.3 0.0 copy-start.7
  19.3 0.8 %collective-permute-done.2.bottom = f32[2,2,64,256]{3,2,1,0:T(8,128)S(1)} collective-permute-done((f32[2,2,64,256]{3,2,1,0:T(8,128)S(1)}, f32[2,2,64,256]{3,2,1,0:T(8,128)S(1)}, u32[]{:S(2)}, u32[]{:S(2)}) %collective-permute-start.2) | collective-permute-done | bytes 262176 | tf_op jit(solution)/shard_map/ppermute | solution.py:446
  20.2 1.9 %collective-permute-done.6.corner_down = f32[2,2,64,128]{3,2,1,0:T(8,128)S(1)} collective-permute-done((f32[2,2,64,128]{3,2,1,0:T(8,128)S(1)}, f32[2,2,64,128]{3,2,1,0:T(8,128)S(1)}, u32[]{:S(2)}, u32[]{:S(2)}) %collective-permute-start.6) | collective-permute-done | bytes 131104 | tf_op jit(solution)/shard_map/ppermute | solution.py:446
  22.1 0.8 %collective-permute-done.near = f32[256,512]{1,0:T(8,128)S(1)} collective-permute-done((f32[256,512]{1,0:T(8,128)S(1)}, f32[256,512]{1,0:T(8,128)S(1)}, u32[]{:S(2)}, u32[]{:S(2)}) %collective-permute-start) | collective-permute-done | bytes 524320 | tf_op jit(solution)/shard_map/ppermute | solution.py:476
  22.8 1.8 %collective-permute-start.7 = (f32[256,512]{1,0:T(8,128)S(1)}, f32[256,512]{1,0:T(8,128)S(1)}, u32[]{:S(2)}, u32[]{:S(2)}) collective-permute-start(f32[256,512]{1,0:T(8,128)S(1)} %collective-permute-done.near), channel_id=1, source_target_pairs={{0,16},{16,0},{32,48},{48,32},{64,80},{80,64},{96,112},{112,96},{1... | collective-permute-start | bytes 1572872 | tf_op jit(solution)/shard_map/ppermute | solution.py:484
  24.7 2.5 %shard_map.114 = (f32[2,256,512]{2,1,0:T(8,128)S(1)}, f32[2,256,512]{2,1,0:T(8,128)S(1)}) custom-call(s32[1,2]{1,0:T(1,128)S(1)} %copy-done.8, f32[2,2,256,256]{3,2,1,0:T(8,128)S(1)} %copy-done.2, f32[2,2,64,256]{3,2,1,0:T(8,128)S(1)} %collective-permute-done.1.top, f32[2,2,64,256]{3,2,1,0:T(8,128)S(1)} %collective-permute-done.2.bottom, ...), custom_call_target="tpu_custom_call" | custom-call | tf_op jit(solution)/shard_map/pallas_call | solution.py:434
  27.2 8.1 %shard_map.115 = (f32[2,2,256,256]{3,2,1,0:T(8,128)S(1)}, f32[2,2,64,256]{3,2,1,0:T(8,128)S(1)}, f32[2,2,64,256]{3,2,1,0:T(8,128)S(1)}, f32[2,256,128]{2,1,0:T(8...) custom-call(s32[1,2]{1,0:T(1,128)S(1)} %copy-done.8, ...), custom_call_target="tpu_custom_call" | custom-call | tf_op jit(solution)/shard_map/pallas_call | solution.py:434
  35.3 0.1 collective-permute-start.8
  35.4 0.1 pad.7.clone
  35.5 2.7 %collective-permute-start.9 = (f32[2,2,64,128]{3,2,1,0:T(8,128)S(1)}, f32[2,2,64,128]{3,2,1,0:T(8,128)S(1)}, u32[]{:S(2)}, u32[]{:S(2)}) collective-permute-start(f32[2,2,64,128]{3,2,1,0:T(8,128)S(1)} %get-tuple-element.41), channel_id=1, source_target_pairs={{0,14},{2,0},{4,2},{6,4},{8,6},{10,8},{12,10},{14,12},{1,15},{3,1}... | collective-permute-start | bytes 393224 | tf_op jit(solution)/shard_map/ppermute | solution.py:446
  38.1 2.7 %collective-permute-start.13 = (f32[2,256,128]{2,1,0:T(8,128)S(1)}, f32[2,256,128]{2,1,0:T(8,128)S(1)}, u32[]{:S(2)}, u32[]{:S(2)}) collective-permute-start(f32[2,256,128]{2,1,0:T(8,128)S(1)} %get-tuple-element.44), channel_id=1, source_target_pairs={{0,14},{2,0},{4,2},{6,4},{8,6},{10,8},{12,10},{14,12},{1,15},{3,1}... | collective-permute-start | bytes 786440 | tf_op jit(solution)/shard_map/ppermute | solution.py:446
  40.8 0.8 %collective-permute-done.8 = f32[2,2,64,128]{3,2,1,0:T(8,128)S(1)} collective-permute-done((f32[2,2,64,128]{3,2,1,0:T(8,128)S(1)}, f32[2,2,64,128]{3,2,1,0:T(8,128)S(1)}, u32[]{:S(2)}, u32[]{:S(2)}) %collective-permute-start.8) | collective-permute-done | bytes 131104 | tf_op jit(solution)/shard_map/ppermute | solution.py:446
  41.7 0.1 fusion
  41.8 0.1 fusion.1
  41.9 0.2 maximum_add_fusion.1
  42.0 2.2 %collective-permute-start.10 = (f32[2,2,64,256]{3,2,1,0:T(8,128)S(1)}, f32[2,2,64,256]{3,2,1,0:T(8,128)S(1)}, u32[]{:S(2)}, u32[]{:S(2)}) collective-permute-start(f32[2,2,64,256]{3,2,1,0:T(8,128)S(1)} %get-tuple-element.61), channel_id=1, source_target_pairs={{0,16},{16,32},{32,48},{48,64},{64,80},{80,96},{96,112},{112,128},... | collective-permute-start | bytes 786440 | tf_op jit(solution)/shard_map/ppermute | solution.py:446
  44.3 4.3 %shard_map.116.gram = f32[32,128]{1,0:T(8,128)S(1)} custom-call(bf16[5,2,2,256,256]{4,3,2,1,0:T(8,128)(2,1)S(1)} %copy-done, bf16[5,2,2,256,256]{4,3,2,1,0:T(8,128)(2,1)S(1)} %copy-done.1, f32[2,2,64,256]{3,2,1,0:T(8,128)S(1)} %get-tuple-element.60.after), custom_call_target="tpu_custom_call" | custom-call | tf_op jit(solution)/shard_map/pallas_call | solution.py:434
  48.6 1.8 %collective-permute-done.11.row_down = f32[2,2,64,256]{3,2,1,0:T(8,128)S(1)} collective-permute-done((f32[2,2,64,256]{3,2,1,0:T(8,128)S(1)}, f32[2,2,64,256]{3,2,1,0:T(8,128)S(1)}, u32[]{:S(2)}, u32[]{:S(2)}) %collective-permute-start.11) | collective-permute-done | bytes 262176 | tf_op jit(solution)/shard_map/ppermute | solution.py:446
  50.4 1.7 %shard_map.117 = (f32[2,2,256,256]{3,2,1,0:T(8,128)S(1)}, f32[128,1,128]{2,1,0:T(1,128)S(1)}, f32[2,2,256,256]{3,2,1,0:T(8,128)}) custom-call(f32[2,2,256,256]{3,2,1,0:T(8,128)S(1)} %get-tuple-element.38.gradient_in, f32[2,2,64,256]{3,2,1,0:T(8,128)S(1)} %collective-permute-done.10.row_up, f32[2,2,64,256]{3,2,1,0:T(8,128)S(1)} %collective-permute-done.11.row_down, ...), custom_call_target="tpu_custom_call" | custom-call | tf_op jit(solution)/shard_map/pallas_call | solution.py:434
  52.1 21.5 %all_to_all.5.parts = f32[128,1,128]{2,1,0:T(1,128)S(1)} all-to-all(f32[128,1,128]{2,1,0:T(1,128)S(1)} %get-tuple-element.45), channel_id=1, replica_groups=mesh['ty'=16,'tx'=8,'mode'=2] {'ty','tx'}, dimensions={0} | all-to-all | bytes 131072 | tf_op jit(solution)/shard_map/all_to_all | solution.py:531
  73.6 2.3 %shard_map.118 = f32[2,2,256,256]{3,2,1,0:T(8,128)} custom-call(f32[128,1,128]{2,1,0:T(1,128)S(1)} %all_to_all.5.parts, f32[2,2,256,256]{3,2,1,0:T(8,128)S(1)} %copy-done.2, f32[2,2,256,256]{3,2,1,0:T(8,128)S(1)} %get-tuple-element.46.gradient, bf16[5,2,2,256,256]{4,3,2,1,0:T(8,128)(2,1)S(1)} %copy-done, bf16[5,2,2,256,256]{4,3,2,1,0:T(8,128)(2,1)S(1)} %copy-done.1), custom_call_target="tpu_custom_call" | custom-call | tf_op jit(solution)/shard_map/pallas_call | solution.py:434
  (29 shorter events, 0.1 us)
Async XLA Ops:
  0.6 24.0 %copy-start.4 = (bf16[512,512]{1,0:T(8,128)(2,1)S(1)}, bf16[512,512]{1,0:T(8,128)(2,1)}, u32[]{:S(2)}) copy-start(bf16[512,512]{1,0:T(8,128)(2,1)} %constant.15.clone.fwd_t) | copy-start | bytes 1572868
  0.6 24.0 %copy-start.5 = (bf16[512,512]{1,0:T(8,128)(2,1)S(1)}, bf16[512,512]{1,0:T(8,128)(2,1)}, u32[]{:S(2)}) copy-start(bf16[512,512]{1,0:T(8,128)(2,1)} %constant.16.clone.inv_t) | copy-start | bytes 1572868
  0.7 24.0 %copy-start.6 = (bf16[256,512]{1,0:T(8,128)(2,1)S(1)}, bf16[256,512]{1,0:T(8,128)(2,1)}, u32[]{:S(2)}) copy-start(bf16[256,512]{1,0:T(8,128)(2,1)} %constant.17.clone.left_t) | copy-start | bytes 786436
  0.7 24.0 %copy-start.2 = (f32[2,2,256,256]{3,2,1,0:T(8,128)S(1)}, f32[2,2,256,256]{3,2,1,0:T(8,128)}, u32[]{:S(2)}) copy-start(f32[2,2,256,256]{3,2,1,0:T(8,128)} %obj.7) | copy-start | bytes 3145732
  0.7 24.0 %copy-start.3 = (f32[2,256,512]{2,1,0:T(8,128)S(1)}, f32[2,256,512]{2,1,0:T(8,128)}, u32[]{:S(2)}) copy-start(f32[2,256,512]{2,1,0:T(8,128)} %probe.5) | copy-start | bytes 3145732
  0.7 24.0 %copy-start.8 = (s32[1,2]{1,0:T(1,128)S(1)}, s32[1,2]{1,0:T(1,128)}, u32[]{:S(2)}) copy-start(s32[1,2]{1,0:T(1,128)} %offsets.3) | copy-start | bytes 28
  2.4 12.5 %collective-permute-start.3 = (f32[2,256,128]{2,1,0:T(8,128)S(1)}, f32[2,256,128]{2,1,0:T(8,128)S(1)}, u32[]{:S(2)}, u32[]{:S(2)}) collective-permute-start(f32[2,256,128]{2,1,0:T(8,128)S(1)} %get-tuple-element.28), channel_id=1, source_target_pairs={{0,2},{2,4},{4,6},{6,8},{8,10},{10,12},{12,14},{14,0},{1,3},{3,5},... | collective-permute-start | bytes 786440 | tf_op jit(solution)/shard_map/ppermute | solution.py:446
  5.0 10.0 %collective-permute-start.4 = (f32[2,256,128]{2,1,0:T(8,128)S(1)}, f32[2,256,128]{2,1,0:T(8,128)S(1)}, u32[]{:S(2)}, u32[]{:S(2)}) collective-permute-start(f32[2,256,128]{2,1,0:T(8,128)S(1)} %get-tuple-element.29), channel_id=1, source_target_pairs={{0,14},{2,0},{4,2},{6,4},{8,6},{10,8},{12,10},{14,12},{1,15},{3,1}... | collective-permute-start | bytes 786440 | tf_op jit(solution)/shard_map/ppermute | solution.py:446
  9.0 13.8 %collective-permute-start = (f32[256,512]{1,0:T(8,128)S(1)}, f32[256,512]{1,0:T(8,128)S(1)}, u32[]{:S(2)}, u32[]{:S(2)}) collective-permute-start(f32[256,512]{1,0:T(8,128)S(1)} %get-tuple-element.25), channel_id=1, source_target_pairs={{0,129},{1,128},{16,145},{17,144},{32,161},{33,160},{48,177},{49,1... | collective-permute-start | bytes 1572872 | tf_op jit(solution)/shard_map/ppermute | solution.py:476
  11.7 7.6 %collective-permute-start.1 = (f32[2,2,64,256]{3,2,1,0:T(8,128)S(1)}, f32[2,2,64,256]{3,2,1,0:T(8,128)S(1)}, u32[]{:S(2)}, u32[]{:S(2)}) collective-permute-start(f32[2,2,64,256]{3,2,1,0:T(8,128)S(1)} %get-tuple-element.26), channel_id=1, source_target_pairs={{0,16},{16,32},{32,48},{48,64},{64,80},{80,96},{96,112},{112,128},... | collective-permute-start | bytes 786440 | tf_op jit(solution)/shard_map/ppermute | solution.py:446
  14.1 6.1 %collective-permute-start.2 = (f32[2,2,64,256]{3,2,1,0:T(8,128)S(1)}, f32[2,2,64,256]{3,2,1,0:T(8,128)S(1)}, u32[]{:S(2)}, u32[]{:S(2)}) collective-permute-start(f32[2,2,64,256]{3,2,1,0:T(8,128)S(1)} %get-tuple-element.27), channel_id=1, source_target_pairs={{0,240},{16,0},{32,16},{48,32},{64,48},{80,64},{96,80},{112,96},{1... | collective-permute-start | bytes 786440 | tf_op jit(solution)/shard_map/ppermute | solution.py:446
  15.0 5.2 %collective-permute-start.5 = (f32[2,2,64,128]{3,2,1,0:T(8,128)S(1)}, f32[2,2,64,128]{3,2,1,0:T(8,128)S(1)}, u32[]{:S(2)}, u32[]{:S(2)}) collective-permute-start(f32[2,2,64,128]{3,2,1,0:T(8,128)S(1)} %get-tuple-element.49), channel_id=1, source_target_pairs={{0,16},{16,32},{32,48},{48,64},{64,80},{80,96},{96,112},{112,128},... | collective-permute-start | bytes 393224 | tf_op jit(solution)/shard_map/ppermute | solution.py:446
  17.4 4.7 %collective-permute-start.6 = (f32[2,2,64,128]{3,2,1,0:T(8,128)S(1)}, f32[2,2,64,128]{3,2,1,0:T(8,128)S(1)}, u32[]{:S(2)}, u32[]{:S(2)}) collective-permute-start(f32[2,2,64,128]{3,2,1,0:T(8,128)S(1)} %get-tuple-element.48), channel_id=1, source_target_pairs={{0,240},{16,0},{32,16},{48,32},{64,48},{80,64},{96,80},{112,96},{1... | collective-permute-start | bytes 393224 | tf_op jit(solution)/shard_map/ppermute | solution.py:446
  19.3 7.9 %copy-start.7 = (f32[1,256,256]{2,1,0:T(8,128)S(1)}, f32[1,256,256]{2,1,0:T(8,128)}, u32[]{:S(2)}) copy-start(f32[1,256,256]{2,1,0:T(8,128)} %patterns.1) | copy-start | bytes 786436
  22.8 4.3 %collective-permute-start.7 = (f32[256,512]{1,0:T(8,128)S(1)}, f32[256,512]{1,0:T(8,128)S(1)}, u32[]{:S(2)}, u32[]{:S(2)}) collective-permute-start(f32[256,512]{1,0:T(8,128)S(1)} %collective-permute-done.near), channel_id=1, source_target_pairs={{0,16},{16,0},{32,48},{48,32},{64,80},{80,64},{96,112},{112,96},{1... | collective-permute-start | bytes 1572872 | tf_op jit(solution)/shard_map/ppermute | solution.py:484
  27.2 17.1 %copy-start.1 = (bf16[5,2,2,256,256]{4,3,2,1,0:T(8,128)(2,1)S(1)}, bf16[5,2,2,256,256]{4,3,2,1,0:T(8,128)(2,1)}, u32[]{:S(2)}) copy-start(bf16[5,2,2,256,256]{4,3,2,1,0:T(8,128)(2,1)} %changes.5) | copy-start | bytes 7864324
  35.3 9.0 %copy-start = (bf16[5,2,2,256,256]{4,3,2,1,0:T(8,128)(2,1)S(1)}, bf16[5,2,2,256,256]{4,3,2,1,0:T(8,128)(2,1)}, u32[]{:S(2)}) copy-start(bf16[5,2,2,256,256]{4,3,2,1,0:T(8,128)(2,1)} %steps.5) | copy-start | bytes 7864324
  35.3 6.4 %collective-permute-start.8 = (f32[2,2,64,128]{3,2,1,0:T(8,128)S(1)}, f32[2,2,64,128]{3,2,1,0:T(8,128)S(1)}, u32[]{:S(2)}, u32[]{:S(2)}) collective-permute-start(f32[2,2,64,128]{3,2,1,0:T(8,128)S(1)} %get-tuple-element.40), channel_id=1, source_target_pairs={{0,2},{2,4},{4,6},{6,8},{8,10},{10,12},{12,14},{14,0},{1,3},{3,5},... | collective-permute-start | bytes 393224 | tf_op jit(solution)/shard_map/ppermute | solution.py:446
  35.5 6.3 %collective-permute-start.9 = (f32[2,2,64,128]{3,2,1,0:T(8,128)S(1)}, f32[2,2,64,128]{3,2,1,0:T(8,128)S(1)}, u32[]{:S(2)}, u32[]{:S(2)}) collective-permute-start(f32[2,2,64,128]{3,2,1,0:T(8,128)S(1)} %get-tuple-element.41), channel_id=1, source_target_pairs={{0,14},{2,0},{4,2},{6,4},{8,6},{10,8},{12,10},{14,12},{1,15},{3,1}... | collective-permute-start | bytes 393224 | tf_op jit(solution)/shard_map/ppermute | solution.py:446
  38.1 10.4 %collective-permute-start.12 = (f32[2,256,128]{2,1,0:T(8,128)S(1)}, f32[2,256,128]{2,1,0:T(8,128)S(1)}, u32[]{:S(2)}, u32[]{:S(2)}) collective-permute-start(f32[2,256,128]{2,1,0:T(8,128)S(1)} %get-tuple-element.43), channel_id=1, source_target_pairs={{0,2},{2,4},{4,6},{6,8},{8,10},{10,12},{12,14},{14,0},{1,3},{3,5},... | collective-permute-start | bytes 786440 | tf_op jit(solution)/shard_map/ppermute | solution.py:446
  38.1 10.4 %collective-permute-start.13 = (f32[2,256,128]{2,1,0:T(8,128)S(1)}, f32[2,256,128]{2,1,0:T(8,128)S(1)}, u32[]{:S(2)}, u32[]{:S(2)}) collective-permute-start(f32[2,256,128]{2,1,0:T(8,128)S(1)} %get-tuple-element.44), channel_id=1, source_target_pairs={{0,14},{2,0},{4,2},{6,4},{8,6},{10,8},{12,10},{14,12},{1,15},{3,1}... | collective-permute-start | bytes 786440 | tf_op jit(solution)/shard_map/ppermute | solution.py:446
  42.0 6.6 %collective-permute-start.10 = (f32[2,2,64,256]{3,2,1,0:T(8,128)S(1)}, f32[2,2,64,256]{3,2,1,0:T(8,128)S(1)}, u32[]{:S(2)}, u32[]{:S(2)}) collective-permute-start(f32[2,2,64,256]{3,2,1,0:T(8,128)S(1)} %get-tuple-element.61), channel_id=1, source_target_pairs={{0,16},{16,32},{32,48},{48,64},{64,80},{80,96},{96,112},{112,128},... | collective-permute-start | bytes 786440 | tf_op jit(solution)/shard_map/ppermute | solution.py:446
  44.3 6.1 %collective-permute-start.11 = (f32[2,2,64,256]{3,2,1,0:T(8,128)S(1)}, f32[2,2,64,256]{3,2,1,0:T(8,128)S(1)}, u32[]{:S(2)}, u32[]{:S(2)}) collective-permute-start(f32[2,2,64,256]{3,2,1,0:T(8,128)S(1)} %get-tuple-element.60.after), channel_id=1, source_target_pairs={{0,240},{16,0},{32,16},{48,32},{64,48},{80,64},{96,80},{112,96},{1... | collective-permute-start | bytes 786440 | tf_op jit(solution)/shard_map/ppermute | solution.py:446

commit v4 on v3

--- a/solution.py
+++ b/solution.py
@@ -201,31 +201,37 @@
         copy.wait()
 
 
-def own_kernel(offsets, obj, top, bottom, left_in, right_in, corner_up, corner_down, probe, kernel,
-               fwd_t, inv_t, left_t, window, psi1, ext, xb, ks, zs):
-    tables = (fwd_t, inv_t, left_t)
-    low = lanes((HALO, 2 * HALO)) < HALO
-
-    def border(right_block, left_block, part):
-        if part == 0:
-            return jnp.where(low, right_block, pltpu.roll(left_block, HALO, 1))
-        return jnp.where(low, pltpu.roll(right_block, HALO, 1), left_block)
-
-    row_base, row_rest = aligned(offsets[0, 0])
-    shift = lax.rem(HALO + FRAME - offsets[0, 1], FRAME)
+def border(right_block, left_block, part):
+    low = lanes(right_block.shape) < HALO
+    if part == 0:
+        return jnp.where(low, right_block, pltpu.roll(left_block, HALO, 1))
+    return jnp.where(low, pltpu.roll(right_block, HALO, 1), left_block)
+
+
+def frame_kernel(obj, top, bottom, left_in, right_in, ext, clear):
+    clear[...] = jnp.zeros(clear.shape, F32)
     for s in range(2):
         for part in range(2):
             q = 2 * s + part
             ext[q, 0:HALO, 0:N] = top[s, part]
             ext[q, HALO : HALO + N, 0:N] = obj[s, part]
             ext[q, HALO + N : FRAME, 0:N] = bottom[s, part]
-            ext[q, 0:HALO, N:FRAME] = border(
-                corner_up[s, 1], corner_up[s, 0], part)
-            ext[q, HALO + N : FRAME, N:FRAME] = border(
-                corner_down[s, 1], corner_down[s, 0], part)
+            ext[q, FRAME : FRAME + 8, :] = jnp.zeros((8, FRAME), F32)
             for rows in chunks(N, HALO):
                 ext[q, HALO + rows.start : HALO + rows.stop, N:FRAME] = border(
                     right_in[s, rows], left_in[s, rows], part)
+
+
+def own_kernel(offsets, ext_in, corner_up, corner_down, probe, kernel, fwd_t, inv_t, left_t,
+               window, psi1, ext, xb, ks, zs):
+    tables = (fwd_t, inv_t, left_t)
+    row_base, row_rest = aligned(offsets[0, 0])
+    shift = lax.rem(HALO + FRAME - offsets[0, 1], FRAME)
+    for s in range(2):
+        for part in range(2):
+            q = 2 * s + part
+            ext[q, 0:HALO, N:FRAME] = border(corner_up[s, 1], corner_up[s, 0], part)
+            ext[q, HALO + N : FRAME, N:FRAME] = border(corner_down[s, 1], corner_down[s, 0], part)
             for rows in chunks(N, 64):
                 block = ext[q, pl.ds(row_base + rows.start, 72), :]
                 block = pltpu.roll(block, lax.rem(72 - row_rest, 72), 0)[:64]
@@ -234,9 +240,9 @@
         enter_mode(m, probe.at[m], psi1.at[m], window, kernel, tables, xb, ks, zs) for m in range(2))])
 
 
-def other_kernel(offsets, obj, probe, near, swapped, kernel, fwd_t, inv_t, left_t, patterns, window, psi1_own,
-                 gradient, row_top, row_bottom, col_left, col_right, corner_left, corner_right,
-                 psi1, far, inten, xb, ks, zs, back, frame):
+def other_kernel(offsets, obj, probe, near, swapped, kernel, fwd_t, inv_t, left_t, patterns, window, psi1_own, clear,
+                 gradient, row_top, row_bottom, col_left, col_right, corner_left, corner_right, frame,
+                 psi1, far, inten, xb, ks, zs, back):
     tables = (fwd_t, inv_t, left_t)
     entering = [(probe.at[0], psi1_own.at[0]), (probe.at[1], psi1_own.at[1]), (near, psi1.at[0]), (swapped, psi1.at[1])]
 
@@ -265,7 +271,6 @@
     low = lanes((HALO, 2 * HALO)) < HALO
     zero = jnp.zeros((HALO, 2 * HALO), F32)
     gap = jnp.zeros((8, FRAME), F32)
-    frame[...] = jnp.zeros(frame.shape, F32)
     for q in range(4):
         s, part = divmod(q, 2)
         for rows in chunks(N, 64):
@@ -313,7 +318,7 @@
         return tuple(a + fold(b) for a, b in zip(carry, terms(q // 2, q % 2, rows)))
 
     zero = tuple(jnp.zeros((8, N // 2), F32) for _ in range(count))
-    put_rows(out, 0, lax.fori_loop(0, 4 * (N // 16), body, zero))
+    put_rows(out, 0, lax.fori_loop(0, 4 * (N // 16), body, zero, unroll=2))
 
 
 def gram_kernel(steps, changes, after, out):
@@ -356,12 +361,11 @@
         return tuple(a + b for a, b in zip(carry, new))
 
     zero = tuple(jnp.zeros((8, N // 2), F32) for _ in range(2 * MEM))
-    sums[...] = jnp.zeros(sums.shape, F32)
     sums[0:SG_ROW, :] = gram[0:SG_ROW, :]
-    put_rows(sums, SG_ROW, lax.fori_loop(0, 4 * (N // 64), body, zero))
+    put_rows(sums, SG_ROW, lax.fori_loop(0, 4 * (N // 64), body, zero, unroll=2))
     totals = jnp.sum(sums[...], axis=1, keepdims=True)
-    row = lax.broadcasted_iota(jnp.int32, (128, 128), 0)
-    spread = jnp.where(row == lanes((128, 128)), totals, 0.0)
+    row = lax.broadcasted_iota(jnp.int32, (ROWS, 128), 0)
+    spread = jnp.where(row == lanes((ROWS, 128)), totals, 0.0)
     total_row = jnp.sum(spread, axis=0, keepdims=True)
     out[...] = jnp.broadcast_to(total_row[None], (128, 1, 128))
     copy.wait()
@@ -369,9 +373,9 @@
 
 def final_kernel(parts, obj, gradient, steps, changes, out, result, sems):
     total = jnp.sum(parts[:, 0, :], axis=0, keepdims=True)
-    row = lax.broadcasted_iota(jnp.int32, (128, 128), 0)
-    diagonal = jnp.where(row == lanes((128, 128)), total, 0.0)
-    splats = jnp.broadcast_to(jnp.sum(diagonal, axis=1, keepdims=True), (128, 128))
+    row = lax.broadcasted_iota(jnp.int32, (ROWS, 128), 0)
+    diagonal = jnp.where(row == lanes((ROWS, 128)), total, 0.0)
+    splats = jnp.broadcast_to(jnp.sum(diagonal, axis=1, keepdims=True), (ROWS, 128))
 
     def value(k):
         return splats[k : k + 1, :]
@@ -396,12 +400,9 @@
             term = term + weights[j] * sy[j, i]
         weights.append(alpha[i] - term * inverse[i])
 
-    def wide(x):
-        return jnp.broadcast_to(jnp.concatenate([x, x], 1), (CHUNK, N))
-
-    scale = wide(scaling)
-    step_weights = [wide(w) for w in weights]
-    change_weights = [wide(scaling * a) for a in alpha]
+    scale = scaling[0, 0]
+    step_weights = [w[0, 0] for w in weights]
+    change_weights = [(scaling * a)[0, 0] for a in alpha]
     copies = []
     for s in range(2):
         for part in range(2):
@@ -415,7 +416,7 @@
                 result[s, part, rows, :] = obj[s, part, rows, :] - acc
                 return carry
 
-            lax.fori_loop(0, N // CHUNK, body, 0)
+            lax.fori_loop(0, N // CHUNK, body, 0, unroll=4)
             copies.append(pltpu.make_async_copy(result.at[s, part], out.at[s, part], sems.at[2 * s + part]))
             copies[-1].start()
     for copy in copies:
@@ -430,7 +431,7 @@
     return pltpu.VMEM(dims, dtype)
 
 
-def call(kernel, outs, scratches, args, smem=0, raw=0, stored=()):
+def call(kernel, outs, scratches, args, smem=0, raw=0, stored=(), alias=None):
     return pl.pallas_call(
         kernel,
         out_shape=outs,
@@ -438,6 +439,7 @@
         out_specs=tuple(ANY if k in stored else VMEM for k in range(len(outs))),
         scratch_shapes=scratches,
         compiler_params=PARAMS,
+        input_output_aliases=alias or {},
     )(*args)
 
 
@@ -479,30 +481,31 @@
     corner_up = shifted(going_down, "ty", 1)
     corner_down = shifted(going_up, "ty", -1)
     kernel = jnp.stack([jnp.cos(phase), jnp.sin(phase)])
-    near, top, bottom, corner_up, corner_down, kernel = lax.optimization_barrier(
-        (near, top, bottom, corner_up, corner_down, kernel))
+    whole = shape(4, FRAME + 8, FRAME)
+    ext, clear = call(frame_kernel, (whole, whole), [], (object_field, top, bottom, left, right))
+    near, ext, clear, corner_up, corner_down, kernel = lax.optimization_barrier(
+        (near, ext, clear, corner_up, corner_down, kernel))
     swapped = lax.ppermute(near, "ty", [(i, i ^ 1) for i in range(rows_axis)])
 
     def work(slots):
         return [scratch(slots, N, 2 * N, dtype=BF16), scratch(slots, 2 * N, 2 * N, dtype=BF16),
                 scratch(slots, N, 2 * N)]
 
-    window, psi1 = call(
+    window, psi1, _ = call(
         own_kernel,
-        (shape(2, N, 2 * N), shape(2, N, 2 * N)),
-        [scratch(4, FRAME + 8, FRAME)] + work(2),
-        (offsets, object_field, top, bottom, left, right, corner_up, corner_down, probe, kernel)
-        + tables,
-        smem=1,
+        (shape(2, N, 2 * N), shape(2, N, 2 * N), whole),
+        work(2),
+        (offsets, ext, corner_up, corner_down, probe, kernel) + tables,
+        smem=1, alias={1: 2},
     )
-    partial, row_top, row_bottom, col_left, col_right, corner_left, corner_right = call(
+    partial, row_top, row_bottom, col_left, col_right, corner_left, corner_right, _ = call(
         other_kernel,
-        (shape(2, 2, N, N), strip, strip, side, side, corner, corner),
+        (shape(2, 2, N, N), strip, strip, side, side, corner, corner, whole),
         [scratch(2, N, 2 * N), scratch(4, N, 2 * N), scratch(N, N)] + work(4)
-        + [scratch(2, 2, N, 2 * N), scratch(4, FRAME + 8, FRAME)],
+        + [scratch(2, 2, N, 2 * N)],
         (offsets, object_field, probe, near, swapped, kernel) + tables
-        + (patterns, window, psi1),
-        smem=1,
+        + (patterns, window, psi1, clear),
+        smem=1, alias={12: 7},
     )
     from_left = shifted(corner_right, "tx", 1)
     from_right = shifted(corner_left, "tx", -1)
@@ -523,7 +526,7 @@
     gradient, sums, stored = call(
         dots_kernel,
         (shape(2, 2, N, N), shape(128, 1, 128), shape(2, 2, N, N)),
-        [scratch(128, 128), pltpu.SemaphoreType.DMA],
+        [scratch(ROWS, 128), pltpu.SemaphoreType.DMA],
         (partial, row_up, row_down, side_left, side_right, past_steps, past_changes,
          gram),
         stored=(2,),

time: 76.3 us -> 75.4 us (0.988)
  waiting for transfers between devices: 7.06 us -> 8.21 us
  local copies, waits for them, and re-layouts: 2.16 us -> 1.26 us
  Pallas kernels: 20.7 us -> 19.8 us
    ppermute x12, waiting for transfers between devices: 6.29 us -> 7.44 us  [shifted(): lax.ppermute(value, axis, [(i, (i + step) % size) for i in range(size)])]
    another operation x1, local copies, waits for them, and re-layouts: 1.85 us -> 0.95 us  [per_device(): kernel = jnp.stack([jnp.cos(phase), jnp.sin(phase)])]
    pallas_call x6 -> x7, Pallas kernels: 20.7 us -> 19.8 us  [call(): pl.pallas_call(kernel, out_shape=outs, in_specs=[SMEM] * smem + [ANY] * r...]
  transfers between devices with their start and end apart: 14 -> 14, of which waited for: 6 -> 6; matrix products, arithmetic and copies ran while one was open for 3% -> 2% of each run, Pallas kernels for 9% -> 8%
where the time goes in v4:
time: 75.4 us; the launch traced here: 75.3 us
  starting transfers between devices  23.3 us (31%)
  blocking collectives  21.5 us (29%)
  Pallas kernels  19.8 us (26%)
  waiting for transfers between devices  8.21 us (11%)
  local copies, waits for them, and re-layouts  1.26 us (2%)
  between operations  1.08 us (1%)
    all_to_all x1, blocking collectives, per_device(): parts = lax.all_to_all(sums, TILES, 0, 0)  21.5 us
    pallas_call x7, Pallas kernels, call(): pl.pallas_call(kernel, out_shape=outs, in_specs=[SMEM] * smem + [ANY] * r...  19.8 us
    ppermute x12, starting transfers between devices, shifted(): lax.ppermute(value, axis, [(i, (i + step) % size) for i in range(size)])  18.8 us
    ppermute x12, waiting for transfers between devices, shifted(): lax.ppermute(value, axis, [(i, (i + step) % size) for i in range(size)])  7.44 us
    ppermute x1, starting transfers between devices, per_device(): lax.ppermute(chosen, ('ty', 'mode'), near_pairs(rows_axis, modes_axis))  2.73 us
    ppermute x1, starting transfers between devices, per_device(): swapped = lax.ppermute(near, 'ty', [(i, i ^ 1) for i in range(rows_axis)])  1.79 us
  transfers between devices with their start and end apart: 14, of which 6 were waited for; matrix products, arithmetic and copies ran while one was open for 2% of the time, Pallas kernels for 8%

profile of v4, /device:TPU:1, one launch (start us, length us, event | category | flops | bytes accessed | tf_op | source)
XLA Modules:
  0.0 75.3 jit_solution(8407298892832944733)
XLA Ops:
  0.7 1.7 %shard_map.113 = (f32[2,2,64,256]{3,2,1,0:T(8,128)S(1)}, f32[2,2,64,256]{3,2,1,0:T(8,128)S(1)}, f32[2,256,128]{2,1,0:T(8,128)S(1)}, f32[2,256,128]{2,1,0:T(8,128)S(1)}, f32[256,512]{1,0:T(8,128)S(1)}) custom-call(s32[1]{0:T(128)} %bitcast.core, f32[2,2,256,256]{3,2,1,0:T(8,128)} %obj.7, f32[2,256,512]{2,1,0:T(8,128)} %probe.5), custom_call_target="tpu_custom_call" | custom-call | tf_op jit(solution)/shard_map/pallas_call | solution.py:435
  2.4 0.0 copy-start.4
  2.4 0.0 copy-start.5
  2.4 0.0 copy-start.6
  2.5 2.5 %collective-permute-start.3 = (f32[2,256,128]{2,1,0:T(8,128)S(1)}, f32[2,256,128]{2,1,0:T(8,128)S(1)}, u32[]{:S(2)}, u32[]{:S(2)}) collective-permute-start(f32[2,256,128]{2,1,0:T(8,128)S(1)} %get-tuple-element.30), channel_id=1, source_target_pairs={{0,2},{2,4},{4,6},{6,8},{8,10},{10,12},{12,14},{14,0},{1,3},{3,5},... | collective-permute-start | bytes 786440 | tf_op jit(solution)/shard_map/ppermute | solution.py:448
  5.0 4.0 %collective-permute-start.4 = (f32[2,256,128]{2,1,0:T(8,128)S(1)}, f32[2,256,128]{2,1,0:T(8,128)S(1)}, u32[]{:S(2)}, u32[]{:S(2)}) collective-permute-start(f32[2,256,128]{2,1,0:T(8,128)S(1)} %get-tuple-element.31), channel_id=1, source_target_pairs={{0,14},{2,0},{4,2},{6,4},{8,6},{10,8},{12,10},{14,12},{1,15},{3,1}... | collective-permute-start | bytes 786440 | tf_op jit(solution)/shard_map/ppermute | solution.py:448
  9.0 2.7 %collective-permute-start = (f32[256,512]{1,0:T(8,128)S(1)}, f32[256,512]{1,0:T(8,128)S(1)}, u32[]{:S(2)}, u32[]{:S(2)}) collective-permute-start(f32[256,512]{1,0:T(8,128)S(1)} %get-tuple-element.27), channel_id=1, source_target_pairs={{0,129},{1,128},{16,145},{17,144},{32,161},{33,160},{48,177},{49,1... | collective-permute-start | bytes 1572872 | tf_op jit(solution)/shard_map/ppermute | solution.py:478
  11.8 2.3 %collective-permute-start.1 = (f32[2,2,64,256]{3,2,1,0:T(8,128)S(1)}, f32[2,2,64,256]{3,2,1,0:T(8,128)S(1)}, u32[]{:S(2)}, u32[]{:S(2)}) collective-permute-start(f32[2,2,64,256]{3,2,1,0:T(8,128)S(1)} %get-tuple-element.28), channel_id=1, source_target_pairs={{0,16},{16,32},{32,48},{48,64},{64,80},{80,96},{96,112},{112,128},... | collective-permute-start | bytes 786440 | tf_op jit(solution)/shard_map/ppermute | solution.py:448
  14.1 0.9 %collective-permute-done.3.left_in = f32[2,256,128]{2,1,0:T(8,128)S(1)} collective-permute-done((f32[2,256,128]{2,1,0:T(8,128)S(1)}, f32[2,256,128]{2,1,0:T(8,128)S(1)}, u32[]{:S(2)}, u32[]{:S(2)}) %collective-permute-start.3) | collective-permute-done | bytes 262176 | tf_op jit(solution)/shard_map/ppermute | solution.py:448
  15.0 2.4 %collective-permute-start.5 = (f32[2,2,64,128]{3,2,1,0:T(8,128)S(1)}, f32[2,2,64,128]{3,2,1,0:T(8,128)S(1)}, u32[]{:S(2)}, u32[]{:S(2)}) collective-permute-start(f32[2,2,64,128]{3,2,1,0:T(8,128)S(1)} %get-tuple-element.53), channel_id=1, source_target_pairs={{0,16},{16,32},{32,48},{48,64},{64,80},{80,96},{96,112},{112,128},... | collective-permute-start | bytes 393224 | tf_op jit(solution)/shard_map/ppermute | solution.py:448
  17.4 0.9 %cosine_bitcast_fusion = (f32[1,256,256]{2,1,0:T(8,128)S(1)}, f32[1,256,256]{2,1,0:T(8,128)S(1)}) fusion(f32[256,256]{1,0:T(8,128)S(1)} %copy-done.9), kind=kLoop, calls=%fused_computation.4 | loop fusion | bytes 786432 | tf_op jit(solution)/shard_map/stack | solution.py:483
  18.4 1.8 %collective-permute-done.2.bottom = f32[2,2,64,256]{3,2,1,0:T(8,128)S(1)} collective-permute-done((f32[2,2,64,256]{3,2,1,0:T(8,128)S(1)}, f32[2,2,64,256]{3,2,1,0:T(8,128)S(1)}, u32[]{:S(2)}, u32[]{:S(2)}) %collective-permute-start.2) | collective-permute-done | bytes 262176 | tf_op jit(solution)/shard_map/ppermute | solution.py:448
  20.2 0.4 shard_map.114
  20.6 1.5 %collective-permute-done.6.corner_down = f32[2,2,64,128]{3,2,1,0:T(8,128)S(1)} collective-permute-done((f32[2,2,64,128]{3,2,1,0:T(8,128)S(1)}, f32[2,2,64,128]{3,2,1,0:T(8,128)S(1)}, u32[]{:S(2)}, u32[]{:S(2)}) %collective-permute-start.6) | collective-permute-done | bytes 131104 | tf_op jit(solution)/shard_map/ppermute | solution.py:448
  22.1 0.8 %collective-permute-done.near = f32[256,512]{1,0:T(8,128)S(1)} collective-permute-done((f32[256,512]{1,0:T(8,128)S(1)}, f32[256,512]{1,0:T(8,128)S(1)}, u32[]{:S(2)}, u32[]{:S(2)}) %collective-permute-start) | collective-permute-done | bytes 524320 | tf_op jit(solution)/shard_map/ppermute | solution.py:478
  22.9 1.8 %collective-permute-start.7 = (f32[256,512]{1,0:T(8,128)S(1)}, f32[256,512]{1,0:T(8,128)S(1)}, u32[]{:S(2)}, u32[]{:S(2)}) collective-permute-start(f32[256,512]{1,0:T(8,128)S(1)} %collective-permute-done.near), channel_id=1, source_target_pairs={{0,16},{16,0},{32,48},{48,32},{64,80},{80,64},{96,112},{112,96},{1... | collective-permute-start | bytes 1572872 | tf_op jit(solution)/shard_map/ppermute | solution.py:488
  24.7 2.3 %shard_map.115 = (f32[2,256,512]{2,1,0:T(8,128)S(1)}, f32[2,256,512]{2,1,0:T(8,128)S(1)}, f32[4,392,384]{2,1,0:T(8,128)S(1)}) custom-call(s32[1,2]{1,0:T(1,128)S(1)} %copy-done.8, f32[4,392,384]{2,1,0:T(8,128)S(1)} %get-tuple-element.36.ext_in, f32[2,2,64,128]{3,2,1,0:T(8,128)S(1)} %collective-permute-done.5.corner_up, ...), custom_call_target="tpu_custom_call", output_to_operand_aliasing={{2}: (1, {})} | custom-call | tf_op jit(solution)/shard_map/pallas_call | solution.py:435
  27.1 8.0 %shard_map.116 = (f32[2,2,256,256]{3,2,1,0:T(8,128)S(1)}, f32[2,2,64,256]{3,2,1,0:T(8,128)S(1)}, f32[2,2,64,256]{3,2,1,0:T(8,128)S(1)}, f32[2,256,128]{2,1,0:T(8...) custom-call(s32[1,2]{1,0:T(1,128)S(1)} %copy-done.8, ...), custom_call_target="tpu_custom_call", output_to_operand_aliasing={{7}: (12, {})} | custom-call | tf_op jit(solution)/shard_map/pallas_call | solution.py:435
  35.1 0.1 collective-permute-start.8
  35.2 0.1 pad.7.clone
  35.3 2.7 %collective-permute-start.9 = (f32[2,2,64,128]{3,2,1,0:T(8,128)S(1)}, f32[2,2,64,128]{3,2,1,0:T(8,128)S(1)}, u32[]{:S(2)}, u32[]{:S(2)}) collective-permute-start(f32[2,2,64,128]{3,2,1,0:T(8,128)S(1)} %get-tuple-element.45), channel_id=1, source_target_pairs={{0,14},{2,0},{4,2},{6,4},{8,6},{10,8},{12,10},{14,12},{1,15},{3,1}... | collective-permute-start | bytes 393224 | tf_op jit(solution)/shard_map/ppermute | solution.py:448
  37.9 2.7 %collective-permute-start.13 = (f32[2,256,128]{2,1,0:T(8,128)S(1)}, f32[2,256,128]{2,1,0:T(8,128)S(1)}, u32[]{:S(2)}, u32[]{:S(2)}) collective-permute-start(f32[2,256,128]{2,1,0:T(8,128)S(1)} %get-tuple-element.48), channel_id=1, source_target_pairs={{0,14},{2,0},{4,2},{6,4},{8,6},{10,8},{12,10},{14,12},{1,15},{3,1}... | collective-permute-start | bytes 786440 | tf_op jit(solution)/shard_map/ppermute | solution.py:448
  40.6 0.8 %collective-permute-done.8 = f32[2,2,64,128]{3,2,1,0:T(8,128)S(1)} collective-permute-done((f32[2,2,64,128]{3,2,1,0:T(8,128)S(1)}, f32[2,2,64,128]{3,2,1,0:T(8,128)S(1)}, u32[]{:S(2)}, u32[]{:S(2)}) %collective-permute-start.8) | collective-permute-done | bytes 131104 | tf_op jit(solution)/shard_map/ppermute | solution.py:448
  41.5 0.1 fusion
  41.6 0.1 fusion.1
  41.7 0.1 maximum_add_fusion.1
  41.8 2.0 %collective-permute-start.10 = (f32[2,2,64,256]{3,2,1,0:T(8,128)S(1)}, f32[2,2,64,256]{3,2,1,0:T(8,128)S(1)}, u32[]{:S(2)}, u32[]{:S(2)}) collective-permute-start(f32[2,2,64,256]{3,2,1,0:T(8,128)S(1)} %get-tuple-element.65), channel_id=1, source_target_pairs={{0,16},{16,32},{32,48},{48,64},{64,80},{80,96},{96,112},{112,128},... | collective-permute-start | bytes 786440 | tf_op jit(solution)/shard_map/ppermute | solution.py:448
  43.9 3.6 %shard_map.117.gram = f32[32,128]{1,0:T(8,128)S(1)} custom-call(bf16[5,2,2,256,256]{4,3,2,1,0:T(8,128)(2,1)S(1)} %copy-done, bf16[5,2,2,256,256]{4,3,2,1,0:T(8,128)(2,1)S(1)} %copy-done.1, f32[2,2,64,256]{3,2,1,0:T(8,128)S(1)} %get-tuple-element.64.after), custom_call_target="tpu_custom_call" | custom-call | tf_op jit(solution)/shard_map/pallas_call | solution.py:435
  47.5 2.4 %collective-permute-done.11.row_down = f32[2,2,64,256]{3,2,1,0:T(8,128)S(1)} collective-permute-done((f32[2,2,64,256]{3,2,1,0:T(8,128)S(1)}, f32[2,2,64,256]{3,2,1,0:T(8,128)S(1)}, u32[]{:S(2)}, u32[]{:S(2)}) %collective-permute-start.11) | collective-permute-done | bytes 262176 | tf_op jit(solution)/shard_map/ppermute | solution.py:448
  49.9 1.5 %shard_map.118 = (f32[2,2,256,256]{3,2,1,0:T(8,128)S(1)}, f32[128,1,128]{2,1,0:T(1,128)S(1)}, f32[2,2,256,256]{3,2,1,0:T(8,128)}) custom-call(f32[2,2,256,256]{3,2,1,0:T(8,128)S(1)} %get-tuple-element.42.gradient_in, f32[2,2,64,256]{3,2,1,0:T(8,128)S(1)} %collective-permute-done.10.row_up, f32[2,2,64,256]{3,2,1,0:T(8,128)S(1)} %collective-permute-done.11.row_down, ...), custom_call_target="tpu_custom_call" | custom-call | tf_op jit(solution)/shard_map/pallas_call | solution.py:435
  51.5 21.5 %all_to_all.5.parts = f32[128,1,128]{2,1,0:T(1,128)S(1)} all-to-all(f32[128,1,128]{2,1,0:T(1,128)S(1)} %get-tuple-element.49), channel_id=1, replica_groups=mesh['ty'=16,'tx'=8,'mode'=2] {'ty','tx'}, dimensions={0} | all-to-all | bytes 131072 | tf_op jit(solution)/shard_map/all_to_all | solution.py:534
  72.9 2.1 %shard_map.119 = f32[2,2,256,256]{3,2,1,0:T(8,128)} custom-call(f32[128,1,128]{2,1,0:T(1,128)S(1)} %all_to_all.5.parts, f32[2,2,256,256]{3,2,1,0:T(8,128)S(1)} %copy-done.2, f32[2,2,256,256]{3,2,1,0:T(8,128)S(1)} %get-tuple-element.50.gradient, bf16[5,2,2,256,256]{4,3,2,1,0:T(8,128)(2,1)S(1)} %copy-done, bf16[5,2,2,256,256]{4,3,2,1,0:T(8,128)(2,1)S(1)} %copy-done.1), custom_call_target="tpu_custom_call" | custom-call | tf_op jit(solution)/shard_map/pallas_call | solution.py:435
  (32 shorter events, 0.1 us)
Async XLA Ops:
  0.6 19.6 %copy-start.2 = (f32[2,2,256,256]{3,2,1,0:T(8,128)S(1)}, f32[2,2,256,256]{3,2,1,0:T(8,128)}, u32[]{:S(2)}) copy-start(f32[2,2,256,256]{3,2,1,0:T(8,128)} %obj.7) | copy-start | bytes 3145732
  0.6 16.8 %copy-start.9 = (f32[256,256]{1,0:T(8,128)S(1)}, f32[256,256]{1,0:T(8,128)}, u32[]{:S(2)}) copy-start(f32[256,256]{1,0:T(8,128)} %param.14) | copy-start | bytes 786436
  2.4 22.3 %copy-start.3 = (f32[2,256,512]{2,1,0:T(8,128)S(1)}, f32[2,256,512]{2,1,0:T(8,128)}, u32[]{:S(2)}) copy-start(f32[2,256,512]{2,1,0:T(8,128)} %probe.5) | copy-start | bytes 3145732
  2.4 22.2 %copy-start.4 = (bf16[512,512]{1,0:T(8,128)(2,1)S(1)}, bf16[512,512]{1,0:T(8,128)(2,1)}, u32[]{:S(2)}) copy-start(bf16[512,512]{1,0:T(8,128)(2,1)} %constant.15.clone.fwd_t) | copy-start | bytes 1572868
  2.4 22.2 %copy-start.5 = (bf16[512,512]{1,0:T(8,128)(2,1)S(1)}, bf16[512,512]{1,0:T(8,128)(2,1)}, u32[]{:S(2)}) copy-start(bf16[512,512]{1,0:T(8,128)(2,1)} %constant.16.clone.inv_t) | copy-start | bytes 1572868
  2.4 22.2 %copy-start.6 = (bf16[256,512]{1,0:T(8,128)(2,1)S(1)}, bf16[256,512]{1,0:T(8,128)(2,1)}, u32[]{:S(2)}) copy-start(bf16[256,512]{1,0:T(8,128)(2,1)} %constant.17.clone.left_t) | copy-start | bytes 786436
  2.5 22.2 %copy-start.8 = (s32[1,2]{1,0:T(1,128)S(1)}, s32[1,2]{1,0:T(1,128)}, u32[]{:S(2)}) copy-start(s32[1,2]{1,0:T(1,128)} %offsets.3) | copy-start | bytes 28
  2.5 12.5 %collective-permute-start.3 = (f32[2,256,128]{2,1,0:T(8,128)S(1)}, f32[2,256,128]{2,1,0:T(8,128)S(1)}, u32[]{:S(2)}, u32[]{:S(2)}) collective-permute-start(f32[2,256,128]{2,1,0:T(8,128)S(1)} %get-tuple-element.30), channel_id=1, source_target_pairs={{0,2},{2,4},{4,6},{6,8},{8,10},{10,12},{12,14},{14,0},{1,3},{3,5},... | collective-permute-start | bytes 786440 | tf_op jit(solution)/shard_map/ppermute | solution.py:448
  5.0 10.0 %collective-permute-start.4 = (f32[2,256,128]{2,1,0:T(8,128)S(1)}, f32[2,256,128]{2,1,0:T(8,128)S(1)}, u32[]{:S(2)}, u32[]{:S(2)}) collective-permute-start(f32[2,256,128]{2,1,0:T(8,128)S(1)} %get-tuple-element.31), channel_id=1, source_target_pairs={{0,14},{2,0},{4,2},{6,4},{8,6},{10,8},{12,10},{14,12},{1,15},{3,1}... | collective-permute-start | bytes 786440 | tf_op jit(solution)/shard_map/ppermute | solution.py:448
  9.0 13.8 %collective-permute-start = (f32[256,512]{1,0:T(8,128)S(1)}, f32[256,512]{1,0:T(8,128)S(1)}, u32[]{:S(2)}, u32[]{:S(2)}) collective-permute-start(f32[256,512]{1,0:T(8,128)S(1)} %get-tuple-element.27), channel_id=1, source_target_pairs={{0,129},{1,128},{16,145},{17,144},{32,161},{33,160},{48,177},{49,1... | collective-permute-start | bytes 1572872 | tf_op jit(solution)/shard_map/ppermute | solution.py:478
  11.8 6.6 %collective-permute-start.1 = (f32[2,2,64,256]{3,2,1,0:T(8,128)S(1)}, f32[2,2,64,256]{3,2,1,0:T(8,128)S(1)}, u32[]{:S(2)}, u32[]{:S(2)}) collective-permute-start(f32[2,2,64,256]{3,2,1,0:T(8,128)S(1)} %get-tuple-element.28), channel_id=1, source_target_pairs={{0,16},{16,32},{32,48},{48,64},{64,80},{80,96},{96,112},{112,128},... | collective-permute-start | bytes 786440 | tf_op jit(solution)/shard_map/ppermute | solution.py:448
  14.1 6.1 %collective-permute-start.2 = (f32[2,2,64,256]{3,2,1,0:T(8,128)S(1)}, f32[2,2,64,256]{3,2,1,0:T(8,128)S(1)}, u32[]{:S(2)}, u32[]{:S(2)}) collective-permute-start(f32[2,2,64,256]{3,2,1,0:T(8,128)S(1)} %get-tuple-element.29), channel_id=1, source_target_pairs={{0,240},{16,0},{32,16},{48,32},{64,48},{80,64},{96,80},{112,96},{1... | collective-permute-start | bytes 786440 | tf_op jit(solution)/shard_map/ppermute | solution.py:448
  15.0 5.6 %collective-permute-start.5 = (f32[2,2,64,128]{3,2,1,0:T(8,128)S(1)}, f32[2,2,64,128]{3,2,1,0:T(8,128)S(1)}, u32[]{:S(2)}, u32[]{:S(2)}) collective-permute-start(f32[2,2,64,128]{3,2,1,0:T(8,128)S(1)} %get-tuple-element.53), channel_id=1, source_target_pairs={{0,16},{16,32},{32,48},{48,64},{64,80},{80,96},{96,112},{112,128},... | collective-permute-start | bytes 393224 | tf_op jit(solution)/shard_map/ppermute | solution.py:448
  17.4 4.7 %collective-permute-start.6 = (f32[2,2,64,128]{3,2,1,0:T(8,128)S(1)}, f32[2,2,64,128]{3,2,1,0:T(8,128)S(1)}, u32[]{:S(2)}, u32[]{:S(2)}) collective-permute-start(f32[2,2,64,128]{3,2,1,0:T(8,128)S(1)} %get-tuple-element.52), channel_id=1, source_target_pairs={{0,240},{16,0},{32,16},{48,32},{64,48},{80,64},{96,80},{112,96},{1... | collective-permute-start | bytes 393224 | tf_op jit(solution)/shard_map/ppermute | solution.py:448
  22.9 4.2 %copy-start.7 = (f32[1,256,256]{2,1,0:T(8,128)S(1)}, f32[1,256,256]{2,1,0:T(8,128)}, u32[]{:S(2)}) copy-start(f32[1,256,256]{2,1,0:T(8,128)} %patterns.1) | copy-start | bytes 786436
  22.9 4.2 %collective-permute-start.7 = (f32[256,512]{1,0:T(8,128)S(1)}, f32[256,512]{1,0:T(8,128)S(1)}, u32[]{:S(2)}, u32[]{:S(2)}) collective-permute-start(f32[256,512]{1,0:T(8,128)S(1)} %collective-permute-done.near), channel_id=1, source_target_pairs={{0,16},{16,0},{32,48},{48,32},{64,80},{80,64},{96,112},{112,96},{1... | collective-permute-start | bytes 1572872 | tf_op jit(solution)/shard_map/ppermute | solution.py:488
  27.0 16.8 %copy-start.1 = (bf16[5,2,2,256,256]{4,3,2,1,0:T(8,128)(2,1)S(1)}, bf16[5,2,2,256,256]{4,3,2,1,0:T(8,128)(2,1)}, u32[]{:S(2)}) copy-start(bf16[5,2,2,256,256]{4,3,2,1,0:T(8,128)(2,1)} %changes.5) | copy-start | bytes 7864324
  35.1 8.8 %copy-start = (bf16[5,2,2,256,256]{4,3,2,1,0:T(8,128)(2,1)S(1)}, bf16[5,2,2,256,256]{4,3,2,1,0:T(8,128)(2,1)}, u32[]{:S(2)}) copy-start(bf16[5,2,2,256,256]{4,3,2,1,0:T(8,128)(2,1)} %steps.5) | copy-start | bytes 7864324
  35.1 6.4 %collective-permute-start.8 = (f32[2,2,64,128]{3,2,1,0:T(8,128)S(1)}, f32[2,2,64,128]{3,2,1,0:T(8,128)S(1)}, u32[]{:S(2)}, u32[]{:S(2)}) collective-permute-start(f32[2,2,64,128]{3,2,1,0:T(8,128)S(1)} %get-tuple-element.44), channel_id=1, source_target_pairs={{0,2},{2,4},{4,6},{6,8},{8,10},{10,12},{12,14},{14,0},{1,3},{3,5},... | collective-permute-start | bytes 393224 | tf_op jit(solution)/shard_map/ppermute | solution.py:448
  35.3 6.3 %collective-permute-start.9 = (f32[2,2,64,128]{3,2,1,0:T(8,128)S(1)}, f32[2,2,64,128]{3,2,1,0:T(8,128)S(1)}, u32[]{:S(2)}, u32[]{:S(2)}) collective-permute-start(f32[2,2,64,128]{3,2,1,0:T(8,128)S(1)} %get-tuple-element.45), channel_id=1, source_target_pairs={{0,14},{2,0},{4,2},{6,4},{8,6},{10,8},{12,10},{14,12},{1,15},{3,1}... | collective-permute-start | bytes 393224 | tf_op jit(solution)/shard_map/ppermute | solution.py:448
  37.9 9.5 %collective-permute-start.12 = (f32[2,256,128]{2,1,0:T(8,128)S(1)}, f32[2,256,128]{2,1,0:T(8,128)S(1)}, u32[]{:S(2)}, u32[]{:S(2)}) collective-permute-start(f32[2,256,128]{2,1,0:T(8,128)S(1)} %get-tuple-element.47), channel_id=1, source_target_pairs={{0,2},{2,4},{4,6},{6,8},{8,10},{10,12},{12,14},{14,0},{1,3},{3,5},... | collective-permute-start | bytes 786440 | tf_op jit(solution)/shard_map/ppermute | solution.py:448
  37.9 9.6 %collective-permute-start.13 = (f32[2,256,128]{2,1,0:T(8,128)S(1)}, f32[2,256,128]{2,1,0:T(8,128)S(1)}, u32[]{:S(2)}, u32[]{:S(2)}) collective-permute-start(f32[2,256,128]{2,1,0:T(8,128)S(1)} %get-tuple-element.48), channel_id=1, source_target_pairs={{0,14},{2,0},{4,2},{6,4},{8,6},{10,8},{12,10},{14,12},{1,15},{3,1}... | collective-permute-start | bytes 786440 | tf_op jit(solution)/shard_map/ppermute | solution.py:448
  41.8 5.7 %collective-permute-start.10 = (f32[2,2,64,256]{3,2,1,0:T(8,128)S(1)}, f32[2,2,64,256]{3,2,1,0:T(8,128)S(1)}, u32[]{:S(2)}, u32[]{:S(2)}) collective-permute-start(f32[2,2,64,256]{3,2,1,0:T(8,128)S(1)} %get-tuple-element.65), channel_id=1, source_target_pairs={{0,16},{16,32},{32,48},{48,64},{64,80},{80,96},{96,112},{112,128},... | collective-permute-start | bytes 786440 | tf_op jit(solution)/shard_map/ppermute | solution.py:448
  43.8 6.1 %collective-permute-start.11 = (f32[2,2,64,256]{3,2,1,0:T(8,128)S(1)}, f32[2,2,64,256]{3,2,1,0:T(8,128)S(1)}, u32[]{:S(2)}, u32[]{:S(2)}) collective-permute-start(f32[2,2,64,256]{3,2,1,0:T(8,128)S(1)} %get-tuple-element.64.after), channel_id=1, source_target_pairs={{0,240},{16,0},{32,16},{48,32},{64,48},{80,64},{96,80},{112,96},{1... | collective-permute-start | bytes 786440 | tf_op jit(solution)/shard_map/ppermute | solution.py:448

commit v5 on v4

--- a/solution.py
+++ b/solution.py
@@ -135,7 +135,7 @@
             yield
 
 
-def backward_mode(slot, psi0, psi1, far, scale, window, kernel, tables, pieces, xb, ks, zs):
+def backward_mode(slot, psi0, psi1, window, kernel, tables, pieces, xb, ks, zs):
     forward, inverse, left = tables
     pair, m = divmod(slot, 2)
     k = slot
@@ -146,12 +146,6 @@
         pieces[pair, s, rows, 0:N] = re
         pieces[pair, s, rows, N : 2 * N] = im
 
-    for rows in chunks():
-        factor = scale[rows, :]
-        re, im = (far[rows, 0:N], far[rows, N : 2 * N])
-        xb[k, rows, 0:N] = (factor * re).astype(BF16)
-        xb[k, rows, N : 2 * N] = (factor * im).astype(BF16)
-    yield
     first_pass(xb, ks, k, inverse, True)
     yield
     zs[k] = second_pass(ks, k, left)
@@ -242,7 +236,7 @@
 
 def other_kernel(offsets, obj, probe, near, swapped, kernel, fwd_t, inv_t, left_t, patterns, window, psi1_own, clear,
                  gradient, row_top, row_bottom, col_left, col_right, corner_left, corner_right, frame,
-                 psi1, far, inten, xb, ks, zs, back):
+                 psi1, far, xb, ks, zs, back):
     tables = (fwd_t, inv_t, left_t)
     entering = [(probe.at[0], psi1_own.at[0]), (probe.at[1], psi1_own.at[1]), (near, psi1.at[0]), (swapped, psi1.at[1])]
 
@@ -254,19 +248,19 @@
             chain(enter_mode(k, *entering[k], window, kernel, tables, xb, ks, zs), leaving(k)) for k in (2, 3)),
         together(leaving(k) for k in (0, 1)),
     ])
-    for rows in chunks():
-        terms = []
-        for k in range(4):
-            re, im = halves(far, k, rows)
-            terms.append(re * re + im * im)
-        inten[rows, :] = (terms[0] + terms[1]) + (terms[2] + terms[3])
-    for rows in chunks():
-        inten[rows, :] = (inten[rows, :] * (1.0 / MODES) - patterns[0, rows, :]) * (2.0 / MODES)
+    for rows in chunks(N, 16):
+        waves = [halves(far, k, rows) for k in range(4)]
+        terms = [re * re + im * im for re, im in waves]
+        total = (terms[0] + terms[1]) + (terms[2] + terms[3])
+        scale = (total * (1.0 / MODES) - patterns[0, rows, :]) * (2.0 / MODES)
+        for k, (re, im) in enumerate(waves):
+            xb[k, rows, 0:N] = (scale * re).astype(BF16)
+            xb[k, rows, N : 2 * N] = (scale * im).astype(BF16)
     row_base, row_rest = aligned(offsets[0, 0])
     shift = lax.rem(HALO + N + offsets[0, 1], FRAME)
     interleave(
         together(
-            backward_mode(k, *entering[k], far.at[k], inten, window, kernel, tables, back, xb, ks, zs) for k in pair)
+            backward_mode(k, *entering[k], window, kernel, tables, back, xb, ks, zs) for k in pair)
         for pair in ((0, 1), (2, 3)))
     low = lanes((HALO, 2 * HALO)) < HALO
     zero = jnp.zeros((HALO, 2 * HALO), F32)
@@ -318,7 +312,7 @@
         return tuple(a + fold(b) for a, b in zip(carry, terms(q // 2, q % 2, rows)))
 
     zero = tuple(jnp.zeros((8, N // 2), F32) for _ in range(count))
-    put_rows(out, 0, lax.fori_loop(0, 4 * (N // 16), body, zero, unroll=2))
+    put_rows(out, 0, lax.fori_loop(0, 4 * (N // 16), body, zero, unroll=4))
 
 
 def gram_kernel(steps, changes, after, out):
@@ -362,7 +356,7 @@
 
     zero = tuple(jnp.zeros((8, N // 2), F32) for _ in range(2 * MEM))
     sums[0:SG_ROW, :] = gram[0:SG_ROW, :]
-    put_rows(sums, SG_ROW, lax.fori_loop(0, 4 * (N // 64), body, zero, unroll=2))
+    put_rows(sums, SG_ROW, lax.fori_loop(0, 4 * (N // 64), body, zero, unroll=4))
     totals = jnp.sum(sums[...], axis=1, keepdims=True)
     row = lax.broadcasted_iota(jnp.int32, (ROWS, 128), 0)
     spread = jnp.where(row == lanes((ROWS, 128)), totals, 0.0)
@@ -416,7 +410,7 @@
                 result[s, part, rows, :] = obj[s, part, rows, :] - acc
                 return carry
 
-            lax.fori_loop(0, N // CHUNK, body, 0, unroll=4)
+            lax.fori_loop(0, N // CHUNK, body, 0, unroll=8)
             copies.append(pltpu.make_async_copy(result.at[s, part], out.at[s, part], sems.at[2 * s + part]))
             copies[-1].start()
     for copy in copies:
@@ -501,7 +495,7 @@
     partial, row_top, row_bottom, col_left, col_right, corner_left, corner_right, _ = call(
         other_kernel,
         (shape(2, 2, N, N), strip, strip, side, side, corner, corner, whole),
-        [scratch(2, N, 2 * N), scratch(4, N, 2 * N), scratch(N, N)] + work(4)
+        [scratch(2, N, 2 * N), scratch(4, N, 2 * N)] + work(4)
         + [scratch(2, 2, N, 2 * N)],
         (offsets, object_field, probe, near, swapped, kernel) + tables
         + (patterns, window, psi1, clear),

time: 75.4 us -> 75.3 us (level)
  no operation moved by 1% of the time
where the time goes in v5:
time: 75.3 us; the launch traced here: 75.2 us
  starting transfers between devices  23.2 us (31%)
  blocking collectives  21.5 us (29%)
  Pallas kernels  19.3 us (26%)
  waiting for transfers between devices  8.59 us (11%)
  local copies, waits for them, and re-layouts  1.26 us (2%)
  between operations  1.07 us (1%)
    all_to_all x1, blocking collectives, per_device(): parts = lax.all_to_all(sums, TILES, 0, 0)  21.5 us
    pallas_call x7, Pallas kernels, call(): pl.pallas_call(kernel, out_shape=outs, in_specs=[SMEM] * smem + [ANY] * r...  19.3 us
    ppermute x12, starting transfers between devices, shifted(): lax.ppermute(value, axis, [(i, (i + step) % size) for i in range(size)])  18.7 us
    ppermute x12, waiting for transfers between devices, shifted(): lax.ppermute(value, axis, [(i, (i + step) % size) for i in range(size)])  7.82 us
    ppermute x1, starting transfers between devices, per_device(): lax.ppermute(chosen, ('ty', 'mode'), near_pairs(rows_axis, modes_axis))  2.73 us
    ppermute x1, starting transfers between devices, per_device(): swapped = lax.ppermute(near, 'ty', [(i, i ^ 1) for i in range(rows_axis)])  1.79 us
  transfers between devices with their start and end apart: 14, of which 6 were waited for; matrix products, arithmetic and copies ran while one was open for 2% of the time, Pallas kernels for 8%

profile of v5, /device:TPU:1, one launch (start us, length us, event | category | flops | bytes accessed | tf_op | source)
XLA Modules:
  0.0 75.2 jit_solution(12351842430888269864)
XLA Ops:
  0.7 1.7 %shard_map.113 = (f32[2,2,64,256]{3,2,1,0:T(8,128)S(1)}, f32[2,2,64,256]{3,2,1,0:T(8,128)S(1)}, f32[2,256,128]{2,1,0:T(8,128)S(1)}, f32[2,256,128]{2,1,0:T(8,128)S(1)}, f32[256,512]{1,0:T(8,128)S(1)}) custom-call(s32[1]{0:T(128)} %bitcast.core, f32[2,2,256,256]{3,2,1,0:T(8,128)} %obj.7, f32[2,256,512]{2,1,0:T(8,128)} %probe.5), custom_call_target="tpu_custom_call" | custom-call | tf_op jit(solution)/shard_map/pallas_call | solution.py:429
  2.4 0.0 copy-start.5
  2.4 0.0 copy-start.6
  2.5 2.5 %collective-permute-start.3 = (f32[2,256,128]{2,1,0:T(8,128)S(1)}, f32[2,256,128]{2,1,0:T(8,128)S(1)}, u32[]{:S(2)}, u32[]{:S(2)}) collective-permute-start(f32[2,256,128]{2,1,0:T(8,128)S(1)} %get-tuple-element.30), channel_id=1, source_target_pairs={{0,2},{2,4},{4,6},{6,8},{8,10},{10,12},{12,14},{14,0},{1,3},{3,5},... | collective-permute-start | bytes 786440 | tf_op jit(solution)/shard_map/ppermute | solution.py:442
  5.0 4.0 %collective-permute-start.4 = (f32[2,256,128]{2,1,0:T(8,128)S(1)}, f32[2,256,128]{2,1,0:T(8,128)S(1)}, u32[]{:S(2)}, u32[]{:S(2)}) collective-permute-start(f32[2,256,128]{2,1,0:T(8,128)S(1)} %get-tuple-element.31), channel_id=1, source_target_pairs={{0,14},{2,0},{4,2},{6,4},{8,6},{10,8},{12,10},{14,12},{1,15},{3,1}... | collective-permute-start | bytes 786440 | tf_op jit(solution)/shard_map/ppermute | solution.py:442
  9.0 2.7 %collective-permute-start = (f32[256,512]{1,0:T(8,128)S(1)}, f32[256,512]{1,0:T(8,128)S(1)}, u32[]{:S(2)}, u32[]{:S(2)}) collective-permute-start(f32[256,512]{1,0:T(8,128)S(1)} %get-tuple-element.27), channel_id=1, source_target_pairs={{0,129},{1,128},{16,145},{17,144},{32,161},{33,160},{48,177},{49,1... | collective-permute-start | bytes 1572872 | tf_op jit(solution)/shard_map/ppermute | solution.py:472
  11.8 2.3 %collective-permute-start.1 = (f32[2,2,64,256]{3,2,1,0:T(8,128)S(1)}, f32[2,2,64,256]{3,2,1,0:T(8,128)S(1)}, u32[]{:S(2)}, u32[]{:S(2)}) collective-permute-start(f32[2,2,64,256]{3,2,1,0:T(8,128)S(1)} %get-tuple-element.28), channel_id=1, source_target_pairs={{0,16},{16,32},{32,48},{48,64},{64,80},{80,96},{96,112},{112,128},... | collective-permute-start | bytes 786440 | tf_op jit(solution)/shard_map/ppermute | solution.py:442
  14.1 0.9 %collective-permute-done.3.left_in = f32[2,256,128]{2,1,0:T(8,128)S(1)} collective-permute-done((f32[2,256,128]{2,1,0:T(8,128)S(1)}, f32[2,256,128]{2,1,0:T(8,128)S(1)}, u32[]{:S(2)}, u32[]{:S(2)}) %collective-permute-start.3) | collective-permute-done | bytes 262176 | tf_op jit(solution)/shard_map/ppermute | solution.py:442
  15.0 2.4 %collective-permute-start.5 = (f32[2,2,64,128]{3,2,1,0:T(8,128)S(1)}, f32[2,2,64,128]{3,2,1,0:T(8,128)S(1)}, u32[]{:S(2)}, u32[]{:S(2)}) collective-permute-start(f32[2,2,64,128]{3,2,1,0:T(8,128)S(1)} %get-tuple-element.53), channel_id=1, source_target_pairs={{0,16},{16,32},{32,48},{48,64},{64,80},{80,96},{96,112},{112,128},... | collective-permute-start | bytes 393224 | tf_op jit(solution)/shard_map/ppermute | solution.py:442
  17.4 0.9 %cosine_bitcast_fusion = (f32[1,256,256]{2,1,0:T(8,128)S(1)}, f32[1,256,256]{2,1,0:T(8,128)S(1)}) fusion(f32[256,256]{1,0:T(8,128)S(1)} %copy-done.9), kind=kLoop, calls=%fused_computation.4 | loop fusion | bytes 786432 | tf_op jit(solution)/shard_map/stack | solution.py:477
  18.4 1.8 %collective-permute-done.2.bottom = f32[2,2,64,256]{3,2,1,0:T(8,128)S(1)} collective-permute-done((f32[2,2,64,256]{3,2,1,0:T(8,128)S(1)}, f32[2,2,64,256]{3,2,1,0:T(8,128)S(1)}, u32[]{:S(2)}, u32[]{:S(2)}) %collective-permute-start.2) | collective-permute-done | bytes 262176 | tf_op jit(solution)/shard_map/ppermute | solution.py:442
  20.2 0.4 shard_map.114
  20.6 1.5 %collective-permute-done.6.corner_down = f32[2,2,64,128]{3,2,1,0:T(8,128)S(1)} collective-permute-done((f32[2,2,64,128]{3,2,1,0:T(8,128)S(1)}, f32[2,2,64,128]{3,2,1,0:T(8,128)S(1)}, u32[]{:S(2)}, u32[]{:S(2)}) %collective-permute-start.6) | collective-permute-done | bytes 131104 | tf_op jit(solution)/shard_map/ppermute | solution.py:442
  22.1 0.8 %collective-permute-done.near = f32[256,512]{1,0:T(8,128)S(1)} collective-permute-done((f32[256,512]{1,0:T(8,128)S(1)}, f32[256,512]{1,0:T(8,128)S(1)}, u32[]{:S(2)}, u32[]{:S(2)}) %collective-permute-start) | collective-permute-done | bytes 524320 | tf_op jit(solution)/shard_map/ppermute | solution.py:472
  22.9 1.8 %collective-permute-start.7 = (f32[256,512]{1,0:T(8,128)S(1)}, f32[256,512]{1,0:T(8,128)S(1)}, u32[]{:S(2)}, u32[]{:S(2)}) collective-permute-start(f32[256,512]{1,0:T(8,128)S(1)} %collective-permute-done.near), channel_id=1, source_target_pairs={{0,16},{16,0},{32,48},{48,32},{64,80},{80,64},{96,112},{112,96},{1... | collective-permute-start | bytes 1572872 | tf_op jit(solution)/shard_map/ppermute | solution.py:482
  24.7 2.3 %shard_map.115 = (f32[2,256,512]{2,1,0:T(8,128)S(1)}, f32[2,256,512]{2,1,0:T(8,128)S(1)}, f32[4,392,384]{2,1,0:T(8,128)S(1)}) custom-call(s32[1,2]{1,0:T(1,128)S(1)} %copy-done.8, f32[4,392,384]{2,1,0:T(8,128)S(1)} %get-tuple-element.36.ext_in, f32[2,2,64,128]{3,2,1,0:T(8,128)S(1)} %collective-permute-done.5.corner_up, ...), custom_call_target="tpu_custom_call", output_to_operand_aliasing={{2}: (1, {})} | custom-call | tf_op jit(solution)/shard_map/pallas_call | solution.py:429
  27.1 8.0 %shard_map.116 = (f32[2,2,256,256]{3,2,1,0:T(8,128)S(1)}, f32[2,2,64,256]{3,2,1,0:T(8,128)S(1)}, f32[2,2,64,256]{3,2,1,0:T(8,128)S(1)}, f32[2,256,128]{2,1,0:T(8...) custom-call(s32[1,2]{1,0:T(1,128)S(1)} %copy-done.8, ...), custom_call_target="tpu_custom_call", output_to_operand_aliasing={{7}: (12, {})} | custom-call | tf_op jit(solution)/shard_map/pallas_call | solution.py:429
  35.1 0.1 collective-permute-start.8
  35.2 0.1 pad.7.clone
  35.3 2.7 %collective-permute-start.9 = (f32[2,2,64,128]{3,2,1,0:T(8,128)S(1)}, f32[2,2,64,128]{3,2,1,0:T(8,128)S(1)}, u32[]{:S(2)}, u32[]{:S(2)}) collective-permute-start(f32[2,2,64,128]{3,2,1,0:T(8,128)S(1)} %get-tuple-element.45), channel_id=1, source_target_pairs={{0,14},{2,0},{4,2},{6,4},{8,6},{10,8},{12,10},{14,12},{1,15},{3,1}... | collective-permute-start | bytes 393224 | tf_op jit(solution)/shard_map/ppermute | solution.py:442
  37.9 2.7 %collective-permute-start.13 = (f32[2,256,128]{2,1,0:T(8,128)S(1)}, f32[2,256,128]{2,1,0:T(8,128)S(1)}, u32[]{:S(2)}, u32[]{:S(2)}) collective-permute-start(f32[2,256,128]{2,1,0:T(8,128)S(1)} %get-tuple-element.48), channel_id=1, source_target_pairs={{0,14},{2,0},{4,2},{6,4},{8,6},{10,8},{12,10},{14,12},{1,15},{3,1}... | collective-permute-start | bytes 786440 | tf_op jit(solution)/shard_map/ppermute | solution.py:442
  40.6 0.9 %collective-permute-done.8 = f32[2,2,64,128]{3,2,1,0:T(8,128)S(1)} collective-permute-done((f32[2,2,64,128]{3,2,1,0:T(8,128)S(1)}, f32[2,2,64,128]{3,2,1,0:T(8,128)S(1)}, u32[]{:S(2)}, u32[]{:S(2)}) %collective-permute-start.8) | collective-permute-done | bytes 131104 | tf_op jit(solution)/shard_map/ppermute | solution.py:442
  41.5 0.1 fusion
  41.6 0.1 fusion.1
  41.7 0.1 maximum_add_fusion.1
  41.8 2.0 %collective-permute-start.10 = (f32[2,2,64,256]{3,2,1,0:T(8,128)S(1)}, f32[2,2,64,256]{3,2,1,0:T(8,128)S(1)}, u32[]{:S(2)}, u32[]{:S(2)}) collective-permute-start(f32[2,2,64,256]{3,2,1,0:T(8,128)S(1)} %get-tuple-element.65), channel_id=1, source_target_pairs={{0,16},{16,32},{32,48},{48,64},{64,80},{80,96},{96,112},{112,128},... | collective-permute-start | bytes 786440 | tf_op jit(solution)/shard_map/ppermute | solution.py:442
  43.8 3.3 %shard_map.117.gram = f32[32,128]{1,0:T(8,128)S(1)} custom-call(bf16[5,2,2,256,256]{4,3,2,1,0:T(8,128)(2,1)S(1)} %copy-done, bf16[5,2,2,256,256]{4,3,2,1,0:T(8,128)(2,1)S(1)} %copy-done.1, f32[2,2,64,256]{3,2,1,0:T(8,128)S(1)} %get-tuple-element.64.after), custom_call_target="tpu_custom_call" | custom-call | tf_op jit(solution)/shard_map/pallas_call | solution.py:429
  47.1 0.0 collective-permute-done.10.row_up
  47.2 2.8 %collective-permute-done.11.row_down = f32[2,2,64,256]{3,2,1,0:T(8,128)S(1)} collective-permute-done((f32[2,2,64,256]{3,2,1,0:T(8,128)S(1)}, f32[2,2,64,256]{3,2,1,0:T(8,128)S(1)}, u32[]{:S(2)}, u32[]{:S(2)}) %collective-permute-start.11) | collective-permute-done | bytes 262176 | tf_op jit(solution)/shard_map/ppermute | solution.py:442
  49.9 1.5 %shard_map.118 = (f32[2,2,256,256]{3,2,1,0:T(8,128)S(1)}, f32[128,1,128]{2,1,0:T(1,128)S(1)}, f32[2,2,256,256]{3,2,1,0:T(8,128)}) custom-call(f32[2,2,256,256]{3,2,1,0:T(8,128)S(1)} %get-tuple-element.42.gradient_in, f32[2,2,64,256]{3,2,1,0:T(8,128)S(1)} %collective-permute-done.10.row_up, f32[2,2,64,256]{3,2,1,0:T(8,128)S(1)} %collective-permute-done.11.row_down, ...), custom_call_target="tpu_custom_call" | custom-call | tf_op jit(solution)/shard_map/pallas_call | solution.py:429
  51.4 21.5 %all_to_all.5.parts = f32[128,1,128]{2,1,0:T(1,128)S(1)} all-to-all(f32[128,1,128]{2,1,0:T(1,128)S(1)} %get-tuple-element.49), channel_id=1, replica_groups=mesh['ty'=16,'tx'=8,'mode'=2] {'ty','tx'}, dimensions={0} | all-to-all | bytes 131072 | tf_op jit(solution)/shard_map/all_to_all | solution.py:528
  72.9 2.1 %shard_map.119 = f32[2,2,256,256]{3,2,1,0:T(8,128)} custom-call(f32[128,1,128]{2,1,0:T(1,128)S(1)} %all_to_all.5.parts, f32[2,2,256,256]{3,2,1,0:T(8,128)S(1)} %copy-done.2, f32[2,2,256,256]{3,2,1,0:T(8,128)S(1)} %get-tuple-element.50.gradient, bf16[5,2,2,256,256]{4,3,2,1,0:T(8,128)(2,1)S(1)} %copy-done, bf16[5,2,2,256,256]{4,3,2,1,0:T(8,128)(2,1)S(1)} %copy-done.1), custom_call_target="tpu_custom_call" | custom-call | tf_op jit(solution)/shard_map/pallas_call | solution.py:429
  (32 shorter events, 0.1 us)
Async XLA Ops:
  0.6 19.6 %copy-start.2 = (f32[2,2,256,256]{3,2,1,0:T(8,128)S(1)}, f32[2,2,256,256]{3,2,1,0:T(8,128)}, u32[]{:S(2)}) copy-start(f32[2,2,256,256]{3,2,1,0:T(8,128)} %obj.7) | copy-start | bytes 3145732
  0.6 16.8 %copy-start.9 = (f32[256,256]{1,0:T(8,128)S(1)}, f32[256,256]{1,0:T(8,128)}, u32[]{:S(2)}) copy-start(f32[256,256]{1,0:T(8,128)} %param.14) | copy-start | bytes 786436
  2.4 22.3 %copy-start.3 = (f32[2,256,512]{2,1,0:T(8,128)S(1)}, f32[2,256,512]{2,1,0:T(8,128)}, u32[]{:S(2)}) copy-start(f32[2,256,512]{2,1,0:T(8,128)} %probe.5) | copy-start | bytes 3145732
  2.4 22.2 %copy-start.4 = (bf16[512,512]{1,0:T(8,128)(2,1)S(1)}, bf16[512,512]{1,0:T(8,128)(2,1)}, u32[]{:S(2)}) copy-start(bf16[512,512]{1,0:T(8,128)(2,1)} %constant.15.clone.fwd_t) | copy-start | bytes 1572868
  2.4 22.2 %copy-start.5 = (bf16[512,512]{1,0:T(8,128)(2,1)S(1)}, bf16[512,512]{1,0:T(8,128)(2,1)}, u32[]{:S(2)}) copy-start(bf16[512,512]{1,0:T(8,128)(2,1)} %constant.16.clone.inv_t) | copy-start | bytes 1572868
  2.4 22.2 %copy-start.6 = (bf16[256,512]{1,0:T(8,128)(2,1)S(1)}, bf16[256,512]{1,0:T(8,128)(2,1)}, u32[]{:S(2)}) copy-start(bf16[256,512]{1,0:T(8,128)(2,1)} %constant.17.clone.left_t) | copy-start | bytes 786436
  2.5 22.2 %copy-start.8 = (s32[1,2]{1,0:T(1,128)S(1)}, s32[1,2]{1,0:T(1,128)}, u32[]{:S(2)}) copy-start(s32[1,2]{1,0:T(1,128)} %offsets.3) | copy-start | bytes 28
  2.5 12.5 %collective-permute-start.3 = (f32[2,256,128]{2,1,0:T(8,128)S(1)}, f32[2,256,128]{2,1,0:T(8,128)S(1)}, u32[]{:S(2)}, u32[]{:S(2)}) collective-permute-start(f32[2,256,128]{2,1,0:T(8,128)S(1)} %get-tuple-element.30), channel_id=1, source_target_pairs={{0,2},{2,4},{4,6},{6,8},{8,10},{10,12},{12,14},{14,0},{1,3},{3,5},... | collective-permute-start | bytes 786440 | tf_op jit(solution)/shard_map/ppermute | solution.py:442
  5.0 10.0 %collective-permute-start.4 = (f32[2,256,128]{2,1,0:T(8,128)S(1)}, f32[2,256,128]{2,1,0:T(8,128)S(1)}, u32[]{:S(2)}, u32[]{:S(2)}) collective-permute-start(f32[2,256,128]{2,1,0:T(8,128)S(1)} %get-tuple-element.31), channel_id=1, source_target_pairs={{0,14},{2,0},{4,2},{6,4},{8,6},{10,8},{12,10},{14,12},{1,15},{3,1}... | collective-permute-start | bytes 786440 | tf_op jit(solution)/shard_map/ppermute | solution.py:442
  9.0 13.8 %collective-permute-start = (f32[256,512]{1,0:T(8,128)S(1)}, f32[256,512]{1,0:T(8,128)S(1)}, u32[]{:S(2)}, u32[]{:S(2)}) collective-permute-start(f32[256,512]{1,0:T(8,128)S(1)} %get-tuple-element.27), channel_id=1, source_target_pairs={{0,129},{1,128},{16,145},{17,144},{32,161},{33,160},{48,177},{49,1... | collective-permute-start | bytes 1572872 | tf_op jit(solution)/shard_map/ppermute | solution.py:472
  11.8 6.6 %collective-permute-start.1 = (f32[2,2,64,256]{3,2,1,0:T(8,128)S(1)}, f32[2,2,64,256]{3,2,1,0:T(8,128)S(1)}, u32[]{:S(2)}, u32[]{:S(2)}) collective-permute-start(f32[2,2,64,256]{3,2,1,0:T(8,128)S(1)} %get-tuple-element.28), channel_id=1, source_target_pairs={{0,16},{16,32},{32,48},{48,64},{64,80},{80,96},{96,112},{112,128},... | collective-permute-start | bytes 786440 | tf_op jit(solution)/shard_map/ppermute | solution.py:442
  14.1 6.1 %collective-permute-start.2 = (f32[2,2,64,256]{3,2,1,0:T(8,128)S(1)}, f32[2,2,64,256]{3,2,1,0:T(8,128)S(1)}, u32[]{:S(2)}, u32[]{:S(2)}) collective-permute-start(f32[2,2,64,256]{3,2,1,0:T(8,128)S(1)} %get-tuple-element.29), channel_id=1, source_target_pairs={{0,240},{16,0},{32,16},{48,32},{64,48},{80,64},{96,80},{112,96},{1... | collective-permute-start | bytes 786440 | tf_op jit(solution)/shard_map/ppermute | solution.py:442
  15.0 5.6 %collective-permute-start.5 = (f32[2,2,64,128]{3,2,1,0:T(8,128)S(1)}, f32[2,2,64,128]{3,2,1,0:T(8,128)S(1)}, u32[]{:S(2)}, u32[]{:S(2)}) collective-permute-start(f32[2,2,64,128]{3,2,1,0:T(8,128)S(1)} %get-tuple-element.53), channel_id=1, source_target_pairs={{0,16},{16,32},{32,48},{48,64},{64,80},{80,96},{96,112},{112,128},... | collective-permute-start | bytes 393224 | tf_op jit(solution)/shard_map/ppermute | solution.py:442
  17.4 4.7 %collective-permute-start.6 = (f32[2,2,64,128]{3,2,1,0:T(8,128)S(1)}, f32[2,2,64,128]{3,2,1,0:T(8,128)S(1)}, u32[]{:S(2)}, u32[]{:S(2)}) collective-permute-start(f32[2,2,64,128]{3,2,1,0:T(8,128)S(1)} %get-tuple-element.52), channel_id=1, source_target_pairs={{0,240},{16,0},{32,16},{48,32},{64,48},{80,64},{96,80},{112,96},{1... | collective-permute-start | bytes 393224 | tf_op jit(solution)/shard_map/ppermute | solution.py:442
  22.9 4.2 %copy-start.7 = (f32[1,256,256]{2,1,0:T(8,128)S(1)}, f32[1,256,256]{2,1,0:T(8,128)}, u32[]{:S(2)}) copy-start(f32[1,256,256]{2,1,0:T(8,128)} %patterns.1) | copy-start | bytes 786436
  22.9 4.2 %collective-permute-start.7 = (f32[256,512]{1,0:T(8,128)S(1)}, f32[256,512]{1,0:T(8,128)S(1)}, u32[]{:S(2)}, u32[]{:S(2)}) collective-permute-start(f32[256,512]{1,0:T(8,128)S(1)} %collective-permute-done.near), channel_id=1, source_target_pairs={{0,16},{16,0},{32,48},{48,32},{64,80},{80,64},{96,112},{112,96},{1... | collective-permute-start | bytes 1572872 | tf_op jit(solution)/shard_map/ppermute | solution.py:482
  27.0 16.8 %copy-start.1 = (bf16[5,2,2,256,256]{4,3,2,1,0:T(8,128)(2,1)S(1)}, bf16[5,2,2,256,256]{4,3,2,1,0:T(8,128)(2,1)}, u32[]{:S(2)}) copy-start(bf16[5,2,2,256,256]{4,3,2,1,0:T(8,128)(2,1)} %changes.5) | copy-start | bytes 7864324
  35.1 8.8 %copy-start = (bf16[5,2,2,256,256]{4,3,2,1,0:T(8,128)(2,1)S(1)}, bf16[5,2,2,256,256]{4,3,2,1,0:T(8,128)(2,1)}, u32[]{:S(2)}) copy-start(bf16[5,2,2,256,256]{4,3,2,1,0:T(8,128)(2,1)} %steps.5) | copy-start | bytes 7864324
  35.1 6.4 %collective-permute-start.8 = (f32[2,2,64,128]{3,2,1,0:T(8,128)S(1)}, f32[2,2,64,128]{3,2,1,0:T(8,128)S(1)}, u32[]{:S(2)}, u32[]{:S(2)}) collective-permute-start(f32[2,2,64,128]{3,2,1,0:T(8,128)S(1)} %get-tuple-element.44), channel_id=1, source_target_pairs={{0,2},{2,4},{4,6},{6,8},{8,10},{10,12},{12,14},{14,0},{1,3},{3,5},... | collective-permute-start | bytes 393224 | tf_op jit(solution)/shard_map/ppermute | solution.py:442
  35.3 6.3 %collective-permute-start.9 = (f32[2,2,64,128]{3,2,1,0:T(8,128)S(1)}, f32[2,2,64,128]{3,2,1,0:T(8,128)S(1)}, u32[]{:S(2)}, u32[]{:S(2)}) collective-permute-start(f32[2,2,64,128]{3,2,1,0:T(8,128)S(1)} %get-tuple-element.45), channel_id=1, source_target_pairs={{0,14},{2,0},{4,2},{6,4},{8,6},{10,8},{12,10},{14,12},{1,15},{3,1}... | collective-permute-start | bytes 393224 | tf_op jit(solution)/shard_map/ppermute | solution.py:442
  37.9 9.2 %collective-permute-start.12 = (f32[2,256,128]{2,1,0:T(8,128)S(1)}, f32[2,256,128]{2,1,0:T(8,128)S(1)}, u32[]{:S(2)}, u32[]{:S(2)}) collective-permute-start(f32[2,256,128]{2,1,0:T(8,128)S(1)} %get-tuple-element.47), channel_id=1, source_target_pairs={{0,2},{2,4},{4,6},{6,8},{8,10},{10,12},{12,14},{14,0},{1,3},{3,5},... | collective-permute-start | bytes 786440 | tf_op jit(solution)/shard_map/ppermute | solution.py:442
  37.9 9.2 %collective-permute-start.13 = (f32[2,256,128]{2,1,0:T(8,128)S(1)}, f32[2,256,128]{2,1,0:T(8,128)S(1)}, u32[]{:S(2)}, u32[]{:S(2)}) collective-permute-start(f32[2,256,128]{2,1,0:T(8,128)S(1)} %get-tuple-element.48), channel_id=1, source_target_pairs={{0,14},{2,0},{4,2},{6,4},{8,6},{10,8},{12,10},{14,12},{1,15},{3,1}... | collective-permute-start | bytes 786440 | tf_op jit(solution)/shard_map/ppermute | solution.py:442
  41.8 5.3 %collective-permute-start.10 = (f32[2,2,64,256]{3,2,1,0:T(8,128)S(1)}, f32[2,2,64,256]{3,2,1,0:T(8,128)S(1)}, u32[]{:S(2)}, u32[]{:S(2)}) collective-permute-start(f32[2,2,64,256]{3,2,1,0:T(8,128)S(1)} %get-tuple-element.65), channel_id=1, source_target_pairs={{0,16},{16,32},{32,48},{48,64},{64,80},{80,96},{96,112},{112,128},... | collective-permute-start | bytes 786440 | tf_op jit(solution)/shard_map/ppermute | solution.py:442
  43.8 6.1 %collective-permute-start.11 = (f32[2,2,64,256]{3,2,1,0:T(8,128)S(1)}, f32[2,2,64,256]{3,2,1,0:T(8,128)S(1)}, u32[]{:S(2)}, u32[]{:S(2)}) collective-permute-start(f32[2,2,64,256]{3,2,1,0:T(8,128)S(1)} %get-tuple-element.64.after), channel_id=1, source_target_pairs={{0,240},{16,0},{32,16},{48,32},{64,48},{80,64},{96,80},{112,96},{1... | collective-permute-start | bytes 786440 | tf_op jit(solution)/shard_map/ppermute | solution.py:442

commit v6 on v5

--- a/solution.py
+++ b/solution.py
@@ -272,7 +272,8 @@
             block = back[0, s, rows, columns] + back[1, s, rows, columns]
             block = pltpu.roll(jnp.concatenate([block, zero], 1), shift, 1)
             block = pltpu.roll(jnp.concatenate([block, gap], 0), row_rest, 0)
-            frame[q, pl.ds(row_base + rows.start, 72), :] += block
+            frame[q, pl.ds(row_base + rows.start, 8), :] += block[:8]
+            frame[q, pl.ds(row_base + rows.start + 8, 64), :] = block[8:]
     for s in range(2):
         for part in range(2):
             q = 2 * s + part

time: 75.3 us -> 75.2 us (level)
  no operation moved by 1% of the time
where the time goes in v6:
time: 75.2 us; the launch traced here: 75.1 us
  starting transfers between devices  23.2 us (31%)
  blocking collectives  21.5 us (29%)
  Pallas kernels  19.3 us (26%)
  waiting for transfers between devices  8.57 us (11%)
  local copies, waits for them, and re-layouts  1.26 us (2%)
  between operations  1.07 us (1%)
    all_to_all x1, blocking collectives, per_device(): parts = lax.all_to_all(sums, TILES, 0, 0)  21.5 us
    pallas_call x7, Pallas kernels, call(): pl.pallas_call(kernel, out_shape=outs, in_specs=[SMEM] * smem + [ANY] * r...  19.3 us
    ppermute x12, starting transfers between devices, shifted(): lax.ppermute(value, axis, [(i, (i + step) % size) for i in range(size)])  18.7 us
    ppermute x12, waiting for transfers between devices, shifted(): lax.ppermute(value, axis, [(i, (i + step) % size) for i in range(size)])  7.81 us
    ppermute x1, starting transfers between devices, per_device(): lax.ppermute(chosen, ('ty', 'mode'), near_pairs(rows_axis, modes_axis))  2.73 us
    ppermute x1, starting transfers between devices, per_device(): swapped = lax.ppermute(near, 'ty', [(i, i ^ 1) for i in range(rows_axis)])  1.79 us
  transfers between devices with their start and end apart: 14, of which 6 were waited for; matrix products, arithmetic and copies ran while one was open for 2% of the time, Pallas kernels for 8%

profile of v6, /device:TPU:1, one launch (start us, length us, event | category | flops | bytes accessed | tf_op | source)
XLA Modules:
  0.0 75.1 jit_solution(9079326435252685145)
XLA Ops:
  0.7 1.7 %shard_map.113 = (f32[2,2,64,256]{3,2,1,0:T(8,128)S(1)}, f32[2,2,64,256]{3,2,1,0:T(8,128)S(1)}, f32[2,256,128]{2,1,0:T(8,128)S(1)}, f32[2,256,128]{2,1,0:T(8,128)S(1)}, f32[256,512]{1,0:T(8,128)S(1)}) custom-call(s32[1]{0:T(128)} %bitcast.core, f32[2,2,256,256]{3,2,1,0:T(8,128)} %obj.7, f32[2,256,512]{2,1,0:T(8,128)} %probe.5), custom_call_target="tpu_custom_call" | custom-call | tf_op jit(solution)/shard_map/pallas_call | solution.py:430
  2.4 0.0 copy-start.4
  2.4 0.0 copy-start.5
  2.5 2.5 %collective-permute-start.3 = (f32[2,256,128]{2,1,0:T(8,128)S(1)}, f32[2,256,128]{2,1,0:T(8,128)S(1)}, u32[]{:S(2)}, u32[]{:S(2)}) collective-permute-start(f32[2,256,128]{2,1,0:T(8,128)S(1)} %get-tuple-element.30), channel_id=1, source_target_pairs={{0,2},{2,4},{4,6},{6,8},{8,10},{10,12},{12,14},{14,0},{1,3},{3,5},... | collective-permute-start | bytes 786440 | tf_op jit(solution)/shard_map/ppermute | solution.py:443
  5.0 4.0 %collective-permute-start.4 = (f32[2,256,128]{2,1,0:T(8,128)S(1)}, f32[2,256,128]{2,1,0:T(8,128)S(1)}, u32[]{:S(2)}, u32[]{:S(2)}) collective-permute-start(f32[2,256,128]{2,1,0:T(8,128)S(1)} %get-tuple-element.31), channel_id=1, source_target_pairs={{0,14},{2,0},{4,2},{6,4},{8,6},{10,8},{12,10},{14,12},{1,15},{3,1}... | collective-permute-start | bytes 786440 | tf_op jit(solution)/shard_map/ppermute | solution.py:443
  9.0 2.7 %collective-permute-start = (f32[256,512]{1,0:T(8,128)S(1)}, f32[256,512]{1,0:T(8,128)S(1)}, u32[]{:S(2)}, u32[]{:S(2)}) collective-permute-start(f32[256,512]{1,0:T(8,128)S(1)} %get-tuple-element.27), channel_id=1, source_target_pairs={{0,129},{1,128},{16,145},{17,144},{32,161},{33,160},{48,177},{49,1... | collective-permute-start | bytes 1572872 | tf_op jit(solution)/shard_map/ppermute | solution.py:473
  11.8 2.3 %collective-permute-start.1 = (f32[2,2,64,256]{3,2,1,0:T(8,128)S(1)}, f32[2,2,64,256]{3,2,1,0:T(8,128)S(1)}, u32[]{:S(2)}, u32[]{:S(2)}) collective-permute-start(f32[2,2,64,256]{3,2,1,0:T(8,128)S(1)} %get-tuple-element.28), channel_id=1, source_target_pairs={{0,16},{16,32},{32,48},{48,64},{64,80},{80,96},{96,112},{112,128},... | collective-permute-start | bytes 786440 | tf_op jit(solution)/shard_map/ppermute | solution.py:443
  14.1 0.9 %collective-permute-done.3.left_in = f32[2,256,128]{2,1,0:T(8,128)S(1)} collective-permute-done((f32[2,256,128]{2,1,0:T(8,128)S(1)}, f32[2,256,128]{2,1,0:T(8,128)S(1)}, u32[]{:S(2)}, u32[]{:S(2)}) %collective-permute-start.3) | collective-permute-done | bytes 262176 | tf_op jit(solution)/shard_map/ppermute | solution.py:443
  15.0 2.4 %collective-permute-start.5 = (f32[2,2,64,128]{3,2,1,0:T(8,128)S(1)}, f32[2,2,64,128]{3,2,1,0:T(8,128)S(1)}, u32[]{:S(2)}, u32[]{:S(2)}) collective-permute-start(f32[2,2,64,128]{3,2,1,0:T(8,128)S(1)} %get-tuple-element.53), channel_id=1, source_target_pairs={{0,16},{16,32},{32,48},{48,64},{64,80},{80,96},{96,112},{112,128},... | collective-permute-start | bytes 393224 | tf_op jit(solution)/shard_map/ppermute | solution.py:443
  17.4 0.9 %cosine_bitcast_fusion = (f32[1,256,256]{2,1,0:T(8,128)S(1)}, f32[1,256,256]{2,1,0:T(8,128)S(1)}) fusion(f32[256,256]{1,0:T(8,128)S(1)} %copy-done.9), kind=kLoop, calls=%fused_computation.4 | loop fusion | bytes 786432 | tf_op jit(solution)/shard_map/stack | solution.py:478
  18.4 1.8 %collective-permute-done.2.bottom = f32[2,2,64,256]{3,2,1,0:T(8,128)S(1)} collective-permute-done((f32[2,2,64,256]{3,2,1,0:T(8,128)S(1)}, f32[2,2,64,256]{3,2,1,0:T(8,128)S(1)}, u32[]{:S(2)}, u32[]{:S(2)}) %collective-permute-start.2) | collective-permute-done | bytes 262176 | tf_op jit(solution)/shard_map/ppermute | solution.py:443
  20.2 0.4 shard_map.114
  20.6 1.5 %collective-permute-done.6.corner_down = f32[2,2,64,128]{3,2,1,0:T(8,128)S(1)} collective-permute-done((f32[2,2,64,128]{3,2,1,0:T(8,128)S(1)}, f32[2,2,64,128]{3,2,1,0:T(8,128)S(1)}, u32[]{:S(2)}, u32[]{:S(2)}) %collective-permute-start.6) | collective-permute-done | bytes 131104 | tf_op jit(solution)/shard_map/ppermute | solution.py:443
  22.1 0.8 %collective-permute-done.near = f32[256,512]{1,0:T(8,128)S(1)} collective-permute-done((f32[256,512]{1,0:T(8,128)S(1)}, f32[256,512]{1,0:T(8,128)S(1)}, u32[]{:S(2)}, u32[]{:S(2)}) %collective-permute-start) | collective-permute-done | bytes 524320 | tf_op jit(solution)/shard_map/ppermute | solution.py:473
  22.9 1.8 %collective-permute-start.7 = (f32[256,512]{1,0:T(8,128)S(1)}, f32[256,512]{1,0:T(8,128)S(1)}, u32[]{:S(2)}, u32[]{:S(2)}) collective-permute-start(f32[256,512]{1,0:T(8,128)S(1)} %collective-permute-done.near), channel_id=1, source_target_pairs={{0,16},{16,0},{32,48},{48,32},{64,80},{80,64},{96,112},{112,96},{1... | collective-permute-start | bytes 1572872 | tf_op jit(solution)/shard_map/ppermute | solution.py:483
  24.7 2.3 %shard_map.115 = (f32[2,256,512]{2,1,0:T(8,128)S(1)}, f32[2,256,512]{2,1,0:T(8,128)S(1)}, f32[4,392,384]{2,1,0:T(8,128)S(1)}) custom-call(s32[1,2]{1,0:T(1,128)S(1)} %copy-done.8, f32[4,392,384]{2,1,0:T(8,128)S(1)} %get-tuple-element.36.ext_in, f32[2,2,64,128]{3,2,1,0:T(8,128)S(1)} %collective-permute-done.5.corner_up, ...), custom_call_target="tpu_custom_call", output_to_operand_aliasing={{2}: (1, {})} | custom-call | tf_op jit(solution)/shard_map/pallas_call | solution.py:430
  27.1 8.0 %shard_map.116 = (f32[2,2,256,256]{3,2,1,0:T(8,128)S(1)}, f32[2,2,64,256]{3,2,1,0:T(8,128)S(1)}, f32[2,2,64,256]{3,2,1,0:T(8,128)S(1)}, f32[2,256,128]{2,1,0:T(8...) custom-call(s32[1,2]{1,0:T(1,128)S(1)} %copy-done.8, ...), custom_call_target="tpu_custom_call", output_to_operand_aliasing={{7}: (12, {})} | custom-call | tf_op jit(solution)/shard_map/pallas_call | solution.py:430
  35.1 0.1 collective-permute-start.8
  35.2 0.1 pad.7.clone
  35.2 2.7 %collective-permute-start.9 = (f32[2,2,64,128]{3,2,1,0:T(8,128)S(1)}, f32[2,2,64,128]{3,2,1,0:T(8,128)S(1)}, u32[]{:S(2)}, u32[]{:S(2)}) collective-permute-start(f32[2,2,64,128]{3,2,1,0:T(8,128)S(1)} %get-tuple-element.45), channel_id=1, source_target_pairs={{0,14},{2,0},{4,2},{6,4},{8,6},{10,8},{12,10},{14,12},{1,15},{3,1}... | collective-permute-start | bytes 393224 | tf_op jit(solution)/shard_map/ppermute | solution.py:443
  37.9 2.7 %collective-permute-start.13 = (f32[2,256,128]{2,1,0:T(8,128)S(1)}, f32[2,256,128]{2,1,0:T(8,128)S(1)}, u32[]{:S(2)}, u32[]{:S(2)}) collective-permute-start(f32[2,256,128]{2,1,0:T(8,128)S(1)} %get-tuple-element.48), channel_id=1, source_target_pairs={{0,14},{2,0},{4,2},{6,4},{8,6},{10,8},{12,10},{14,12},{1,15},{3,1}... | collective-permute-start | bytes 786440 | tf_op jit(solution)/shard_map/ppermute | solution.py:443
  40.6 0.9 %collective-permute-done.8 = f32[2,2,64,128]{3,2,1,0:T(8,128)S(1)} collective-permute-done((f32[2,2,64,128]{3,2,1,0:T(8,128)S(1)}, f32[2,2,64,128]{3,2,1,0:T(8,128)S(1)}, u32[]{:S(2)}, u32[]{:S(2)}) %collective-permute-start.8) | collective-permute-done | bytes 131104 | tf_op jit(solution)/shard_map/ppermute | solution.py:443
  41.5 0.1 fusion
  41.6 0.1 fusion.1
  41.7 0.1 maximum_add_fusion.1
  41.8 2.0 %collective-permute-start.10 = (f32[2,2,64,256]{3,2,1,0:T(8,128)S(1)}, f32[2,2,64,256]{3,2,1,0:T(8,128)S(1)}, u32[]{:S(2)}, u32[]{:S(2)}) collective-permute-start(f32[2,2,64,256]{3,2,1,0:T(8,128)S(1)} %get-tuple-element.65), channel_id=1, source_target_pairs={{0,16},{16,32},{32,48},{48,64},{64,80},{80,96},{96,112},{112,128},... | collective-permute-start | bytes 786440 | tf_op jit(solution)/shard_map/ppermute | solution.py:443
  43.8 3.3 %shard_map.117.gram = f32[32,128]{1,0:T(8,128)S(1)} custom-call(bf16[5,2,2,256,256]{4,3,2,1,0:T(8,128)(2,1)S(1)} %copy-done, bf16[5,2,2,256,256]{4,3,2,1,0:T(8,128)(2,1)S(1)} %copy-done.1, f32[2,2,64,256]{3,2,1,0:T(8,128)S(1)} %get-tuple-element.64.after), custom_call_target="tpu_custom_call" | custom-call | tf_op jit(solution)/shard_map/pallas_call | solution.py:430
  47.1 0.0 collective-permute-done.10.row_up
  47.1 2.8 %collective-permute-done.11.row_down = f32[2,2,64,256]{3,2,1,0:T(8,128)S(1)} collective-permute-done((f32[2,2,64,256]{3,2,1,0:T(8,128)S(1)}, f32[2,2,64,256]{3,2,1,0:T(8,128)S(1)}, u32[]{:S(2)}, u32[]{:S(2)}) %collective-permute-start.11) | collective-permute-done | bytes 262176 | tf_op jit(solution)/shard_map/ppermute | solution.py:443
  49.9 1.5 %shard_map.118 = (f32[2,2,256,256]{3,2,1,0:T(8,128)S(1)}, f32[128,1,128]{2,1,0:T(1,128)S(1)}, f32[2,2,256,256]{3,2,1,0:T(8,128)}) custom-call(f32[2,2,256,256]{3,2,1,0:T(8,128)S(1)} %get-tuple-element.42.gradient_in, f32[2,2,64,256]{3,2,1,0:T(8,128)S(1)} %collective-permute-done.10.row_up, f32[2,2,64,256]{3,2,1,0:T(8,128)S(1)} %collective-permute-done.11.row_down, ...), custom_call_target="tpu_custom_call" | custom-call | tf_op jit(solution)/shard_map/pallas_call | solution.py:430
  51.3 21.5 %all_to_all.5.parts = f32[128,1,128]{2,1,0:T(1,128)S(1)} all-to-all(f32[128,1,128]{2,1,0:T(1,128)S(1)} %get-tuple-element.49), channel_id=1, replica_groups=mesh['ty'=16,'tx'=8,'mode'=2] {'ty','tx'}, dimensions={0} | all-to-all | bytes 131072 | tf_op jit(solution)/shard_map/all_to_all | solution.py:529
  72.8 2.1 %shard_map.119 = f32[2,2,256,256]{3,2,1,0:T(8,128)} custom-call(f32[128,1,128]{2,1,0:T(1,128)S(1)} %all_to_all.5.parts, f32[2,2,256,256]{3,2,1,0:T(8,128)S(1)} %copy-done.2, f32[2,2,256,256]{3,2,1,0:T(8,128)S(1)} %get-tuple-element.50.gradient, bf16[5,2,2,256,256]{4,3,2,1,0:T(8,128)(2,1)S(1)} %copy-done, bf16[5,2,2,256,256]{4,3,2,1,0:T(8,128)(2,1)S(1)} %copy-done.1), custom_call_target="tpu_custom_call" | custom-call | tf_op jit(solution)/shard_map/pallas_call | solution.py:430
  (32 shorter events, 0.1 us)
Async XLA Ops:
  0.6 19.6 %copy-start.2 = (f32[2,2,256,256]{3,2,1,0:T(8,128)S(1)}, f32[2,2,256,256]{3,2,1,0:T(8,128)}, u32[]{:S(2)}) copy-start(f32[2,2,256,256]{3,2,1,0:T(8,128)} %obj.7) | copy-start | bytes 3145732
  0.6 16.8 %copy-start.9 = (f32[256,256]{1,0:T(8,128)S(1)}, f32[256,256]{1,0:T(8,128)}, u32[]{:S(2)}) copy-start(f32[256,256]{1,0:T(8,128)} %param.14) | copy-start | bytes 786436
  2.4 22.3 %copy-start.3 = (f32[2,256,512]{2,1,0:T(8,128)S(1)}, f32[2,256,512]{2,1,0:T(8,128)}, u32[]{:S(2)}) copy-start(f32[2,256,512]{2,1,0:T(8,128)} %probe.5) | copy-start | bytes 3145732
  2.4 22.2 %copy-start.4 = (bf16[512,512]{1,0:T(8,128)(2,1)S(1)}, bf16[512,512]{1,0:T(8,128)(2,1)}, u32[]{:S(2)}) copy-start(bf16[512,512]{1,0:T(8,128)(2,1)} %constant.15.clone.fwd_t) | copy-start | bytes 1572868
  2.4 22.2 %copy-start.5 = (bf16[512,512]{1,0:T(8,128)(2,1)S(1)}, bf16[512,512]{1,0:T(8,128)(2,1)}, u32[]{:S(2)}) copy-start(bf16[512,512]{1,0:T(8,128)(2,1)} %constant.16.clone.inv_t) | copy-start | bytes 1572868
  2.4 22.2 %copy-start.6 = (bf16[256,512]{1,0:T(8,128)(2,1)S(1)}, bf16[256,512]{1,0:T(8,128)(2,1)}, u32[]{:S(2)}) copy-start(bf16[256,512]{1,0:T(8,128)(2,1)} %constant.17.clone.left_t) | copy-start | bytes 786436
  2.5 22.2 %copy-start.8 = (s32[1,2]{1,0:T(1,128)S(1)}, s32[1,2]{1,0:T(1,128)}, u32[]{:S(2)}) copy-start(s32[1,2]{1,0:T(1,128)} %offsets.3) | copy-start | bytes 28
  2.5 12.5 %collective-permute-start.3 = (f32[2,256,128]{2,1,0:T(8,128)S(1)}, f32[2,256,128]{2,1,0:T(8,128)S(1)}, u32[]{:S(2)}, u32[]{:S(2)}) collective-permute-start(f32[2,256,128]{2,1,0:T(8,128)S(1)} %get-tuple-element.30), channel_id=1, source_target_pairs={{0,2},{2,4},{4,6},{6,8},{8,10},{10,12},{12,14},{14,0},{1,3},{3,5},... | collective-permute-start | bytes 786440 | tf_op jit(solution)/shard_map/ppermute | solution.py:443
  5.0 10.0 %collective-permute-start.4 = (f32[2,256,128]{2,1,0:T(8,128)S(1)}, f32[2,256,128]{2,1,0:T(8,128)S(1)}, u32[]{:S(2)}, u32[]{:S(2)}) collective-permute-start(f32[2,256,128]{2,1,0:T(8,128)S(1)} %get-tuple-element.31), channel_id=1, source_target_pairs={{0,14},{2,0},{4,2},{6,4},{8,6},{10,8},{12,10},{14,12},{1,15},{3,1}... | collective-permute-start | bytes 786440 | tf_op jit(solution)/shard_map/ppermute | solution.py:443
  9.0 13.8 %collective-permute-start = (f32[256,512]{1,0:T(8,128)S(1)}, f32[256,512]{1,0:T(8,128)S(1)}, u32[]{:S(2)}, u32[]{:S(2)}) collective-permute-start(f32[256,512]{1,0:T(8,128)S(1)} %get-tuple-element.27), channel_id=1, source_target_pairs={{0,129},{1,128},{16,145},{17,144},{32,161},{33,160},{48,177},{49,1... | collective-permute-start | bytes 1572872 | tf_op jit(solution)/shard_map/ppermute | solution.py:473
  11.8 6.6 %collective-permute-start.1 = (f32[2,2,64,256]{3,2,1,0:T(8,128)S(1)}, f32[2,2,64,256]{3,2,1,0:T(8,128)S(1)}, u32[]{:S(2)}, u32[]{:S(2)}) collective-permute-start(f32[2,2,64,256]{3,2,1,0:T(8,128)S(1)} %get-tuple-element.28), channel_id=1, source_target_pairs={{0,16},{16,32},{32,48},{48,64},{64,80},{80,96},{96,112},{112,128},... | collective-permute-start | bytes 786440 | tf_op jit(solution)/shard_map/ppermute | solution.py:443
  14.1 6.1 %collective-permute-start.2 = (f32[2,2,64,256]{3,2,1,0:T(8,128)S(1)}, f32[2,2,64,256]{3,2,1,0:T(8,128)S(1)}, u32[]{:S(2)}, u32[]{:S(2)}) collective-permute-start(f32[2,2,64,256]{3,2,1,0:T(8,128)S(1)} %get-tuple-element.29), channel_id=1, source_target_pairs={{0,240},{16,0},{32,16},{48,32},{64,48},{80,64},{96,80},{112,96},{1... | collective-permute-start | bytes 786440 | tf_op jit(solution)/shard_map/ppermute | solution.py:443
  15.0 5.6 %collective-permute-start.5 = (f32[2,2,64,128]{3,2,1,0:T(8,128)S(1)}, f32[2,2,64,128]{3,2,1,0:T(8,128)S(1)}, u32[]{:S(2)}, u32[]{:S(2)}) collective-permute-start(f32[2,2,64,128]{3,2,1,0:T(8,128)S(1)} %get-tuple-element.53), channel_id=1, source_target_pairs={{0,16},{16,32},{32,48},{48,64},{64,80},{80,96},{96,112},{112,128},... | collective-permute-start | bytes 393224 | tf_op jit(solution)/shard_map/ppermute | solution.py:443
  17.4 4.7 %collective-permute-start.6 = (f32[2,2,64,128]{3,2,1,0:T(8,128)S(1)}, f32[2,2,64,128]{3,2,1,0:T(8,128)S(1)}, u32[]{:S(2)}, u32[]{:S(2)}) collective-permute-start(f32[2,2,64,128]{3,2,1,0:T(8,128)S(1)} %get-tuple-element.52), channel_id=1, source_target_pairs={{0,240},{16,0},{32,16},{48,32},{64,48},{80,64},{96,80},{112,96},{1... | collective-permute-start | bytes 393224 | tf_op jit(solution)/shard_map/ppermute | solution.py:443
  22.9 4.2 %copy-start.7 = (f32[1,256,256]{2,1,0:T(8,128)S(1)}, f32[1,256,256]{2,1,0:T(8,128)}, u32[]{:S(2)}) copy-start(f32[1,256,256]{2,1,0:T(8,128)} %patterns.1) | copy-start | bytes 786436
  22.9 4.2 %collective-permute-start.7 = (f32[256,512]{1,0:T(8,128)S(1)}, f32[256,512]{1,0:T(8,128)S(1)}, u32[]{:S(2)}, u32[]{:S(2)}) collective-permute-start(f32[256,512]{1,0:T(8,128)S(1)} %collective-permute-done.near), channel_id=1, source_target_pairs={{0,16},{16,0},{32,48},{48,32},{64,80},{80,64},{96,112},{112,96},{1... | collective-permute-start | bytes 1572872 | tf_op jit(solution)/shard_map/ppermute | solution.py:483
  27.0 16.8 %copy-start.1 = (bf16[5,2,2,256,256]{4,3,2,1,0:T(8,128)(2,1)S(1)}, bf16[5,2,2,256,256]{4,3,2,1,0:T(8,128)(2,1)}, u32[]{:S(2)}) copy-start(bf16[5,2,2,256,256]{4,3,2,1,0:T(8,128)(2,1)} %changes.5) | copy-start | bytes 7864324
  35.1 8.7 %copy-start = (bf16[5,2,2,256,256]{4,3,2,1,0:T(8,128)(2,1)S(1)}, bf16[5,2,2,256,256]{4,3,2,1,0:T(8,128)(2,1)}, u32[]{:S(2)}) copy-start(bf16[5,2,2,256,256]{4,3,2,1,0:T(8,128)(2,1)} %steps.5) | copy-start | bytes 7864324
  35.1 6.4 %collective-permute-start.8 = (f32[2,2,64,128]{3,2,1,0:T(8,128)S(1)}, f32[2,2,64,128]{3,2,1,0:T(8,128)S(1)}, u32[]{:S(2)}, u32[]{:S(2)}) collective-permute-start(f32[2,2,64,128]{3,2,1,0:T(8,128)S(1)} %get-tuple-element.44), channel_id=1, source_target_pairs={{0,2},{2,4},{4,6},{6,8},{8,10},{10,12},{12,14},{14,0},{1,3},{3,5},... | collective-permute-start | bytes 393224 | tf_op jit(solution)/shard_map/ppermute | solution.py:443
  35.2 6.3 %collective-permute-start.9 = (f32[2,2,64,128]{3,2,1,0:T(8,128)S(1)}, f32[2,2,64,128]{3,2,1,0:T(8,128)S(1)}, u32[]{:S(2)}, u32[]{:S(2)}) collective-permute-start(f32[2,2,64,128]{3,2,1,0:T(8,128)S(1)} %get-tuple-element.45), channel_id=1, source_target_pairs={{0,14},{2,0},{4,2},{6,4},{8,6},{10,8},{12,10},{14,12},{1,15},{3,1}... | collective-permute-start | bytes 393224 | tf_op jit(solution)/shard_map/ppermute | solution.py:443
  37.9 9.2 %collective-permute-start.12 = (f32[2,256,128]{2,1,0:T(8,128)S(1)}, f32[2,256,128]{2,1,0:T(8,128)S(1)}, u32[]{:S(2)}, u32[]{:S(2)}) collective-permute-start(f32[2,256,128]{2,1,0:T(8,128)S(1)} %get-tuple-element.47), channel_id=1, source_target_pairs={{0,2},{2,4},{4,6},{6,8},{8,10},{10,12},{12,14},{14,0},{1,3},{3,5},... | collective-permute-start | bytes 786440 | tf_op jit(solution)/shard_map/ppermute | solution.py:443
  37.9 9.2 %collective-permute-start.13 = (f32[2,256,128]{2,1,0:T(8,128)S(1)}, f32[2,256,128]{2,1,0:T(8,128)S(1)}, u32[]{:S(2)}, u32[]{:S(2)}) collective-permute-start(f32[2,256,128]{2,1,0:T(8,128)S(1)} %get-tuple-element.48), channel_id=1, source_target_pairs={{0,14},{2,0},{4,2},{6,4},{8,6},{10,8},{12,10},{14,12},{1,15},{3,1}... | collective-permute-start | bytes 786440 | tf_op jit(solution)/shard_map/ppermute | solution.py:443
  41.8 5.3 %collective-permute-start.10 = (f32[2,2,64,256]{3,2,1,0:T(8,128)S(1)}, f32[2,2,64,256]{3,2,1,0:T(8,128)S(1)}, u32[]{:S(2)}, u32[]{:S(2)}) collective-permute-start(f32[2,2,64,256]{3,2,1,0:T(8,128)S(1)} %get-tuple-element.65), channel_id=1, source_target_pairs={{0,16},{16,32},{32,48},{48,64},{64,80},{80,96},{96,112},{112,128},... | collective-permute-start | bytes 786440 | tf_op jit(solution)/shard_map/ppermute | solution.py:443
  43.8 6.1 %collective-permute-start.11 = (f32[2,2,64,256]{3,2,1,0:T(8,128)S(1)}, f32[2,2,64,256]{3,2,1,0:T(8,128)S(1)}, u32[]{:S(2)}, u32[]{:S(2)}) collective-permute-start(f32[2,2,64,256]{3,2,1,0:T(8,128)S(1)} %get-tuple-element.64.after), channel_id=1, source_target_pairs={{0,240},{16,0},{32,16},{48,32},{64,48},{80,64},{96,80},{112,96},{1... | collective-permute-start | bytes 786440 | tf_op jit(solution)/shard_map/ppermute | solution.py:443
